TPU v7x, 32 devices: a whole 2x2x4 slice. The times are simulated.
32 devices in a mesh: dp: 4 (over x, core), fsdp: 8 (over z, y).
Axes of the slice: x: 2, y: 2, z: 4, core: 2. Of those that a mesh axis runs over, the one named last changes fastest.
Arguments:
- inputs: bfloat16 [45056, 768], P(('dp', 'fsdp')), may hold values from -6 to 6
- segment_ids: int32 [45056], P(('dp', 'fsdp')), may hold values from 0 to 5, as said below
- cotangent: bfloat16 [45056, 768], P(('dp', 'fsdp')), may hold values from -6 to 6
- in_weight: bfloat16 [768, 2304], P(('dp', 'fsdp')), may hold values from -0.21875 to 0.21875
- in_bias: bfloat16 [1536], P(('dp', 'fsdp')), may hold values from -1 to 1
- out_weight: bfloat16 [768, 768], P(('dp', 'fsdp')), may hold values from -0.875 to 0.875
- out_bias: bfloat16 [768], P(('dp', 'fsdp')), may hold values from -1 to 1
- first_gain: bfloat16 [768], P(('dp', 'fsdp')), may hold values from 0.5 to 1.5
- first_shift: bfloat16 [768], P(('dp', 'fsdp')), may hold values from -1 to 1
- first_scale: bfloat16 [768], P(('dp', 'fsdp')), may hold values from 0.059814453 to 0.15917969
- up_weight: bfloat16 [768, 3072], P(('dp', 'fsdp')), may hold values from -0.21875 to 0.21875
- up_bias: bfloat16 [3072], P(('dp', 'fsdp')), may hold values from -1 to 1
- down_weight: bfloat16 [3072, 768], P(('dp', 'fsdp')), may hold values from -0.109375 to 0.109375
- down_bias: bfloat16 [768], P(('dp', 'fsdp')), may hold values from -1 to 1
- second_gain: bfloat16 [768], P(('dp', 'fsdp')), may hold values from 0.5 to 1.5
- second_shift: bfloat16 [768], P(('dp', 'fsdp')), may hold values from -1 to 1
- second_scale: bfloat16 [768], P(('dp', 'fsdp')), may hold values from 0.059814453 to 0.15917969
Outputs:
- outputs: bfloat16 [45056, 768], P(('dp', 'fsdp'))
- inputs_grad: float32 [45056, 768], P(('dp', 'fsdp'))
- in_weight_grad: float32 [768, 2304], P(('dp', 'fsdp'))
- in_bias_grad: float32 [1536], P(('dp', 'fsdp'))
- out_weight_grad: float32 [768, 768], P(('dp', 'fsdp'))
- out_bias_grad: float32 [768], P(('dp', 'fsdp'))
- first_gain_grad: float32 [768], P(('dp', 'fsdp'))
- first_shift_grad: float32 [768], P(('dp', 'fsdp'))
- first_scale_grad: float32 [768], P(('dp', 'fsdp'))
- up_weight_grad: float32 [768, 3072], P(('dp', 'fsdp'))
- up_bias_grad: float32 [3072], P(('dp', 'fsdp'))
- down_weight_grad: float32 [3072, 768], P(('dp', 'fsdp'))
- down_bias_grad: float32 [768], P(('dp', 'fsdp'))
- second_gain_grad: float32 [768], P(('dp', 'fsdp'))
- second_shift_grad: float32 [768], P(('dp', 'fsdp'))
- second_scale_grad: float32 [768], P(('dp', 'fsdp'))
Inputs may be any that keep to these rules, and one draw needn't show every extreme that they name: `segment_ids`: on every device, a quarter of all devices (rounded down, chosen by the seed) hold one image: rows 0 to 1373 have id 0; every other device holds 5 images of 261 rows each, with ids 0 to 4 in order; the remaining rows of each device are padding with id 5.
All inputs are finite; a program needn't handle non-finite values.
Results may differ from a plain program's by a relative error of at most 0.0091.
Values may be sent and summed in bfloat16 or wider, within the bound.
A program may use at most 192 MiB of HBM per device.

v0:
```python
import jax
import jax.numpy as jnp
from jax import lax
from jax.sharding import PartitionSpec as P

HD = 64
SMALLS = 5


epsilon = 1e-06


def norm_rows(values, gain, shift):
    centre = jnp.mean(values, axis=-1, keepdims=True)
    centred = values - centre
    spread = jnp.mean(centred * centred, axis=-1, keepdims=True)
    return centred * lax.rsqrt(spread + epsilon) * gain + shift


def as_float(items):
    return tuple((item.astype(jnp.float32) for item in items))


def shards(
    inputs,
    segment_ids,
    cotangent,
    in_weight,
    in_bias,
    out_weight,
    out_bias,
    first_gain,
    first_shift,
    first_scale,
    up_weight,
    up_bias,
    down_weight,
    down_bias,
    second_gain,
    second_shift,
    second_scale,
):
    row_count = inputs.shape[0]
    feature_count = inputs.shape[1]
    pair_count = feature_count // 128
    factor = HD ** (-0.5)
    attention_set = (
        lax.all_gather(in_weight, ("dp", "fsdp"), axis=0, tiled=True),
        lax.all_gather(in_bias, ("dp", "fsdp"), axis=0, tiled=True),
        lax.all_gather(out_weight, ("dp", "fsdp"), axis=0, tiled=True),
        lax.all_gather(out_bias, ("dp", "fsdp"), axis=0, tiled=True),
        lax.all_gather(first_gain, ("dp", "fsdp"), axis=0, tiled=True),
        lax.all_gather(first_shift, ("dp", "fsdp"), axis=0, tiled=True),
        lax.all_gather(first_scale, ("dp", "fsdp"), axis=0, tiled=True),
    )
    feedforward_set = (
        lax.all_gather(up_weight, ("dp", "fsdp"), axis=0, tiled=True),
        lax.all_gather(up_bias, ("dp", "fsdp"), axis=0, tiled=True),
        lax.all_gather(down_weight, ("dp", "fsdp"), axis=0, tiled=True),
        lax.all_gather(down_bias, ("dp", "fsdp"), axis=0, tiled=True),
        lax.all_gather(second_gain, ("dp", "fsdp"), axis=0, tiled=True),
        lax.all_gather(second_shift, ("dp", "fsdp"), axis=0, tiled=True),
        lax.all_gather(second_scale, ("dp", "fsdp"), axis=0, tiled=True),
    )
    full_in, full_in_bias, full_out, full_out_bias, gain_one, shift_one, scale_one = attention_set
    full_up, full_up_bias, full_down, full_down_bias, gain_two, shift_two, scale_two = (
        feedforward_set
    )
    in_bias_f, out_bias_f, gain_one_f, shift_one_f, scale_one_f = as_float(
        (full_in_bias, full_out_bias, gain_one, shift_one, scale_one)
    )
    up_bias_f, down_bias_f, gain_two_f, shift_two_f, scale_two_f = as_float(
        (full_up_bias, full_down_bias, gain_two, shift_two, scale_two)
    )
    source = inputs.astype(jnp.float32)
    same_image = segment_ids[:, None] == segment_ids[None, :]
    normed, first_norm_back = jax.vjp(norm_rows, source, gain_one_f, shift_one_f)
    normed_low = normed.astype(jnp.bfloat16)
    projected = jnp.dot(normed_low, full_in, preferred_element_type=jnp.float32)
    offsets = jnp.concatenate(
        [
            in_bias_f[:feature_count],
            jnp.zeros((feature_count,), jnp.float32),
            in_bias_f[feature_count:],
        ]
    )
    joined = (projected + offsets).astype(jnp.bfloat16)
    stacked = joined.reshape(row_count, 3, pair_count, 128).transpose(1, 2, 0, 3)

    def masked_scores(query_pair, key_pair):
        raw = (
            jnp.einsum("qhd,khd->hqk", query_pair, key_pair, preferred_element_type=jnp.float32)
            * factor
        )
        return jnp.where(same_image[None], raw, -1e30)

    def forward_pair(triple):
        query_part, key_part, value_part = triple
        query_pair = query_part.reshape(row_count, 2, HD)
        key_pair = key_part.reshape(row_count, 2, HD)
        value_pair = value_part.reshape(row_count, 2, HD)
        scores = masked_scores(query_pair, key_pair)
        row_max = jnp.max(scores, axis=-1, keepdims=True)
        expd = jnp.exp(scores - row_max)
        row_total = jnp.sum(expd, axis=-1, keepdims=True)
        probs = expd / row_total
        summary = row_max[..., 0] + jnp.log(row_total[..., 0])
        result = jnp.einsum(
            "hqk,khd->qhd",
            probs.astype(jnp.bfloat16),
            value_pair,
            preferred_element_type=jnp.float32,
        ).reshape(row_count, 128)
        return (result.astype(jnp.bfloat16), summary)

    attended_pairs, summaries = lax.map(forward_pair, (stacked[0], stacked[1], stacked[2]))
    attended = attended_pairs.transpose(1, 0, 2).reshape(row_count, feature_count)
    branch = jnp.dot(attended, full_out, preferred_element_type=jnp.float32) + out_bias_f
    middle = source + scale_one_f * branch
    normed_two, second_norm_back = jax.vjp(norm_rows, middle, gain_two_f, shift_two_f)
    normed_two_low = normed_two.astype(jnp.bfloat16)
    hidden = jnp.dot(normed_two_low, full_up, preferred_element_type=jnp.float32) + up_bias_f
    active, gelu_back = jax.vjp(lambda value: jax.nn.gelu(value, approximate=False), hidden)
    active_low = active.astype(jnp.bfloat16)
    mixed = jnp.dot(active_low, full_down, preferred_element_type=jnp.float32) + down_bias_f
    outputs = (middle + scale_two_f * mixed).astype(jnp.bfloat16)
    attention_set = (
        lax.all_gather(in_weight, ("dp", "fsdp"), axis=0, tiled=True),
        lax.all_gather(in_bias, ("dp", "fsdp"), axis=0, tiled=True),
        lax.all_gather(out_weight, ("dp", "fsdp"), axis=0, tiled=True),
        lax.all_gather(out_bias, ("dp", "fsdp"), axis=0, tiled=True),
        lax.all_gather(first_gain, ("dp", "fsdp"), axis=0, tiled=True),
        lax.all_gather(first_shift, ("dp", "fsdp"), axis=0, tiled=True),
        lax.all_gather(first_scale, ("dp", "fsdp"), axis=0, tiled=True),
    )
    feedforward_set = (
        lax.all_gather(up_weight, ("dp", "fsdp"), axis=0, tiled=True),
        lax.all_gather(up_bias, ("dp", "fsdp"), axis=0, tiled=True),
        lax.all_gather(down_weight, ("dp", "fsdp"), axis=0, tiled=True),
        lax.all_gather(down_bias, ("dp", "fsdp"), axis=0, tiled=True),
        lax.all_gather(second_gain, ("dp", "fsdp"), axis=0, tiled=True),
        lax.all_gather(second_shift, ("dp", "fsdp"), axis=0, tiled=True),
        lax.all_gather(second_scale, ("dp", "fsdp"), axis=0, tiled=True),
    )
    full_in = attention_set[0]
    full_out = attention_set[2]
    full_up = feedforward_set[0]
    full_down = feedforward_set[2]
    valid = (segment_ids < SMALLS).astype(jnp.float32)[:, None]
    upstream = cotangent.astype(jnp.float32) * valid
    second_scale_grad = jnp.sum(upstream * mixed, axis=0)
    mixed_grad = (scale_two_f * upstream).astype(jnp.bfloat16)
    down_weight_grad = jnp.dot(active_low.T, mixed_grad, preferred_element_type=jnp.float32)
    down_bias_grad = jnp.sum(mixed_grad.astype(jnp.float32), axis=0)
    active_grad = jnp.dot(mixed_grad, full_down.T, preferred_element_type=jnp.float32)
    hidden_grad = gelu_back(active_grad)[0].astype(jnp.bfloat16)
    up_weight_grad = jnp.dot(normed_two_low.T, hidden_grad, preferred_element_type=jnp.float32)
    up_bias_grad = jnp.sum(hidden_grad.astype(jnp.float32), axis=0)
    normed_two_grad = jnp.dot(hidden_grad, full_up.T, preferred_element_type=jnp.float32)
    middle_part, second_gain_grad, second_shift_grad = second_norm_back(normed_two_grad)
    middle_grad = upstream + middle_part
    feedforward_sums = (
        lax.psum_scatter(up_weight_grad, ("dp", "fsdp"), scatter_dimension=0, tiled=True),
        lax.psum_scatter(up_bias_grad, ("dp", "fsdp"), scatter_dimension=0, tiled=True),
        lax.psum_scatter(down_weight_grad, ("dp", "fsdp"), scatter_dimension=0, tiled=True),
        lax.psum_scatter(down_bias_grad, ("dp", "fsdp"), scatter_dimension=0, tiled=True),
        lax.psum_scatter(second_gain_grad, ("dp", "fsdp"), scatter_dimension=0, tiled=True),
        lax.psum_scatter(second_shift_grad, ("dp", "fsdp"), scatter_dimension=0, tiled=True),
        lax.psum_scatter(second_scale_grad, ("dp", "fsdp"), scatter_dimension=0, tiled=True),
    )
    first_scale_grad = jnp.sum(middle_grad * branch, axis=0)
    branch_grad = (scale_one_f * middle_grad).astype(jnp.bfloat16)
    out_weight_grad = jnp.dot(attended.T, branch_grad, preferred_element_type=jnp.float32)
    out_bias_grad = jnp.sum(branch_grad.astype(jnp.float32), axis=0)
    attended_grad = jnp.dot(branch_grad, full_out.T, preferred_element_type=jnp.float32).astype(
        jnp.bfloat16
    )
    attended_grad_pairs = attended_grad.reshape(row_count, pair_count, 128).transpose(1, 0, 2)

    def backward_pair(item):
        query_part, key_part, value_part, out_part, summary = item
        query_pair = query_part.reshape(row_count, 2, HD)
        key_pair = key_part.reshape(row_count, 2, HD)
        value_pair = value_part.reshape(row_count, 2, HD)
        grad_pair = out_part.reshape(row_count, 2, HD)
        scores = masked_scores(query_pair, key_pair)
        probs = jnp.exp(scores - summary[..., None])
        probs_low = probs.astype(jnp.bfloat16)
        value_grad = jnp.einsum(
            "hqk,qhd->khd", probs_low, grad_pair, preferred_element_type=jnp.float32
        )
        prob_grad = jnp.einsum(
            "qhd,khd->hqk", grad_pair, value_pair, preferred_element_type=jnp.float32
        )
        centre = jnp.sum(probs * prob_grad, axis=-1, keepdims=True)
        score_grad = (probs * (prob_grad - centre)).astype(jnp.bfloat16)
        query_grad = (
            jnp.einsum("hqk,khd->qhd", score_grad, key_pair, preferred_element_type=jnp.float32)
            * factor
        )
        key_grad = (
            jnp.einsum("hqk,qhd->khd", score_grad, query_pair, preferred_element_type=jnp.float32)
            * factor
        )
        return (
            query_grad.reshape(row_count, 128).astype(jnp.bfloat16),
            key_grad.reshape(row_count, 128).astype(jnp.bfloat16),
            value_grad.reshape(row_count, 128).astype(jnp.bfloat16),
        )

    query_grads, key_grads, value_grads = lax.map(
        backward_pair, (stacked[0], stacked[1], stacked[2], attended_grad_pairs, summaries)
    )
    joined_grad = (
        jnp.stack([query_grads, key_grads, value_grads])
        .transpose(2, 0, 1, 3)
        .reshape(row_count, 3 * feature_count)
    )
    in_weight_grad = jnp.dot(normed_low.T, joined_grad, preferred_element_type=jnp.float32)
    column_sums = jnp.sum(joined_grad.astype(jnp.float32), axis=0)
    in_bias_grad = jnp.concatenate([column_sums[:feature_count], column_sums[2 * feature_count :]])
    normed_grad = jnp.dot(joined_grad, full_in.T, preferred_element_type=jnp.float32)
    source_part, first_gain_grad, first_shift_grad = first_norm_back(normed_grad)
    inputs_grad = middle_grad + source_part
    attention_sums = (
        lax.psum_scatter(in_weight_grad, ("dp", "fsdp"), scatter_dimension=0, tiled=True),
        lax.psum_scatter(in_bias_grad, ("dp", "fsdp"), scatter_dimension=0, tiled=True),
        lax.psum_scatter(out_weight_grad, ("dp", "fsdp"), scatter_dimension=0, tiled=True),
        lax.psum_scatter(out_bias_grad, ("dp", "fsdp"), scatter_dimension=0, tiled=True),
        lax.psum_scatter(first_gain_grad, ("dp", "fsdp"), scatter_dimension=0, tiled=True),
        lax.psum_scatter(first_shift_grad, ("dp", "fsdp"), scatter_dimension=0, tiled=True),
        lax.psum_scatter(first_scale_grad, ("dp", "fsdp"), scatter_dimension=0, tiled=True),
    )
    return (
        outputs,
        inputs_grad,
        attention_sums[0],
        attention_sums[1],
        attention_sums[2],
        attention_sums[3],
        attention_sums[4],
        attention_sums[5],
        attention_sums[6],
        feedforward_sums[0],
        feedforward_sums[1],
        feedforward_sums[2],
        feedforward_sums[3],
        feedforward_sums[4],
        feedforward_sums[5],
        feedforward_sums[6],
    )


def solution(mesh):
    return jax.shard_map(
        shards,
        mesh=mesh,
        in_specs=(
            P(("dp", "fsdp"), None),
            P(("dp", "fsdp")),
            P(("dp", "fsdp"), None),
            P(("dp", "fsdp"), None),
            P(("dp", "fsdp")),
            P(("dp", "fsdp"), None),
            P(("dp", "fsdp")),
            P(("dp", "fsdp")),
            P(("dp", "fsdp")),
            P(("dp", "fsdp")),
            P(("dp", "fsdp"), None),
            P(("dp", "fsdp")),
            P(("dp", "fsdp"), None),
            P(("dp", "fsdp")),
            P(("dp", "fsdp")),
            P(("dp", "fsdp")),
            P(("dp", "fsdp")),
        ),
        out_specs=(
            P(("dp", "fsdp"), None),
            P(("dp", "fsdp"), None),
            P(("dp", "fsdp"), None),
            P(("dp", "fsdp")),
            P(("dp", "fsdp"), None),
            P(("dp", "fsdp")),
            P(("dp", "fsdp")),
            P(("dp", "fsdp")),
            P(("dp", "fsdp")),
            P(("dp", "fsdp"), None),
            P(("dp", "fsdp")),
            P(("dp", "fsdp"), None),
            P(("dp", "fsdp")),
            P(("dp", "fsdp")),
            P(("dp", "fsdp")),
            P(("dp", "fsdp")),
        ),
        check_vma=False,
    )
```

profile of v0, /device:TPU:0, one launch (start us, length us, event | category | flops | bytes accessed | tf_op | source)
XLA Modules:
  0.0 1150.8 jit_solution(7094091919058666021)
XLA Ops:
  18.4 42.9 %all-reduce.21 = (bf16[1536]{0:T(1024)(128)(2,1)S(1)}, bf16[768]{0:T(1024)(128)(2,1)S(1)}, bf16[768]{0:T(1024)(128)(2,1)S(1)}, bf16[768]{0:T(1024)(128)(2,1)S(1)...) all-reduce(bf16[1536]{0:T(1024)(128)(2,1)S(1)} %dynamic-update-slic, ...), channel_id=1, replica_groups=mesh['dp'=4,'fsdp'=8] {'dp','fsdp'}, use_global_device_ids=true, to_apply=%add.3 | all-reduce | flops 10752 | bytes 43008
  75.0 10.1 fusion.20
  85.1 9.7 copy.66
  102.2 169.5 %while.28 = (s32[]{:T(128)}, bf16[6,1408,128]{1,2,0:T(8,128)(2,1)}, f32[6,2,1408]{2,1,0:T(2,128)}, bf16[6,1408,128]{1,2,0:T(8,128)(2,1)}, bf16[6,1408,128]{1,2,0...) while((s32[]{:T(128)}, bf16[6,1408,128]{1,2,0:T(8,128)(2,1)}, ...), condition=%wide.region_5.6_spmd.clone, body=%wide.region_2.5_spmd.clone.sunk | while | flops 1048900864 | bytes 55965292 | solution.py:116
  121.0 8.4 fusion.107
  177.3 8.4 fusion.107
  205.4 8.4 fusion.107
  233.5 8.4 fusion.107
  262.0 8.4 fusion.107
  282.8 49.9 %multiply_convert_fusion.1 = (bf16[1408,3072]{1,0:T(8,128)(2,1)}, f32[1408,3072]{1,0:T(8,128)}, f32[1408,3072]{1,0:T(8,128)}) fusion(f32[3072]{0:T(1024)S(1)} %copy-done.46, bf16[768,3072]{1,0:T(8,128)(2,1)} %all-gather.9.cloned.1.call-done, bf16[1408,768]{0,1:T(8,128)(2,1)} %add_convert_fusion.4.clone.4), kind=kOutput, calls=%fused_computation.37 | convolution fusion | flops 6929252352 | bytes 50147328 | tf_op jit(solution)/shard_map/dot_general | solution.py:122
  332.8 23.0 %convert_reduce_fusion = (f32[3072]{0:T(1024)}, bf16[1408,3072]{1,0:T(8,128)(2,1)}) fusion(f32[1408,3072]{1,0:T(8,128)} %get-tuple-element.269, bf16[3072,768]{1,0:T(8,128)(2,1)} %all-gather.11.cloned.1.call-done, bf16[1408,768]{0,1:T(8,128)(2,1)S(1)} %copy-done.10, f32[1408]{0:T(1024)S(1)} %copy-done.34, f32[768]{0:T(1024)S(1)} %copy-done.48, ...), kind=kOutput, calls=%fused_computation.35 | convolution fusion | flops 6721631232 | bytes 50168320 | tf_op jit(solution)/shard_map/dot_general | solution.py:155
  355.8 11.7 %fusion.47 = (f32[768]{0:T(1024)}, f32[1408,768]{1,0:T(8,128)}) fusion(bf16[1408,3072]{1,0:T(8,128)(2,1)} %get-tuple-element.294, bf16[768,3072]{1,0:T(8,128)(2,1)S(1)} %copy-done.56), kind=kOutput, calls=%fused_computation.114 | convolution fusion | flops 6644857856 | bytes 17697792 | tf_op jit(solution)/shard_map/dot_general | solution.py:159
  395.8 328.0 %while.29 = (s32[]{:T(128)}, bf16[6,1408,128]{1,2,0:T(8,128)(2,1)}, bf16[6,1408,128]{1,2,0:T(8,128)(2,1)}, bf16[6,1408,128]{1,2,0:T(8,128)(2,1)S(1)}, bf16[6,140...) while((s32[]{:T(128)}, bf16[6,1408,128]{1,2,0:T(8,128)(2,1)}, ...), condition=%wide.region_12.13_spmd.clone, body=%wide.region_10.12_spmd.clone.sunk | while | flops 2576119040 | bytes 226783952 | solution.py:211
  409.9 11.7 %multiply_reduce_fusion.7 = (f32[2,1408]{1,0:T(2,128)S(1)}, f32[2,1408,1408]{1,2,0:T(8,128)}) fusion(f32[2,1408,1408]{1,2,0:T(8,128)} %fusion.118, f32[2,1408]{1,0:T(2,128)S(1)} %dynamic-slice_bitcast_fusion.2, bf16[1408,2,64]{0,2,1:T(8,128)(2,1)S(1)} %bitcast.136, bf16[1408,2,64]{0,2,1:T(8,128)(2,1)S(1)} %bitcast.131, ...), kind=kOutput, calls=%fused_computation.15.clone.1 | convolution fusion | flops 527332608 | bytes 34445312 | tf_op jit(solution)/shard_map/while/body/eval_jaxpr/qhd,khd->hqk/dot_general | solution.py:92
  421.7 14.6 %multiply_convert_fusion.8 = bf16[2,1408,1408]{1,2,0:T(8,128)(2,1)} fusion(f32[2,1408,1408]{1,2,0:T(8,128)} %get-tuple-element.413, f32[2,1408,1408]{1,2,0:T(8,128)} %fusion.118, f32[2,1408]{1,0:T(2,128)S(1)} %get-tuple-element.414), kind=kLoop, calls=%fused_computation.14.clone.1 | loop fusion | flops 11894784 | bytes 39660544 | tf_op jit(solution)/shard_map/while/body/eval_jaxpr/convert_element_type | solution.py:196
  465.1 11.7 %multiply_reduce_fusion.7 = (f32[2,1408]{1,0:T(2,128)S(1)}, f32[2,1408,1408]{1,2,0:T(8,128)}) fusion(f32[2,1408,1408]{1,2,0:T(8,128)} %fusion.118, f32[2,1408]{1,0:T(2,128)S(1)} %dynamic-slice_bitcast_fusion.2, bf16[1408,2,64]{0,2,1:T(8,128)(2,1)S(1)} %bitcast.136, bf16[1408,2,64]{0,2,1:T(8,128)(2,1)S(1)} %bitcast.131, ...), kind=kOutput, calls=%fused_computation.15.clone.1 | convolution fusion | flops 527332608 | bytes 34445312 | tf_op jit(solution)/shard_map/while/body/eval_jaxpr/qhd,khd->hqk/dot_general | solution.py:92
  476.8 14.4 %multiply_convert_fusion.8 = bf16[2,1408,1408]{1,2,0:T(8,128)(2,1)} fusion(f32[2,1408,1408]{1,2,0:T(8,128)} %get-tuple-element.413, f32[2,1408,1408]{1,2,0:T(8,128)} %fusion.118, f32[2,1408]{1,0:T(2,128)S(1)} %get-tuple-element.414), kind=kLoop, calls=%fused_computation.14.clone.1 | loop fusion | flops 11894784 | bytes 39660544 | tf_op jit(solution)/shard_map/while/body/eval_jaxpr/convert_element_type | solution.py:196
  519.8 11.6 %multiply_reduce_fusion.7 = (f32[2,1408]{1,0:T(2,128)S(1)}, f32[2,1408,1408]{1,2,0:T(8,128)}) fusion(f32[2,1408,1408]{1,2,0:T(8,128)} %fusion.118, f32[2,1408]{1,0:T(2,128)S(1)} %dynamic-slice_bitcast_fusion.2, bf16[1408,2,64]{0,2,1:T(8,128)(2,1)S(1)} %bitcast.136, bf16[1408,2,64]{0,2,1:T(8,128)(2,1)S(1)} %bitcast.131, ...), kind=kOutput, calls=%fused_computation.15.clone.1 | convolution fusion | flops 527332608 | bytes 34445312 | tf_op jit(solution)/shard_map/while/body/eval_jaxpr/qhd,khd->hqk/dot_general | solution.py:92
  531.4 14.3 %multiply_convert_fusion.8 = bf16[2,1408,1408]{1,2,0:T(8,128)(2,1)} fusion(f32[2,1408,1408]{1,2,0:T(8,128)} %get-tuple-element.413, f32[2,1408,1408]{1,2,0:T(8,128)} %fusion.118, f32[2,1408]{1,0:T(2,128)S(1)} %get-tuple-element.414), kind=kLoop, calls=%fused_computation.14.clone.1 | loop fusion | flops 11894784 | bytes 39660544 | tf_op jit(solution)/shard_map/while/body/eval_jaxpr/convert_element_type | solution.py:196
  574.3 11.6 %multiply_reduce_fusion.7 = (f32[2,1408]{1,0:T(2,128)S(1)}, f32[2,1408,1408]{1,2,0:T(8,128)}) fusion(f32[2,1408,1408]{1,2,0:T(8,128)} %fusion.118, f32[2,1408]{1,0:T(2,128)S(1)} %dynamic-slice_bitcast_fusion.2, bf16[1408,2,64]{0,2,1:T(8,128)(2,1)S(1)} %bitcast.136, bf16[1408,2,64]{0,2,1:T(8,128)(2,1)S(1)} %bitcast.131, ...), kind=kOutput, calls=%fused_computation.15.clone.1 | convolution fusion | flops 527332608 | bytes 34445312 | tf_op jit(solution)/shard_map/while/body/eval_jaxpr/qhd,khd->hqk/dot_general | solution.py:92
  585.9 14.3 %multiply_convert_fusion.8 = bf16[2,1408,1408]{1,2,0:T(8,128)(2,1)} fusion(f32[2,1408,1408]{1,2,0:T(8,128)} %get-tuple-element.413, f32[2,1408,1408]{1,2,0:T(8,128)} %fusion.118, f32[2,1408]{1,0:T(2,128)S(1)} %get-tuple-element.414), kind=kLoop, calls=%fused_computation.14.clone.1 | loop fusion | flops 11894784 | bytes 39660544 | tf_op jit(solution)/shard_map/while/body/eval_jaxpr/convert_element_type | solution.py:196
  628.8 11.6 %multiply_reduce_fusion.7 = (f32[2,1408]{1,0:T(2,128)S(1)}, f32[2,1408,1408]{1,2,0:T(8,128)}) fusion(f32[2,1408,1408]{1,2,0:T(8,128)} %fusion.118, f32[2,1408]{1,0:T(2,128)S(1)} %dynamic-slice_bitcast_fusion.2, bf16[1408,2,64]{0,2,1:T(8,128)(2,1)S(1)} %bitcast.136, bf16[1408,2,64]{0,2,1:T(8,128)(2,1)S(1)} %bitcast.131, ...), kind=kOutput, calls=%fused_computation.15.clone.1 | convolution fusion | flops 527332608 | bytes 34445312 | tf_op jit(solution)/shard_map/while/body/eval_jaxpr/qhd,khd->hqk/dot_general | solution.py:92
  640.4 14.3 %multiply_convert_fusion.8 = bf16[2,1408,1408]{1,2,0:T(8,128)(2,1)} fusion(f32[2,1408,1408]{1,2,0:T(8,128)} %get-tuple-element.413, f32[2,1408,1408]{1,2,0:T(8,128)} %fusion.118, f32[2,1408]{1,0:T(2,128)S(1)} %get-tuple-element.414), kind=kLoop, calls=%fused_computation.14.clone.1 | loop fusion | flops 11894784 | bytes 39660544 | tf_op jit(solution)/shard_map/while/body/eval_jaxpr/convert_element_type | solution.py:196
  683.2 11.6 %multiply_reduce_fusion.7 = (f32[2,1408]{1,0:T(2,128)S(1)}, f32[2,1408,1408]{1,2,0:T(8,128)}) fusion(f32[2,1408,1408]{1,2,0:T(8,128)} %fusion.118, f32[2,1408]{1,0:T(2,128)S(1)} %dynamic-slice_bitcast_fusion.2, bf16[1408,2,64]{0,2,1:T(8,128)(2,1)S(1)} %bitcast.136, bf16[1408,2,64]{0,2,1:T(8,128)(2,1)S(1)} %bitcast.131, ...), kind=kOutput, calls=%fused_computation.15.clone.1 | convolution fusion | flops 527332608 | bytes 34445312 | tf_op jit(solution)/shard_map/while/body/eval_jaxpr/qhd,khd->hqk/dot_general | solution.py:92
  694.9 14.3 %multiply_convert_fusion.8 = bf16[2,1408,1408]{1,2,0:T(8,128)(2,1)} fusion(f32[2,1408,1408]{1,2,0:T(8,128)} %get-tuple-element.413, f32[2,1408,1408]{1,2,0:T(8,128)} %fusion.118, f32[2,1408]{1,0:T(2,128)S(1)} %get-tuple-element.414), kind=kLoop, calls=%fused_computation.14.clone.1 | loop fusion | flops 11894784 | bytes 39660544 | tf_op jit(solution)/shard_map/while/body/eval_jaxpr/convert_element_type | solution.py:196
  739.1 13.6 %fusion.39 = f32[768,3072]{1,0:T(8,128)} fusion(bf16[1408,3072]{1,0:T(8,128)(2,1)} %get-tuple-element.294, f32[1408,768]{0,1:T(8,128)} %copy-done.2, f32[768]{0:T(1024)S(1)} %copy-done.44, f32[768]{0:T(1024)S(1)} %copy-done.31, f32[1408]{0:T(1024)S(1)} %copy-done.24, f32[1408]{0:T(1024)S(1)} %copy-done.19), kind=kOutput, calls=%fused_computation.107 | convolution fusion | flops 6649184256 | bytes 22430720 | tf_op jit(solution)/shard_map/dot_general | solution.py:157
  754.4 12.7 %fusion.38 = f32[3072,768]{1,0:T(8,128)} fusion(bf16[1408,3072]{1,0:T(8,128)(2,1)} %get-tuple-element.268, bf16[1408,768]{0,1:T(8,128)(2,1)S(1)} %copy-done.11, f32[1408]{0:T(1024)S(1)} %copy-done.35, f32[768]{0:T(1024)S(1)} %copy-done.49), kind=kOutput, calls=%fused_computation.106 | convolution fusion | flops 6648102912 | bytes 20259328 | tf_op jit(solution)/shard_map/dot_general | solution.py:153
  767.8 11.6 %fusion.46 = (f32[768]{0:T(1024)S(1)}, f32[1408,768]{1,0:T(8,128)}) fusion(bf16[1408,2304]{0,1:T(8,128)(2,1)} %bitcast.154, bf16[768,2304]{1,0:T(8,128)(2,1)} %all-gather.5.cloned.1.call-done), kind=kOutput, calls=%fused_computation.113 | convolution fusion | flops 4983913472 | bytes 14355456 | tf_op jit(solution)/shard_map/dot_general | solution.py:222
  792.2 21.5 %multiply_reduce_fusion.1 = (f32[768]{0:T(1024)S(1)}, f32[768]{0:T(1024)S(1)}, f32[768]{0:T(1024)S(1)}, f32[1408,768]{0,1:T(8,128)}, bf16[1408,768]{0,1:T(8,128)(2,1)}) fusion(bf16[1408,768]{0,1:T(8,128)(2,1)} %copy.68, f32[1408]{0:T(1024)S(1)} %copy-done.35, f32[768]{0:T(1024)S(1)} %convert_element_type.166, f32[768]{0:T(1024)S(1)} %copy-done.49, ...), kind=kOutput, calls=%fused_computation.71 | convolution fusion | flops 6671889408 | bytes 41539584 | tf_op jit(solution)/shard_map/dot_general | solution.py:125
  813.8 43.8 %all-reduce.20 = (f32[1536]{0:T(1024)S(1)}, f32[768]{0:T(1024)S(1)}, f32[768]{0:T(1024)S(1)}, f32[768]{0:T(1024)S(1)}, f32[768]{0:T(1024)S(1)}, /*index=5*/f32[3...) all-reduce(f32[1536]{0:T(1024)S(1)} %pad_maximum_fusion.2, ...), channel_id=3, replica_groups=mesh['dp'=4,'fsdp'=8] {'dp','fsdp'}, use_global_device_ids=true, to_apply=%region_17.18.clone | all-reduce | flops 10752 | bytes 86016
  873.3 128.6 %reduce-scatter.9.cloned.1.call-done = f32[24,3072]{1,0:T(8,128)} async-done(((f32[768,3072]{1,0:T(8,128)}), f32[24,3072]{1,0:T(8,128)}) %reduce-scatter.9.cloned.1.call-update) | async-done | bytes 294928 | tf_op jit(solution)/shard_map/reduce_scatter | solution.py:163
  1001.9 141.6 %reduce-scatter.11.cloned.1.call-done = f32[96,768]{1,0:T(8,128)} async-done(((f32[3072,768]{1,0:T(8,128)}), f32[96,768]{1,0:T(8,128)}) %reduce-scatter.11.cloned.1.call-update) | async-done | bytes 294928 | tf_op jit(solution)/shard_map/reduce_scatter | solution.py:165
  (362 shorter events, 416.0 us)
Async XLA Ops:
  7.2 67.8 %all-gather.5.cloned.1.call-start = ((), (), s32[]{:S(2)}) async-start(), calls=%async_computation.4 | async-start | bytes 3649536 | tf_op jit(solution)/shard_map/all_gather | solution.py:48
  7.9 263.9 %all-gather.7.cloned.1.call-start = ((), (), s32[]{:S(2)}) async-start(), calls=%async_computation.5 | async-start | bytes 1216512 | tf_op jit(solution)/shard_map/all_gather | solution.py:50
  8.7 274.1 %all-gather.9.cloned.1.call-start = ((), (), s32[]{:S(2)}) async-start(), calls=%async_computation.6 | async-start | bytes 4866048 | tf_op jit(solution)/shard_map/all_gather | solution.py:57
  9.4 323.4 %all-gather.11.cloned.1.call-start = ((), (), s32[]{:S(2)}) async-start(), calls=%async_computation.7 | async-start | bytes 4866048 | tf_op jit(solution)/shard_map/all_gather | solution.py:59
  10.0 863.3 %reduce-scatter.7.cloned.1.call-start = ((), (), s32[]{:S(2)}) async-start(), calls=%async_computation.9 | async-start | bytes 2433024 | tf_op jit(solution)/shard_map/reduce_scatter | solution.py:228
  61.4 13.6 %copy-start.32 = (f32[768]{0:T(1024)}, f32[768]{0:T(1024)S(1)}, u32[]{:S(2)}) copy-start(f32[768]{0:T(1024)S(1)} %convert_element_type.154) | copy-start | bytes 9220
  62.6 12.4 %copy-start.52 = (f32[768]{0:T(1024)}, f32[768]{0:T(1024)S(1)}, u32[]{:S(2)}) copy-start(f32[768]{0:T(1024)S(1)} %convert_element_type.155) | copy-start | bytes 9220
  69.6 15.5 %copy-start.20 = (f32[1408]{0:T(1024)}, f32[1408]{0:T(1024)S(1)}, u32[]{:S(2)}) copy-start(f32[1408]{0:T(1024)S(1)} %broadcast_multiply_fusion.1) | copy-start | bytes 16900
  70.8 14.3 %copy-start.36 = (f32[1408]{0:T(1024)}, f32[1408]{0:T(1024)S(1)}, u32[]{:S(2)}) copy-start(f32[1408]{0:T(1024)S(1)} %fusion.33) | copy-start | bytes 16900
  94.8 7.4 copy-start.13
  102.2 169.6 %copy-start.4 = (bf16[1408,768]{0,1:T(8,128)(2,1)S(1)}, bf16[1408,768]{0,1:T(8,128)(2,1)}, u32[]{:S(2)}) copy-start(bf16[1408,768]{0,1:T(8,128)(2,1)} %copy-done.3) | copy-start | bytes 6488068
  102.2 169.6 %copy-start.40 = (f32[768]{0:T(1024)S(1)}, f32[768]{0:T(1024)}, u32[]{:S(2)}) copy-start(f32[768]{0:T(1024)} %convert_element_type.153) | copy-start | bytes 9220
  102.2 169.6 %copy-start.50 = (f32[768]{0:T(1024)S(1)}, f32[768]{0:T(1024)}, u32[]{:S(2)}) copy-start(f32[768]{0:T(1024)} %convert_element_type.159) | copy-start | bytes 9220
  282.8 50.0 %copy-start.10 = (bf16[1408,768]{0,1:T(8,128)(2,1)S(1)}, bf16[1408,768]{0,1:T(8,128)(2,1)}, u32[]{:S(2)}) copy-start(bf16[1408,768]{0,1:T(8,128)(2,1)} %copy.68) | copy-start | bytes 6488068
  282.8 50.0 %copy-start.34 = (f32[1408]{0:T(1024)S(1)}, f32[1408]{0:T(1024)}, u32[]{:S(2)}) copy-start(f32[1408]{0:T(1024)} %compare_convert_fusion) | copy-start | bytes 16900
  282.8 50.0 %copy-start.48 = (f32[768]{0:T(1024)S(1)}, f32[768]{0:T(1024)}, u32[]{:S(2)}) copy-start(f32[768]{0:T(1024)} %convert_element_type.160) | copy-start | bytes 9220
  332.8 23.0 %copy-start.56 = (bf16[768,3072]{1,0:T(8,128)(2,1)S(1)}, bf16[768,3072]{1,0:T(8,128)(2,1)}, u32[]{:S(2)}) copy-start(bf16[768,3072]{1,0:T(8,128)(2,1)} %all-gather.9.cloned.1.call-done) | copy-start | bytes 14155780
  367.5 11.3 slice-start
  387.6 485.7 %reduce-scatter.5.cloned.1.call-start = ((), (), s32[]{:S(2)}) async-start(), calls=%async_computation.8 | async-start | bytes 7299072 | tf_op jit(solution)/shard_map/reduce_scatter | solution.py:226
  421.7 18.0 %copy-start = (f32[2,1408,1408]{1,2,0:T(8,128)S(1)}, f32[2,1408,1408]{1,2,0:T(8,128)}, u32[]{:S(2)}) copy-start(f32[2,1408,1408]{1,2,0:T(8,128)} %get-tuple-element.413) | copy-start | bytes 47579140 | tf_op jit(solution)/shard_map/while
  476.8 17.6 %copy-start = (f32[2,1408,1408]{1,2,0:T(8,128)S(1)}, f32[2,1408,1408]{1,2,0:T(8,128)}, u32[]{:S(2)}) copy-start(f32[2,1408,1408]{1,2,0:T(8,128)} %get-tuple-element.413) | copy-start | bytes 47579140 | tf_op jit(solution)/shard_map/while
  531.4 17.5 %copy-start = (f32[2,1408,1408]{1,2,0:T(8,128)S(1)}, f32[2,1408,1408]{1,2,0:T(8,128)}, u32[]{:S(2)}) copy-start(f32[2,1408,1408]{1,2,0:T(8,128)} %get-tuple-element.413) | copy-start | bytes 47579140 | tf_op jit(solution)/shard_map/while
  585.9 17.5 %copy-start = (f32[2,1408,1408]{1,2,0:T(8,128)S(1)}, f32[2,1408,1408]{1,2,0:T(8,128)}, u32[]{:S(2)}) copy-start(f32[2,1408,1408]{1,2,0:T(8,128)} %get-tuple-element.413) | copy-start | bytes 47579140 | tf_op jit(solution)/shard_map/while
  640.4 17.5 %copy-start = (f32[2,1408,1408]{1,2,0:T(8,128)S(1)}, f32[2,1408,1408]{1,2,0:T(8,128)}, u32[]{:S(2)}) copy-start(f32[2,1408,1408]{1,2,0:T(8,128)} %get-tuple-element.413) | copy-start | bytes 47579140 | tf_op jit(solution)/shard_map/while
  694.9 17.5 %copy-start = (f32[2,1408,1408]{1,2,0:T(8,128)S(1)}, f32[2,1408,1408]{1,2,0:T(8,128)}, u32[]{:S(2)}) copy-start(f32[2,1408,1408]{1,2,0:T(8,128)} %get-tuple-element.413) | copy-start | bytes 47579140 | tf_op jit(solution)/shard_map/while
  738.4 263.5 %reduce-scatter.9.cloned.1.call-start = ((), (), s32[]{:S(2)}) async-start(), calls=%async_computation.10 | async-start | bytes 9732096 | tf_op jit(solution)/shard_map/reduce_scatter | solution.py:163
  752.7 390.7 %reduce-scatter.11.cloned.1.call-start = ((), (), s32[]{:S(2)}) async-start(), calls=%async_computation.11 | async-start | bytes 9732096 | tf_op jit(solution)/shard_map/reduce_scatter | solution.py:165
  779.3 12.8 %slice-start.2 = ((s8[4325376]{0:T(1024)(128)(4,1)}), s8[131072]{0:T(1024)(128)(4,1)S(1)}, s32[]{:S(2)}) async-start(s8[4325376]{0:T(1024)(128)(4,1)} %bitcast.140), calls=%async_computation.14 | async-start | bytes 262144
  792.2 21.6 %copy-start.42 = (f32[768]{0:T(1024)S(1)}, f32[768]{0:T(1024)}, u32[]{:S(2)}) copy-start(f32[768]{0:T(1024)} %get-tuple-element.262) | copy-start | bytes 9220
  792.2 21.6 %copy-start.45 = (f32[768]{0:T(1024)S(1)}, f32[768]{0:T(1024)}, u32[]{:S(2)}) copy-start(f32[768]{0:T(1024)} %get-tuple-element.201) | copy-start | bytes 9220
  792.2 21.6 %copy-start.47 = (f32[3072]{0:T(1024)S(1)}, f32[3072]{0:T(1024)}, u32[]{:S(2)}) copy-start(f32[3072]{0:T(1024)} %get-tuple-element.293) | copy-start | bytes 36868
  792.2 21.6 %copy-start.54 = (f32[768]{0:T(1024)S(1)}, f32[768]{0:T(1024)}, u32[]{:S(2)}) copy-start(f32[768]{0:T(1024)} %get-tuple-element.295) | copy-start | bytes 9220
  (48 other events, 176.2 us)
Sparse Core Ops, SparseCore 0:
  10.9 62.9 all-gather.4
  76.8 52.8 all-gather.6
  132.6 62.3 all-gather.8
  197.8 61.8 all-gather.10
  387.7 101.2 reduce-scatter.6
  738.5 121.4 reduce-scatter.4
  866.5 135.3 reduce-scatter.8
  1008.4 135.0 reduce-scatter.10
where the time goes:
time: 1160 us; the launch traced here: 1150 us
  matrix products  446 us (38%)
  waiting for transfers between devices  273 us (24%)
  other arithmetic  179 us (15%)
  local copies, waits for them, and re-layouts  150 us (13%)
  blocking collectives  86.7 us (7%)
  between operations  15.1 us (1%)
    reduce_scatter x1, waiting for transfers between devices, shards(): lax.psum_scatter(down_weight_grad, ('dp', 'fsdp'), scatter_dimension=0, t...  142 us
    reduce_scatter x1, waiting for transfers between devices, shards(): lax.psum_scatter(up_weight_grad, ('dp', 'fsdp'), scatter_dimension=0, til...  129 us
    dot_general x12, matrix products, masked_scores(): jnp.einsum('qhd,khd->hqk', query_pair, key_pair, preferred_element_type=j...  113 us
    unnamed x2, blocking collectives  86.7 us
    convert_element_type x6, other arithmetic, backward_pair(): score_grad = (probs * (prob_grad - centre)).astype(jnp.bfloat16)  86.3 us
    dot_general x6, matrix products, forward_pair(): jnp.einsum('hqk,khd->qhd', probs.astype(jnp.bfloat16), value_pair, prefer...  50.3 us
    dot_general x1, matrix products, shards(): jnp.dot(normed_two_low, full_up, preferred_element_type=jnp.float32)  49.9 us
    dot_general x6, matrix products, backward_pair(): jnp.einsum('qhd,khd->hqk', grad_pair, value_pair, preferred_element_type=...  46.4 us
  transfers between devices with their start and end apart: 8, of which 2 were waited for; matrix products, arithmetic and copies ran while one was open for 60% of the time, Pallas kernels for 0%

commit v1 on v0

v1 whole, which is shorter than its diff:
```python
import functools

import jax
import jax.numpy as jnp
from jax import lax
from jax.experimental import pallas as pl
from jax.experimental.pallas import tpu as pltpu
from jax.sharding import PartitionSpec as P

HD = 64
PADDING = 5
EPSILON = 1e-06
LOG2E = 1.4426950408889634
FAR = -1e30
BF = jnp.bfloat16
F32 = jnp.float32
AXES = ("dp", "fsdp")
VMEM_LIMIT = 62 * 1024 * 1024


def dot(a, b, da, db):
    return lax.dot_general(a, b, (((da,), (db,)), ((), ())), preferred_element_type=F32)


def params(**more):
    return pltpu.CompilerParams(vmem_limit_bytes=VMEM_LIMIT, **more)


def cost(flops, moved, special=0):
    return pl.CostEstimate(flops=int(flops), bytes_accessed=int(moved), transcendentals=int(special))


def whole(shape):
    return pl.BlockSpec(shape, lambda *_: (0,) * len(shape), pipeline_mode=pl.Buffered(1))


def row_loop(rows, size, body):
    def step(index, carry):
        body(pl.ds(pl.multiple_of(index * size, size), size))
        return carry

    lax.fori_loop(0, rows // size, step, 0)


def normalised(values):
    centred = values - jnp.mean(values, axis=-1, keepdims=True)
    spread = jnp.mean(centred * centred, axis=-1, keepdims=True)
    inverse = lax.rsqrt(spread + EPSILON)
    return centred * inverse, inverse


def norm_back(unit, inverse, scaled):
    return inverse * (
        scaled
        - jnp.mean(scaled, axis=-1, keepdims=True)
        - unit * jnp.mean(scaled * unit, axis=-1, keepdims=True)
    )


def project_kernel(x_ref, w_ref, gain_ref, shift_ref, offset_ref, a1_ref, qkv_ref):
    @pl.when(pl.program_id(0) == 0)
    def _():
        def body(rows):
            unit, _ = normalised(x_ref[rows, :].astype(F32))
            a1_ref[rows, :] = (unit * gain_ref[...] + shift_ref[...]).astype(BF)

        row_loop(x_ref.shape[0], 32, body)

    qkv_ref[...] = (dot(a1_ref[...], w_ref[...], 1, 0) + offset_ref[...]).astype(BF)


def project(x, w_in, gain, shift, offset):
    rows, d = x.shape
    return pl.pallas_call(
        project_kernel,
        grid=(3,),
        in_specs=[
            whole((rows, d)),
            pl.BlockSpec((d, d), lambda t: (0, t)),
            whole((1, d)),
            whole((1, d)),
            pl.BlockSpec((1, d), lambda t: (0, t)),
        ],
        out_specs=[whole((rows, d)), pl.BlockSpec((rows, d), lambda t: (0, t))],
        out_shape=[
            jax.ShapeDtypeStruct((rows, d), BF),
            jax.ShapeDtypeStruct((rows, 3 * d), BF),
        ],
        compiler_params=params(),
        cost_estimate=cost(6 * rows * d * d, 2 * (5 * rows * d + 3 * d * d)),
        name="project",
    )(x, w_in, gain, shift, offset)


def chunks(rows, size):
    return [(start, min(size, rows - start)) for start in range(0, rows, size)]


def attend_kernel(chunk, q_ref, k_ref, v_ref, mark_ref, far_ref, o_ref, e_ref, inv_ref, vt_ref, k2_ref):
    rows = q_ref.shape[0]
    vt_ref[...] = v_ref[...].astype(F32).T.astype(BF)
    low = lax.broadcasted_iota(jnp.int32, (1, 128), 1) < HD
    for half in range(2):
        mine = low if half == 0 else jnp.logical_not(low)
        k2_ref[half] = jnp.where(mine, k_ref[...], far_ref[...])
    for start, size in chunks(rows, chunk):
        for half in range(2):
            mine = low if half == 0 else jnp.logical_not(low)
            span = pl.ds(start, size)
            query = jnp.where(mine, q_ref[span, :], mark_ref[span, :])
            scores = dot(k2_ref[half], query, 1, 1)
            top = jnp.max(scores, axis=0, keepdims=True)
            weights = jnp.exp2((scores - top) * (LOG2E * HD ** (-0.5)))
            total = jnp.sum(weights, axis=0, keepdims=True)
            weights_low = weights.astype(BF)
            e_ref[half, :, span] = weights_low
            inverse = 1.0 / total
            inv_ref[0, half : half + 1, span] = inverse
            head = pl.ds(half * HD, HD)
            o_ref[head, span] = (dot(vt_ref[head, :], weights_low, 1, 0) * inverse).astype(BF)


def attend(qkv, mark, far, chunk=256):
    rows, width = qkv.shape
    pairs = width // 384
    return pl.pallas_call(
        functools.partial(attend_kernel, chunk),
        grid=(pairs,),
        in_specs=[
            pl.BlockSpec((rows, 128), lambda p: (0, p)),
            pl.BlockSpec((rows, 128), lambda p: (0, pairs + p)),
            pl.BlockSpec((rows, 128), lambda p: (0, 2 * pairs + p)),
            whole((rows, 128)),
            whole((rows, 128)),
        ],
        out_specs=[
            pl.BlockSpec((128, rows), lambda p: (p, 0)),
            pl.BlockSpec((2, rows, rows), lambda p: (p, 0, 0)),
            pl.BlockSpec((1, 2, rows), lambda p: (p, 0, 0)),
        ],
        out_shape=[
            jax.ShapeDtypeStruct((pairs * 128, rows), BF),
            jax.ShapeDtypeStruct((2 * pairs, rows, rows), BF),
            jax.ShapeDtypeStruct((pairs, 2, rows), F32),
        ],
        scratch_shapes=[pltpu.VMEM((128, rows), BF), pltpu.VMEM((2, rows, 128), BF)],
        compiler_params=params(),
        cost_estimate=cost(2 * pairs * 4 * rows * rows * 256, 4 * pairs * rows * rows, 2 * pairs * rows * rows),
        name="attend",
    )(qkv, qkv, qkv, mark, far)


def middle_kernel(o_ref, x_ref, g_ref, w_ref, vec_ref, m1_ref, a2_ref, gm_ref, gmsum_ref):
    bias, scale1, gain2, shift2, scale2 = (vec_ref[i : i + 1, :] for i in range(5))
    m1_ref[...] = dot(o_ref[...], w_ref[...], 0, 0)
    gmsum_ref[...] = jnp.zeros_like(gmsum_ref)

    def body(rows):
        m1 = x_ref[rows, :].astype(F32) + scale1 * (m1_ref[rows, :] + bias)
        m1_ref[rows, :] = m1
        unit, _ = normalised(m1)
        a2_ref[rows, :] = (unit * gain2 + shift2).astype(BF)
        gm = (scale2 * g_ref[rows, :].astype(F32)).astype(BF)
        gm_ref[rows, :] = gm
        gmsum_ref[...] += jnp.sum(gm.astype(F32).reshape(-1, 8, gm.shape[-1]), axis=0)

    row_loop(x_ref.shape[0], 32, body)


def middle(o, x, g, w_out, vec):
    rows, d = x.shape
    return pl.pallas_call(
        middle_kernel,
        out_shape=[
            jax.ShapeDtypeStruct((rows, d), F32),
            jax.ShapeDtypeStruct((rows, d), BF),
            jax.ShapeDtypeStruct((rows, d), BF),
            jax.ShapeDtypeStruct((8, d), F32),
        ],
        compiler_params=params(),
        cost_estimate=cost(2 * rows * d * d, 14 * rows * d),
        name="middle",
    )(o, x, g, w_out, vec)


def gelu_parts(u):
    near = jnp.abs(u)
    t = 1.0 / (1.0 + (0.3275911 * 0.7071067811865476) * near)
    bell = jnp.exp2((-0.5 * LOG2E) * (u * u))
    poly = t * (
        0.5 * 0.254829592
        + t * (0.5 * -0.284496736 + t * (0.5 * 1.421413741 + t * (0.5 * -1.453152027 + t * (0.5 * 1.061405429))))
    )
    tail = poly * bell
    phi = jnp.where(u < 0, tail, 1.0 - tail)
    return u * phi, phi + u * bell * 0.3989422804014327


def feed_kernel(chunk, a2_ref, gm_ref, up_ref, ub_ref, down_ref, bm_ref, ga_ref, dup_ref, ddown_ref, dub_ref, gl_ref, gu_ref):
    first = pl.program_id(0) == 0

    @pl.when(first)
    def _():
        bm_ref[...] = jnp.zeros_like(bm_ref)
        ga_ref[...] = jnp.zeros_like(ga_ref)

    total = jnp.zeros((8, ub_ref.shape[-1]), F32)
    for start, size in chunks(a2_ref.shape[0], chunk):
        rows = pl.ds(start, size)
        u = dot(a2_ref[rows, :], up_ref[...], 1, 0) + ub_ref[...]
        back = dot(gm_ref[rows, :], down_ref[...], 1, 1)
        active, slope = gelu_parts(u)
        low = active.astype(BF)
        gl_ref[rows, :] = low
        gu = (slope * back).astype(BF)
        gu_ref[rows, :] = gu
        total += jnp.sum(gu.astype(F32).reshape(-1, 8, gu.shape[-1]), axis=0)
        bm_ref[rows, :] += dot(low, down_ref[...], 1, 0)
        ga_ref[rows, :] += dot(gu, up_ref[...], 1, 1)
    dub_ref[...] = total
    ddown_ref[...] = dot(gl_ref[...], gm_ref[...], 0, 0).astype(ddown_ref.dtype)
    dup_ref[...] = dot(a2_ref[...], gu_ref[...], 0, 0).astype(dup_ref.dtype)


def feed(a2, gm, w_up, b_up, w_down, block=512, chunk=704, kind=BF):
    rows, d = a2.shape
    ff = w_up.shape[1]
    return pl.pallas_call(
        functools.partial(feed_kernel, chunk),
        grid=(ff // block,),
        in_specs=[
            whole((rows, d)),
            whole((rows, d)),
            pl.BlockSpec((d, block), lambda f: (0, f)),
            pl.BlockSpec((1, block), lambda f: (0, f)),
            pl.BlockSpec((block, d), lambda f: (f, 0)),
        ],
        out_specs=[
            whole((rows, d)),
            whole((rows, d)),
            pl.BlockSpec((d, block), lambda f: (0, f)),
            pl.BlockSpec((block, d), lambda f: (f, 0)),
            pl.BlockSpec((8, block), lambda f: (0, f)),
        ],
        out_shape=[
            jax.ShapeDtypeStruct((rows, d), F32),
            jax.ShapeDtypeStruct((rows, d), F32),
            jax.ShapeDtypeStruct((d, ff), kind),
            jax.ShapeDtypeStruct((ff, d), kind),
            jax.ShapeDtypeStruct((8, ff), F32),
        ],
        scratch_shapes=[pltpu.VMEM((rows, block), BF), pltpu.VMEM((rows, block), BF)],
        compiler_params=params(),
        cost_estimate=cost(12 * rows * d * ff, 4 * 4 * d * ff),
        name="feed",
    )(a2, gm, w_up, b_up, w_down)


def join_kernel(size, m1_ref, bm_ref, ga_ref, x_ref, g_ref, o_ref, w_ref, vec_ref, out_ref, gm1_ref, go_ref, dout_ref, sums_ref, gb_ref):
    bias2, scale1, gain2, scale2 = (vec_ref[i : i + 1, :] for i in range(4))
    step = pl.program_id(0)

    @pl.when(step == 0)
    def _():
        sums_ref[...] = jnp.zeros_like(sums_ref)

    base = step * m1_ref.shape[0]

    def body(rows):
        m1 = m1_ref[rows, :]
        bm = bm_ref[rows, :] + bias2
        g = g_ref[rows, :].astype(F32)
        out_ref[rows, :] = (m1 + scale2 * bm).astype(BF)
        unit, inverse = normalised(m1)
        ga = ga_ref[rows, :]
        gm1 = g + norm_back(unit, inverse, ga * gain2)
        gm1_ref[rows, :] = gm1
        gb = (scale1 * gm1).astype(BF)
        gb_ref[pl.ds(pl.multiple_of(base + rows.start, size), size), :] = gb
        for index, value in enumerate(
            (g * bm, ga * unit, ga, gm1 * (m1 - x_ref[rows, :].astype(F32)), gb.astype(F32))
        ):
            sums_ref[index] += jnp.sum(value.reshape(-1, 8, value.shape[-1]), axis=0)

    row_loop(m1_ref.shape[0], size, body)

    @pl.when(step == pl.num_programs(0) - 1)
    def _():
        go_ref[...] = dot(w_ref[...], gb_ref[...], 1, 1).astype(BF)
        dout_ref[...] = dot(o_ref[...], gb_ref[...], 1, 0).astype(dout_ref.dtype)


def join(m1, bm, ga, x, g, o, w_out, vec, tile=128, kind=BF):
    rows, d = x.shape
    by_rows = pl.BlockSpec((tile, d), lambda i: (i, 0))
    return pl.pallas_call(
        functools.partial(join_kernel, 32),
        grid=(rows // tile,),
        in_specs=[by_rows] * 5 + [whole((d, rows)), whole((d, d)), whole((8, d))],
        out_specs=[by_rows, by_rows, whole((d, rows)), whole((d, d)), whole((5, 8, d))],
        out_shape=[
            jax.ShapeDtypeStruct((rows, d), BF),
            jax.ShapeDtypeStruct((rows, d), F32),
            jax.ShapeDtypeStruct((d, rows), BF),
            jax.ShapeDtypeStruct((d, d), kind),
            jax.ShapeDtypeStruct((5, 8, d), F32),
        ],
        scratch_shapes=[pltpu.VMEM((rows, d), BF)],
        compiler_params=params(),
        cost_estimate=cost(4 * rows * d * d, 26 * rows * d),
        name="join",
    )(m1, bm, ga, x, g, o, w_out, vec)


def attend_back_kernel(chunk, q_ref, k_ref, v_ref, go_ref, o_ref, e_ref, inv_ref, out_ref, kt_ref, gq_ref, gs_ref, gp_ref):
    rows = q_ref.shape[0]
    factor = HD ** (-0.5)
    kt_ref[...] = k_ref[...].astype(F32).T.astype(BF)
    low = lax.broadcasted_iota(jnp.int32, (1, 128), 1) < HD
    below = lax.broadcasted_iota(jnp.int32, (128, 1), 0) < HD
    gp_ref[...] = jnp.zeros_like(gp_ref)
    for start, size in chunks(rows, chunk):
        span = pl.ds(start, size)
        for half in range(2):
            head = pl.ds(half * HD, HD)
            incoming = go_ref[head, span].astype(F32) * inv_ref[0, half : half + 1, span]
            centre = jnp.sum(incoming * o_ref[head, span].astype(F32), axis=0, keepdims=True)
            gp_ref[half, head, span] = incoming.astype(BF)
            gp = dot(v_ref[...], gp_ref[half, :, span], 1, 0)
            gs = (e_ref[half, :, span].astype(F32) * (gp - centre)).astype(BF)
            gs_ref[half, :, span] = gs
            gq_ref[head, span] = dot(kt_ref[head, :], gs, 1, 0) * factor
    out_ref[0] = gq_ref[...].T.astype(BF)
    gk = [dot(gs_ref[half], q_ref[...], 1, 0) for half in range(2)]
    out_ref[1] = (jnp.where(low, gk[0], gk[1]) * factor).astype(BF)
    out_ref[2] = (dot(e_ref[0], gp_ref[0], 1, 1) + dot(e_ref[1], gp_ref[1], 1, 1)).astype(BF)


def attend_back(qkv, go, o, e, inv, chunk=256):
    rows, width = qkv.shape
    pairs = width // 384
    return pl.pallas_call(
        functools.partial(attend_back_kernel, chunk),
        grid=(pairs,),
        in_specs=[
            pl.BlockSpec((rows, 128), lambda p: (0, p)),
            pl.BlockSpec((rows, 128), lambda p: (0, pairs + p)),
            pl.BlockSpec((rows, 128), lambda p: (0, 2 * pairs + p)),
            pl.BlockSpec((128, rows), lambda p: (p, 0)),
            pl.BlockSpec((128, rows), lambda p: (p, 0)),
            pl.BlockSpec((2, rows, rows), lambda p: (p, 0, 0)),
            pl.BlockSpec((1, 2, rows), lambda p: (p, 0, 0)),
        ],
        out_specs=pl.BlockSpec((3, rows, 128), lambda p: (0, 0, p)),
        out_shape=jax.ShapeDtypeStruct((3, rows, pairs * 128), BF),
        scratch_shapes=[
            pltpu.VMEM((128, rows), BF),
            pltpu.VMEM((128, rows), F32),
            pltpu.VMEM((2, rows, rows), BF),
            pltpu.VMEM((2, 128, rows), BF),
        ],
        compiler_params=params(),
        cost_estimate=cost(2 * pairs * 8 * rows * rows * 256, 4 * pairs * rows * rows),
        name="attend_back",
    )(qkv, qkv, qkv, go, o, e, inv)


def finish_kernel(a1_ref, gqkv_ref, w_ref, x_ref, gm1_ref, gain_ref, dw_ref, cols_ref, gx_ref, sums_ref, ga_ref):
    step = pl.program_id(0)
    grads = gqkv_ref[0]
    dw_ref[...] = dot(a1_ref[...], grads, 0, 0).astype(dw_ref.dtype)
    cols_ref[0] = jnp.sum(grads.astype(F32).reshape(-1, 8, grads.shape[-1]), axis=0)
    part = dot(grads, w_ref[...], 1, 1)

    @pl.when(step == 0)
    def _():
        ga_ref[...] = part

    @pl.when(step > 0)
    def _():
        ga_ref[...] += part

    @pl.when(step == pl.num_programs(0) - 1)
    def _():
        sums_ref[...] = jnp.zeros_like(sums_ref)

        def body(rows):
            unit, inverse = normalised(x_ref[rows, :].astype(F32))
            ga = ga_ref[rows, :]
            gx_ref[rows, :] = gm1_ref[rows, :] + norm_back(unit, inverse, ga * gain_ref[...])
            for index, value in enumerate((ga * unit, ga)):
                sums_ref[index] += jnp.sum(value.reshape(-1, 8, value.shape[-1]), axis=0)

        row_loop(x_ref.shape[0], 32, body)


def finish(a1, gqkv, w_in, x, gm1, gain, kind=BF):
    rows, d = x.shape
    return pl.pallas_call(
        finish_kernel,
        grid=(3,),
        in_specs=[
            whole((rows, d)),
            pl.BlockSpec((1, rows, d), lambda t: (t, 0, 0)),
            pl.BlockSpec((d, d), lambda t: (0, t)),
            whole((rows, d)),
            whole((rows, d)),
            whole((1, d)),
        ],
        out_specs=[
            pl.BlockSpec((d, d), lambda t: (0, t)),
            pl.BlockSpec((1, 8, d), lambda t: (t, 0, 0)),
            whole((rows, d)),
            whole((2, 8, d)),
        ],
        out_shape=[
            jax.ShapeDtypeStruct((d, 3 * d), kind),
            jax.ShapeDtypeStruct((3, 8, d), F32),
            jax.ShapeDtypeStruct((rows, d), F32),
            jax.ShapeDtypeStruct((2, 8, d), F32),
        ],
        scratch_shapes=[pltpu.VMEM((rows, d), F32)],
        compiler_params=params(),
        cost_estimate=cost(12 * rows * d * d, 20 * rows * d),
        name="finish",
    )(a1, gqkv, w_in, x, gm1, gain)


def layer(gather, scatter, scatter_small, inputs, segment_ids, cotangent, in_weight, out_weight, up_weight, down_weight, vectors):
    rows, d = inputs.shape
    w_in, w_out, w_up, w_down, vecs = gather(in_weight, out_weight, up_weight, down_weight, vectors)
    in_bias, out_bias, gain1, shift1, scale1, up_bias, down_bias, gain2, shift2, scale2 = vecs
    lane = lax.broadcasted_iota(jnp.int32, (1, 128), 1) % HD
    same = segment_ids[:, None] == lane
    mark = same.astype(BF)
    far = jnp.where(same | (lane > PADDING), 0.0, FAR).astype(BF)
    g = jnp.where((segment_ids < PADDING)[:, None], cotangent, jnp.zeros_like(cotangent))
    offset = jnp.concatenate([in_bias[:, :d], jnp.zeros((1, d), F32), in_bias[:, d:]], axis=1)
    a1, qkv = project(inputs, w_in, gain1, shift1, offset)
    o, e, inv = attend(qkv, mark, far)
    blank = jnp.zeros((1, d), F32)
    m1, a2, gm, gm_sum = middle(
        o, inputs, g, w_out, jnp.concatenate([out_bias, scale1, gain2, shift2, scale2, blank, blank, blank])
    )
    bm, ga2, d_up, d_down, ub_sum = feed(a2, gm, w_up, up_bias, w_down)
    outputs, gm1, go, d_out, join_sums = join(
        m1, bm, ga2, inputs, g, o, w_out, jnp.concatenate([down_bias, scale1, gain2, scale2, blank, blank, blank, blank])
    )
    gqkv = attend_back(qkv, go, o, e, inv)
    d_in, col_sums, gx, last_sums = finish(a1, gqkv, w_in, inputs, gm1, gain1)
    s = jnp.sum
    j = s(join_sums, axis=1)
    c = s(col_sums, axis=1)
    t = s(last_sums, axis=1)
    small = scatter_small(
        [
            jnp.concatenate([c[0], c[2]]),
            j[4],
            t[0],
            t[1],
            j[3] / scale1[0],
            s(ub_sum, axis=0),
            s(gm_sum, axis=0),
            j[1],
            j[2],
            j[0],
        ]
    )
    d_in, d_out, d_up, d_down = scatter(d_in, d_out, d_up, d_down)
    return (
        outputs, gx, d_in, small[0], d_out, small[1], small[2], small[3], small[4],
        d_up, small[5], d_down, small[6], small[7], small[8], small[9],
    )


def shards(
    inputs, segment_ids, cotangent, in_weight, in_bias, out_weight, out_bias, first_gain, first_shift, first_scale,
    up_weight, up_bias, down_weight, down_bias, second_gain, second_shift, second_scale,
):
    vectors = (
        in_bias, out_bias, first_gain, first_shift, first_scale,
        up_bias, down_bias, second_gain, second_shift, second_scale,
    )

    def gather(w_in, w_out, w_up, w_down, vectors):
        take = lambda a: lax.all_gather(a, AXES, axis=0, tiled=True)
        joined = jnp.concatenate(vectors)[None]
        vec = take(joined)
        vecs = []
        at = 0
        for v in vectors:
            vecs.append(vec[:, at : at + v.shape[0]].reshape(1, -1).astype(F32))
            at += v.shape[0]
        return take(w_in), take(w_out), take(w_up), take(w_down), vecs

    def scatter(*grads):
        return [lax.psum_scatter(g, AXES, scatter_dimension=0, tiled=True).astype(F32) for g in grads]

    def scatter_small(sums):
        n = lax.axis_size(AXES)
        joined = jnp.concatenate([v.reshape(n, -1) for v in sums], axis=1)
        mine = lax.psum_scatter(joined, AXES, scatter_dimension=0, tiled=True)[0]
        out = []
        at = 0
        for v in sums:
            size = v.shape[0] // n
            out.append(mine[at : at + size])
            at += size
        return out

    return layer(
        gather, scatter, scatter_small, inputs, segment_ids, cotangent, in_weight, out_weight, up_weight, down_weight, vectors
    )


def solution(mesh):
    wide, flat = P(AXES, None), P(AXES)
    return jax.shard_map(
        shards,
        mesh=mesh,
        in_specs=(wide, flat, wide, wide, flat, wide, flat, flat, flat, flat, wide, flat, wide, flat, flat, flat, flat),
        out_specs=(wide, wide, wide, flat, wide, flat, flat, flat, flat, wide, flat, wide, flat, flat, flat, flat),
        check_vma=False,
    )
```

time: 1160 us -> 783 us (0.68)
  matrix products: 446 us -> 0 us
  Pallas kernels: 0 us -> 286 us
  other arithmetic: 179 us -> 14.6 us
  local copies, waits for them, and re-layouts: 150 us -> 13.9 us
  waiting for transfers between devices: 273 us -> 366 us
    dot_general x54 -> x0, matrix products: 446 us -> none  [the longest x12 113 us: masked_scores(): jnp.einsum('qhd,khd->hqk', query_pair, key_pair, preferred_element_type=j...]
    pallas_call x0 -> x7, Pallas kernels: none -> 286 us  [the longest x1 70.9 us: attend(): pl.pallas_call(functools.partial(attend_kernel, chunk), grid=(pairs,), in...]
    convert_element_type x17 -> x9, other arithmetic: 93.2 us -> 9.82 us  [the longest x4 6.29 us: scatter(): lax.psum_scatter(g, AXES, scatter_dimension=0, tiled=True).astype(F32)]
    all_gather x4, waiting for transfers between devices: 0.02 us -> 82 us  [gather(): take = lambda a: lax.all_gather(a, AXES, axis=0, tiled=True)]
    reduce_sum x15 -> x5, other arithmetic: 65.1 us -> 0.14 us  [the longest x1 0.04 us: layer(): j = s(join_sums, axis=1)]
    unnamed x154 -> x12, local copies, waits for them, and re-layouts: 43.1 us -> 0.31 us
    dynamic_slice x36 -> x0, local copies, waits for them, and re-layouts: 37.6 us -> none  [shards(): lax.map(forward_pair, (stacked[0], stacked[1], stacked[2]))]
    while x24 -> x0, local copies, waits for them, and re-layouts: 19.2 us -> none
  transfers between devices with their start and end apart: 8 -> 8, of which waited for: 2 -> 6; matrix products, arithmetic and copies ran while one was open for 60% -> 3% of each run, Pallas kernels for 0% -> 26%
where the time goes in v1:
time: 783 us; the launch traced here: 778 us
  waiting for transfers between devices  366 us (47%)
  Pallas kernels  286 us (37%)
  blocking collectives  81.9 us (10%)
  between operations  14.7 us (2%)
  other arithmetic  14.6 us (2%)
  local copies, waits for them, and re-layouts  13.9 us (2%)
    reduce_scatter x4, waiting for transfers between devices, scatter(): lax.psum_scatter(g, AXES, scatter_dimension=0, tiled=True).astype(F32)  280 us
    all_gather x4, waiting for transfers between devices, gather(): take = lambda a: lax.all_gather(a, AXES, axis=0, tiled=True)  82 us
    unnamed x2, blocking collectives  81.9 us
    pallas_call x1, Pallas kernels, attend(): pl.pallas_call(functools.partial(attend_kernel, chunk), grid=(pairs,), in...  70.9 us
    pallas_call x1, Pallas kernels, attend_back(): pl.pallas_call(functools.partial(attend_back_kernel, chunk), grid=(pairs,...  66.6 us
    pallas_call x1, Pallas kernels, feed(): pl.pallas_call(functools.partial(feed_kernel, chunk), grid=(ff // block,)...  57.7 us
    pallas_call x1, Pallas kernels, finish(): pl.pallas_call(finish_kernel, grid=(3,), in_specs=[whole((rows, d)), pl.B...  31.7 us
    pallas_call x1, Pallas kernels, join(): pl.pallas_call(functools.partial(join_kernel, 32), grid=(rows // tile,),...  24 us
  transfers between devices with their start and end apart: 8, of which 6 were waited for; matrix products, arithmetic and copies ran while one was open for 3% of the time, Pallas kernels for 26%

profile of v1, /device:TPU:0, one launch (start us, length us, event | category | flops | bytes accessed | tf_op | source)
XLA Modules:
  0.0 777.9 jit_solution(10153748857835951586)
XLA Ops:
  7.2 0.7 all-gather.6.cloned.1.call-update
  8.0 0.7 all-gather.8.cloned.1.call-update
  8.7 0.7 all-gather.10.cloned.1.call-update
  10.0 6.8 concatenate.29
  17.1 42.4 %all-reduce = bf16[10752]{0:T(1024)(128)(2,1)S(1)} all-reduce(bf16[10752]{0:T(1024)(128)(2,1)S(1)} %dynamic-update-slice), channel_id=2, replica_groups=mesh['dp'=4,'fsdp'=8] {'dp','fsdp'}, use_global_device_ids=true, to_apply=%add | all-reduce | flops 10752 | bytes 43008
  59.7 0.7 reshape.236.ub_ref
  60.9 0.7 reshape.228.gain_ref
  61.7 0.7 reshape.229.shift_ref
  63.1 0.6 concatenate.32.vec_ref
  63.7 0.7 broadcast_compare_fusion
  65.0 1.7 compare_convert_fusion.mark_ref
  66.7 1.7 select_convert_fusion.far_ref
  68.4 3.3 broadcast_select_fusion.g_ref
  71.7 2.1 all-gather.6.cloned.1.call-done.w_ref
  73.8 17.5 %project.1 = (bf16[1408,768]{1,0:T(8,128)(2,1)}, bf16[1408,2304]{1,0:T(8,128)(2,1)}) custom-call(bf16[1408,768]{1,0:T(8,128)(2,1)} %x_ref.7, bf16[768,2304]{1,0:T(8,128)(2,1)} %all-gather.6.cloned.1.call-done.w_ref, f32[1,768]{1,0:T(1,128)} %reshape.228.gain_ref, f32[1,768]{1,0:T(1,128)} %reshape.229.shift_ref, f32[1,2304]{1,0:T(1,128)} %fusion.offset_ref), custom_call_target="tpu_custom_call" | custom-call | flops 4982833152 | bytes 14352384 | tf_op jit(solution)/shard_map/project/pallas_call | solution.py:74
  91.3 70.9 %attend.1 = (bf16[768,1408]{1,0:T(8,128)(2,1)}, bf16[12,1408,1408]{2,1,0:T(8,128)(2,1)}, f32[6,2,1408]{2,1,0:T(2,128)}) custom-call(bf16[1408,2304]{1,0:T(8,128)(2,1)} %get-tuple-element.39.q_ref.k_ref.v_ref, bf16[1408,2304]{1,0:T(8,128)(2,1)} %get-tuple-element.39.q_ref.k_ref.v_ref, bf16[1408,2304]{1,0:T(8,128)(2,1)} %get-tuple-element.39.q_ref.k_ref.v_ref, ...), custom_call_target="tpu_custom_call" | custom-call | flops 24360517632 | bytes 47579136 | tf_op jit(solution)/shard_map/attend/pallas_call | solution.py:126
  162.2 17.9 %middle.1 = (f32[1408,768]{1,0:T(8,128)}, bf16[1408,768]{1,0:T(8,128)(2,1)}, bf16[1408,768]{1,0:T(8,128)(2,1)}, f32[8,768]{1,0:T(8,128)}) custom-call(bf16[768,1408]{1,0:T(8,128)(2,1)} %get-tuple-element.40.o_ref, bf16[1408,768]{1,0:T(8,128)(2,1)} %x_ref.7, bf16[1408,768]{1,0:T(8,128)(2,1)} %broadcast_select_fusion.g_ref, ...), custom_call_target="tpu_custom_call" | custom-call | flops 1660944384 | bytes 15138816 | tf_op jit(solution)/shard_map/middle/pallas_call | solution.py:172
  180.1 15.2 %all-gather.10.cloned.1.call-done.up_ref = bf16[768,3072]{1,0:T(8,128)(2,1)} async-done(((bf16[24,3072]{1,0:T(8,128)(2,1)}), bf16[768,3072]{1,0:T(8,128)(2,1)}) %all-gather.10.cloned.1.call-update) | async-done | bytes 4718608 | tf_op jit(solution)/shard_map/all_gather | solution.py:486
  195.4 64.6 %all-gather.12.cloned.1.call-done.down_ref = bf16[3072,768]{1,0:T(8,128)(2,1)} async-done(((bf16[96,768]{1,0:T(8,128)(2,1)}), bf16[3072,768]{1,0:T(8,128)(2,1)}) %all-gather.12.cloned.1.call-update) | async-done | bytes 4718608 | tf_op jit(solution)/shard_map/all_gather | solution.py:486
  260.0 57.7 %feed.1 = (f32[1408,768]{1,0:T(8,128)}, f32[1408,768]{1,0:T(8,128)}, bf16[768,3072]{1,0:T(8,128)(2,1)}, bf16[3072,768]{1,0:T(8,128)(2,1)}, f32[8,3072]{1,0:T(8,128)}) custom-call(bf16[1408,768]{1,0:T(8,128)(2,1)} %get-tuple-element.42.a2_ref, bf16[1408,768]{1,0:T(8,128)(2,1)} %get-tuple-element.43.gm_ref, ...), custom_call_target="tpu_custom_call" | custom-call | flops 39862665216 | bytes 37748736 | tf_op jit(solution)/shard_map/feed/pallas_call | solution.py:228
  317.6 24.0 %join.1 = (bf16[1408,768]{1,0:T(8,128)(2,1)}, f32[1408,768]{1,0:T(8,128)}, bf16[768,1408]{1,0:T(8,128)(2,1)}, bf16[768,768]{1,0:T(8,128)(2,1)}, f32[5,8,768]{2,1,0:T(8,128)}) custom-call(f32[1408,768]{1,0:T(8,128)} %get-tuple-element.41.m1_ref, f32[1408,768]{1,0:T(8,128)} %get-tuple-element.44.bm_ref, f32[1408,768]{1,0:T(8,128)} %get-tuple-element.45.ga_ref, ...), custom_call_target="tpu_custom_call" | custom-call | flops 3321888768 | bytes 28114944 | tf_op jit(solution)/shard_map/join/pallas_call | solution.py:296
  341.8 66.6 %attend_back.1.gqkv_ref = bf16[3,1408,768]{2,1,0:T(8,128)(2,1)} custom-call(bf16[1408,2304]{1,0:T(8,128)(2,1)} %get-tuple-element.39.q_ref.k_ref.v_ref, bf16[1408,2304]{1,0:T(8,128)(2,1)} %get-tuple-element.39.q_ref.k_ref.v_ref, bf16[1408,2304]{1,0:T(8,128)(2,1)} %get-tuple-element.39.q_ref.k_ref.v_ref, bf16[768,1408]{1,0:T(8,128)(2,1)} %get-tuple-element.48.go_ref, ...), custom_call_target="tpu_custom_call" | custom-call | flops 48721035264 | bytes 47579136 | tf_op jit(solution)/shard_map/attend_back/pallas_call | solution.py:342
  408.4 31.7 %finish.1 = (bf16[768,2304]{1,0:T(8,128)(2,1)}, f32[3,8,768]{2,1,0:T(8,128)}, f32[1408,768]{1,0:T(8,128)}, f32[2,8,768]{2,1,0:T(8,128)}) custom-call(bf16[1408,768]{1,0:T(8,128)(2,1)} %get-tuple-element.47.a1_ref, bf16[3,1408,768]{2,1,0:T(8,128)(2,1)} %attend_back.1.gqkv_ref, bf16[768,2304]{1,0:T(8,128)(2,1)} %all-gather.6.cloned.1.call-done.w_ref, ...), custom_call_target="tpu_custom_call" | custom-call | flops 9965666304 | bytes 21626880 | tf_op jit(solution)/shard_map/finish/pallas_call | solution.py:399
  440.1 0.7 reduce-scatter.11.cloned.1.call-update
  443.0 39.5 %all-reduce.1 = f32[32,336]{1,0:T(8,128)S(1)} all-reduce(f32[32,336]{1,0:T(8,128)S(1)} %concatenate.38), channel_id=4, replica_groups=mesh['dp'=4,'fsdp'=8] {'dp','fsdp'}, use_global_device_ids=true, to_apply=%region_6.7.clone | all-reduce | flops 10752 | bytes 86016
  484.2 1.4 convert_element_type.159
  485.6 59.5 %reduce-scatter.5.cloned.1.call-done = bf16[24,2304]{1,0:T(8,128)(2,1)} async-done(((bf16[768,2304]{1,0:T(8,128)(2,1)}), bf16[24,2304]{1,0:T(8,128)(2,1)}) %reduce-scatter.5.cloned.1.call-update) | async-done | bytes 110608 | tf_op jit(solution)/shard_map/reduce_scatter | solution.py:497
  545.2 1.6 convert_element_type.157
  546.8 110.4 %reduce-scatter.11.cloned.1.call-done = bf16[96,768]{1,0:T(8,128)(2,1)} async-done(((bf16[3072,768]{1,0:T(8,128)(2,1)}), bf16[96,768]{1,0:T(8,128)(2,1)}) %reduce-scatter.11.cloned.1.call-update) | async-done | bytes 147472 | tf_op jit(solution)/shard_map/reduce_scatter | solution.py:497
  657.1 1.6 convert_element_type.161
  658.8 110.3 %reduce-scatter.9.cloned.1.call-done = bf16[24,3072]{1,0:T(8,128)(2,1)} async-done(((bf16[768,3072]{1,0:T(8,128)(2,1)}), bf16[24,3072]{1,0:T(8,128)(2,1)}) %reduce-scatter.9.cloned.1.call-update) | async-done | bytes 147472 | tf_op jit(solution)/shard_map/reduce_scatter | solution.py:497
  769.1 1.6 convert_element_type.160
  (71 shorter events, 7.0 us)
Async XLA Ops:
  7.2 66.6 %all-gather.6.cloned.1.call-start = ((), (), s32[]{:S(2)}) async-start(), calls=%async_computation.4 | async-start | bytes 3649536 | tf_op jit(solution)/shard_map/all_gather | solution.py:486
  7.9 154.3 %all-gather.8.cloned.1.call-start = ((), (), s32[]{:S(2)}) async-start(), calls=%async_computation.5 | async-start | bytes 1216512 | tf_op jit(solution)/shard_map/all_gather | solution.py:486
  8.7 186.7 %all-gather.10.cloned.1.call-start = ((), (), s32[]{:S(2)}) async-start(), calls=%async_computation.6 | async-start | bytes 4866048 | tf_op jit(solution)/shard_map/all_gather | solution.py:486
  9.4 250.6 %all-gather.12.cloned.1.call-start = ((), (), s32[]{:S(2)}) async-start(), calls=%async_computation.7 | async-start | bytes 4866048 | tf_op jit(solution)/shard_map/all_gather | solution.py:486
  10.0 474.3 %reduce-scatter.7.cloned.1.call-start = ((), (), s32[]{:S(2)}) async-start(), calls=%async_computation.9 | async-start | bytes 1216512 | tf_op jit(solution)/shard_map/reduce_scatter | solution.py:497
  341.7 203.5 %reduce-scatter.5.cloned.1.call-start = ((), (), s32[]{:S(2)}) async-start(), calls=%async_computation.8 | async-start | bytes 3649536 | tf_op jit(solution)/shard_map/reduce_scatter | solution.py:497
  440.1 217.1 %reduce-scatter.11.cloned.1.call-start = ((), (), s32[]{:S(2)}) async-start(), calls=%async_computation.11 | async-start | bytes 4866048 | tf_op jit(solution)/shard_map/reduce_scatter | solution.py:497
  440.8 328.3 %reduce-scatter.9.cloned.1.call-start = ((), (), s32[]{:S(2)}) async-start(), calls=%async_computation.10 | async-start | bytes 4866048 | tf_op jit(solution)/shard_map/reduce_scatter | solution.py:497
  440.9 0.7 copy-start.4
  440.9 0.8 copy-start.3
  440.9 1.0 copy-start.2
  440.9 1.2 copy-start.1
  440.9 1.2 copy-start
Sparse Core Ops, SparseCore 0:
  10.9 62.8 all-gather.5
  76.7 53.0 all-gather.7
  132.7 62.5 all-gather.9
  198.1 61.8 all-gather.11
  341.8 95.4 reduce-scatter.6
  442.6 102.4 reduce-scatter.4
  550.7 106.4 reduce-scatter.10
  662.6 106.4 reduce-scatter.8

commit v2 on v1

--- a/solution.py
+++ b/solution.py
@@ -55,6 +55,338 @@
         - jnp.mean(scaled, axis=-1, keepdims=True)
         - unit * jnp.mean(scaled * unit, axis=-1, keepdims=True)
     )
+
+
+MESH = pl.DeviceIdType.MESH
+ALL = slice(None)
+
+
+class Near:
+    def __init__(self, sizes):
+        self.sizes = sizes
+        dp, fsdp = lax.axis_index("dp"), lax.axis_index("fsdp")
+        ny = sizes["y"]
+        self.at = {"x": lax.div(dp, 2), "c": lax.rem(dp, 2), "z": lax.div(fsdp, ny), "y": lax.rem(fsdp, ny)}
+
+    def along(self, axis, shift):
+        return lax.rem(self.at[axis] + shift, self.sizes[axis])
+
+    def device(self, axis, shift):
+        at = {**self.at, axis: self.along(axis, shift)}
+        return (at["x"] * 2 + at["c"], at["z"] * self.sizes["y"] + at["y"])
+
+    def shifts(self, axis):
+        return range(1, self.sizes[axis])
+
+    def greet(self):
+        barrier = pltpu.get_barrier_semaphore()
+        count = 0
+        for axis in "cxyz":
+            for shift in self.shifts(axis):
+                pl.semaphore_signal(barrier, inc=1, device_id=self.device(axis, shift), device_id_type=MESH)
+                count += 1
+        pl.semaphore_wait(barrier, count)
+
+
+class Wires:
+    def __init__(self, near, send, recv):
+        self.near, self.send, self.recv, self.used = near, send, recv, 0
+
+    def wire(self, src, dst, axis, shift):
+        n = self.used
+        self.used += 1
+        return lambda: pltpu.make_async_remote_copy(
+            src_ref=src, dst_ref=dst, send_sem=self.send.at[n], recv_sem=self.recv.at[n],
+            device_id=self.near.device(axis, shift), device_id_type=MESH,
+        )
+
+
+def start(*groups):
+    for group in groups:
+        for wire in group:
+            wire().start()
+
+
+def landed(*groups):
+    for group in groups:
+        for wire in group:
+            wire().wait_recv()
+
+
+def left(*groups):
+    for group in groups:
+        for wire in group:
+            wire().wait_send()
+
+
+def halves(width):
+    cut = (width // 256) * 128
+    return (pl.ds(0, cut), pl.ds(cut, width - cut)) if width > 512 else (pl.ds(0, width), None)
+
+
+def gather_wires(sizes):
+    return sizes["z"] + 4 * (sizes["x"] + sizes["y"] - 2)
+
+
+def gather_stages(near, mine, full, send, recv, own):
+    wires = Wires(near, send, recv)
+    at = near.at
+
+    def piece(cols, **fixed):
+        return full.at[tuple(fixed.get(a, at[a]) for a in "xczy") + (ALL, cols)]
+
+    def spread(axis, done, cols, src=None):
+        here = piece(cols, **{a: ALL for a in done})
+        return [wires.wire(here if src is None else src, here, axis, k) for k in near.shifts(axis)]
+
+    def forward(axis, done, cols):
+        size = near.sizes[axis]
+        parts = [piece(cols, **{a: ALL for a in done}, **{axis: near.along(axis, size - k)}) for k in near.shifts(axis)]
+        return [wires.wire(p, p, "c", 1) for p in parts]
+
+    first, second = halves(mine.shape[-1])
+    whole_z = spread("z", "", ALL, mine)
+    column = piece(ALL, z=ALL)
+    pair = [wires.wire(column, column, "c", 1)]
+    one, two, one_on, two_on = [], [], [], []
+    for cols, (a, b) in ((first, "yx"), (second, "xy")):
+        if cols is not None:
+            one += spread(a, "z", cols)
+            one_on += forward(a, "z", cols)
+            two += spread(b, "z" + a, cols)
+            two_on += forward(b, "z" + a, cols)
+    keep = lambda: pltpu.make_async_copy(mine, piece(ALL), own)
+
+    def stage0():
+        keep().start()
+        start(whole_z)
+
+    def stage1():
+        keep().wait()
+        landed(whole_z)
+        start(one, pair)
+
+    def stage2():
+        landed(one)
+        start(two, one_on)
+
+    def stage3():
+        landed(two)
+        start(two_on)
+
+    def stage4():
+        left(whole_z, pair, one, two, one_on, two_on)
+        landed(pair, one_on, two_on)
+
+    return [stage0, stage1, stage2, stage3, stage4]
+
+
+def gather_scratch(sizes):
+    n = gather_wires(sizes)
+    return [pltpu.SemaphoreType.DMA((n,)), pltpu.SemaphoreType.DMA((n,)), pltpu.SemaphoreType.DMA(())]
+
+
+def lead(sizes):
+    return (sizes["x"], 2, sizes["z"], sizes["y"])
+
+
+def gathered(sizes, arrays):
+    return [jax.ShapeDtypeStruct(lead(sizes) + a.shape, a.dtype) for a in arrays]
+
+
+def run_all(plans, lag=0):
+    for t in range(5 + lag * (len(plans) - 1)):
+        for i, plan in enumerate(plans):
+            if 0 <= t - lag * i < 5:
+                plan[t - lag * i]()
+
+
+def gather_kernel(sizes, count, *refs):
+    near = Near(sizes)
+    near.greet()
+    sems = refs[2 * count :]
+    run_all([
+        gather_stages(near, refs[i], refs[count + i], *sems[3 * i : 3 * i + 3]) for i in range(count)
+    ])
+
+
+def gather_all(sizes, arrays, collective_id):
+    return pl.pallas_call(
+        functools.partial(gather_kernel, sizes, len(arrays)),
+        in_specs=[pl.BlockSpec(memory_space=pltpu.VMEM)] * len(arrays),
+        out_specs=[pl.BlockSpec(memory_space=pltpu.HBM)] * len(arrays),
+        out_shape=gathered(sizes, arrays),
+        scratch_shapes=gather_scratch(sizes) * len(arrays),
+        compiler_params=params(collective_id=collective_id, has_side_effects=True),
+        name="gather_all",
+    )(*arrays)
+
+
+def scatter_wires(sizes):
+    return 1 + 2 * (sizes["x"] + sizes["y"] - 2) + sizes["z"] - 1
+
+
+SCATTER_REFS = 10
+
+
+def scatter_scratch(sizes, block, width, kind):
+    nx, ny, nz = sizes["x"], sizes["y"], sizes["z"]
+    first, second = halves(width)
+    a, b = first.size, second.size
+    vmem = lambda *shape: pltpu.VMEM(shape, kind)
+    n = scatter_wires(sizes)
+    return [
+        vmem(nx, nz, ny, block, width), vmem(nx, nz, ny, block, width),
+        vmem(nx - 1, nz, ny, block, a), vmem(ny - 1, nx, nz, block, b),
+        vmem(ny - 1, nz, block, a), vmem(nx - 1, nz, block, b),
+        vmem(nz - 1, block, width),
+        pltpu.SemaphoreType.DMA((n,)), pltpu.SemaphoreType.DMA((n,)), pltpu.SemaphoreType.DMA(()),
+    ]
+
+
+def scatter_stages(near, grad, out, held, got, x_first, y_first, y_then, x_then, z_last, send, recv, own):
+    wires = Wires(near, send, recv)
+    at, sizes = near.at, near.sizes
+    nz, ny, nx = sizes["z"], sizes["y"], sizes["x"]
+    x, y, z = at["x"], at["y"], at["z"]
+    first, second = halves(held.shape[-1])
+    load = lambda: pltpu.make_async_copy(grad.at[:, at["c"]], held, own)
+    pair = [wires.wire(grad.at[:, 1 - at["c"]], got, "c", 1)]
+    one = [wires.wire(held.at[near.along("x", k), :, :, :, first], x_first.at[k - 1], "x", k) for k in near.shifts("x")]
+    one += [wires.wire(held.at[:, :, near.along("y", k), :, second], y_first.at[k - 1], "y", k) for k in near.shifts("y")]
+    two = [wires.wire(held.at[x, :, near.along("y", k), :, first], y_then.at[k - 1], "y", k) for k in near.shifts("y")]
+    two += [wires.wire(held.at[near.along("x", k), :, y, :, second], x_then.at[k - 1], "x", k) for k in near.shifts("x")]
+    last = [wires.wire(held.at[x, near.along("z", k), y], z_last.at[k - 1], "z", k) for k in near.shifts("z")]
+
+    def add(where, terms):
+        held[where] = sum([t.astype(F32) for t in terms], held[where].astype(F32)).astype(held.dtype)
+
+    def over_z(body):
+        lax.fori_loop(0, nz, lambda i, carry: (body(i), carry)[1], 0)
+
+    def stage0():
+        start(pair)
+        load().start()
+
+    def stage1():
+        load().wait()
+        landed(pair)
+
+        @over_z
+        def _(i):
+            for a in range(nx):
+                for b in range(ny):
+                    add((a, i, b), [got[a, i, b]])
+
+        start(one)
+
+    def stage2():
+        landed(one)
+
+        @over_z
+        def _(i):
+            for b in range(ny):
+                add((x, i, b, ALL, first), [x_first[k - 1, i, b] for k in near.shifts("x")])
+            for a in range(nx):
+                add((a, i, y, ALL, second), [y_first[k - 1, a, i] for k in near.shifts("y")])
+
+        start(two)
+
+    def stage3():
+        landed(two)
+
+        @over_z
+        def _(i):
+            add((x, i, y, ALL, first), [y_then[k - 1, i] for k in near.shifts("y")])
+            add((x, i, y, ALL, second), [x_then[k - 1, i] for k in near.shifts("x")])
+
+        start(last)
+
+    def stage4():
+        landed(last)
+        out[...] = sum([z_last[k - 1].astype(F32) for k in near.shifts("z")], held[x, z, y].astype(F32))
+        left(pair, one, two, last)
+
+    return [stage0, stage1, stage2, stage3, stage4]
+
+
+def total_scratch(sizes, shape):
+    n = sum(sizes[a] - 1 for a in "cxyz")
+    return [pltpu.VMEM((n,) + shape, F32), pltpu.VMEM((3,) + shape, F32), pltpu.SemaphoreType.DMA((n,)), pltpu.SemaphoreType.DMA((n,))]
+
+
+def total_stages(near, mine, out, got, held, send, recv):
+    wires = Wires(near, send, recv)
+    groups, slots = [], []
+    for step, axis in enumerate("cxyz"):
+        src = mine if step == 0 else held.at[step - 1]
+        slots.append([wires.used + k - 1 for k in near.shifts(axis)])
+        groups.append([wires.wire(src, got.at[wires.used], axis, k) for k in near.shifts(axis)])
+
+    def stage(step):
+        def run():
+            if step > 0:
+                landed(groups[step - 1])
+                total = mine[...] if step == 1 else held[step - 2]
+                for slot in slots[step - 1]:
+                    total = total + got[slot]
+                if step < 4:
+                    held[step - 1] = total
+                else:
+                    out[...] = total
+                    left(*groups)
+            if step < 4:
+                start(groups[step])
+
+        return run
+
+    return [stage(step) for step in range(5)]
+
+
+def scatter_kernel(sizes, count, lag, *refs):
+    near = Near(sizes)
+    near.greet()
+    ins, outs, rest = refs[: count + 1], refs[count + 1 : 2 * count + 2], refs[2 * count + 2 :]
+    plans = [
+        scatter_stages(near, ins[i], outs[i], *rest[SCATTER_REFS * i : SCATTER_REFS * (i + 1)]) for i in range(count)
+    ]
+    small = total_stages(near, ins[count], outs[count], *rest[SCATTER_REFS * count :])
+    run_all([*plans, small] if lag == 0 else plans, lag)
+    if lag:
+        run_all([small])
+
+
+def blocks_of(sizes, grads):
+    return [g.reshape(lead(sizes) + (-1, g.shape[1])) for g in grads]
+
+
+def scatter_all(sizes, grads, small, collective_id, lag=0):
+    blocks = blocks_of(sizes, grads)
+    vmem, hbm = pl.BlockSpec(memory_space=pltpu.VMEM), pl.BlockSpec(memory_space=pltpu.HBM)
+    return pl.pallas_call(
+        functools.partial(scatter_kernel, sizes, len(grads), lag),
+        in_specs=[hbm] * len(grads) + [vmem],
+        out_specs=[vmem] * (len(grads) + 1),
+        out_shape=[jax.ShapeDtypeStruct(b.shape[-2:], F32) for b in blocks] + [jax.ShapeDtypeStruct(small.shape, F32)],
+        scratch_shapes=[s for b in blocks for s in scatter_scratch(sizes, *b.shape[-2:], b.dtype)] + total_scratch(sizes, small.shape),
+        compiler_params=params(collective_id=collective_id, has_side_effects=True),
+        name="scatter_all",
+    )(*blocks, small)
+
+
+def pump(schedule, plans, chunk):
+    for step in sorted({at[0] for at in schedule if at[1] == chunk}):
+
+        @pl.when(pl.program_id(0) == step)
+        def _():
+            for plan, stage in schedule[step, chunk]:
+                plans[plan][stage]()
+
+
+def mesh_sizes(mesh):
+    fsdp = mesh.shape["fsdp"]
+    ny = 1 << ((fsdp.bit_length() - 1) // 2)
+    return {"x": mesh.shape["dp"] // 2, "c": 2, "z": fsdp // ny, "y": ny}
 
 
 def project_kernel(x_ref, w_ref, gain_ref, shift_ref, offset_ref, a1_ref, qkv_ref):
@@ -96,14 +428,36 @@
     return [(start, min(size, rows - start)) for start in range(0, rows, size)]
 
 
-def attend_kernel(chunk, q_ref, k_ref, v_ref, mark_ref, far_ref, o_ref, e_ref, inv_ref, vt_ref, k2_ref):
+GATHER_AT = {
+    (0, 0): [(0, 0), (1, 0)],
+    (0, 3): [(0, 1)],
+    (1, 0): [(2, 0), (0, 2)],
+    (1, 3): [(1, 1)],
+    (2, 0): [(0, 3)],
+    (2, 3): [(1, 2)],
+    (3, 0): [(2, 1)],
+    (4, 0): [(1, 3), (2, 2)],
+    (5, 3): [(2, 3)],
+    (5, 5): [(0, 4), (1, 4), (2, 4)],
+}
+
+
+def attend_kernel(chunk, sizes, count, q_ref, k_ref, v_ref, mark_ref, far_ref, *refs):
+    shards, (o_ref, e_ref, inv_ref) = refs[:count], refs[count : count + 3]
+    full, (vt_ref, k2_ref), sems = refs[count + 3 : 2 * count + 3], refs[2 * count + 3 : 2 * count + 5], refs[2 * count + 5 :]
     rows = q_ref.shape[0]
+    plans, schedule = [], {}
+    if count:
+        near, schedule = Near(sizes), GATHER_AT
+        pl.when(pl.program_id(0) == 0)(near.greet)
+        plans = [gather_stages(near, shards[i], full[i], *sems[3 * i : 3 * i + 3]) for i in range(count)]
     vt_ref[...] = v_ref[...].astype(F32).T.astype(BF)
     low = lax.broadcasted_iota(jnp.int32, (1, 128), 1) < HD
     for half in range(2):
         mine = low if half == 0 else jnp.logical_not(low)
         k2_ref[half] = jnp.where(mine, k_ref[...], far_ref[...])
-    for start, size in chunks(rows, chunk):
+    for turn, (start, size) in enumerate(chunks(rows, chunk)):
+        pump(schedule, plans, turn)
         for half in range(2):
             mine = low if half == 0 else jnp.logical_not(low)
             span = pl.ds(start, size)
@@ -120,11 +474,12 @@
             o_ref[head, span] = (dot(vt_ref[head, :], weights_low, 1, 0) * inverse).astype(BF)
 
 
-def attend(qkv, mark, far, chunk=256):
+def attend(qkv, mark, far, sizes, shards, chunk=256):
+    count = len(shards)
     rows, width = qkv.shape
     pairs = width // 384
     return pl.pallas_call(
-        functools.partial(attend_kernel, chunk),
+        functools.partial(attend_kernel, chunk, sizes, count),
         grid=(pairs,),
         in_specs=[
             pl.BlockSpec((rows, 128), lambda p: (0, p)),
@@ -132,22 +487,29 @@
             pl.BlockSpec((rows, 128), lambda p: (0, 2 * pairs + p)),
             whole((rows, 128)),
             whole((rows, 128)),
+            *[whole(a.shape) for a in shards],
         ],
         out_specs=[
             pl.BlockSpec((128, rows), lambda p: (p, 0)),
             pl.BlockSpec((2, rows, rows), lambda p: (p, 0, 0)),
             pl.BlockSpec((1, 2, rows), lambda p: (p, 0, 0)),
+            *[pl.BlockSpec(memory_space=pltpu.HBM)] * count,
         ],
         out_shape=[
             jax.ShapeDtypeStruct((pairs * 128, rows), BF),
             jax.ShapeDtypeStruct((2 * pairs, rows, rows), BF),
             jax.ShapeDtypeStruct((pairs, 2, rows), F32),
-        ],
-        scratch_shapes=[pltpu.VMEM((128, rows), BF), pltpu.VMEM((2, rows, 128), BF)],
-        compiler_params=params(),
+            *(gathered(sizes, shards) if count else []),
+        ],
+        scratch_shapes=[
+            pltpu.VMEM((128, rows), BF),
+            pltpu.VMEM((2, rows, 128), BF),
+            *(gather_scratch(sizes) * count if count else []),
+        ],
+        compiler_params=params(collective_id=1, has_side_effects=True) if count else params(),
         cost_estimate=cost(2 * pairs * 4 * rows * rows * 256, 4 * pairs * rows * rows, 2 * pairs * rows * rows),
         name="attend",
-    )(qkv, qkv, qkv, mark, far)
+    )(qkv, qkv, qkv, mark, far, *shards)
 
 
 def middle_kernel(o_ref, x_ref, g_ref, w_ref, vec_ref, m1_ref, a2_ref, gm_ref, gmsum_ref):
@@ -312,14 +674,38 @@
     )(m1, bm, ga, x, g, o, w_out, vec)
 
 
-def attend_back_kernel(chunk, q_ref, k_ref, v_ref, go_ref, o_ref, e_ref, inv_ref, out_ref, kt_ref, gq_ref, gs_ref, gp_ref):
+SCATTER_AT = {
+    (0, 0): [(0, 0)],
+    (0, 3): [(0, 1), (1, 0)],
+    (1, 3): [(2, 0)],
+    (2, 0): [(0, 2), (1, 1)],
+    (3, 0): [(0, 3)],
+    (4, 0): [(1, 2), (2, 1)],
+    (4, 3): [(0, 4)],
+    (5, 0): [(1, 3), (2, 2)],
+    (5, 3): [(2, 3)],
+    (5, 5): [(1, 4), (2, 4)],
+}
+
+
+def attend_back_kernel(chunk, sizes, count, q_ref, k_ref, v_ref, go_ref, o_ref, e_ref, inv_ref, *refs):
+    grads, out_ref, sums = refs[:count], refs[count], refs[count + 1 : 2 * count + 1]
+    (kt_ref, gq_ref, gs_ref, gp_ref), rest = refs[2 * count + 1 : 2 * count + 5], refs[2 * count + 5 :]
     rows = q_ref.shape[0]
+    plans, schedule = [], {}
+    if count:
+        near, schedule = Near(sizes), SCATTER_AT
+        pl.when(pl.program_id(0) == 0)(near.greet)
+        plans = [
+            scatter_stages(near, grads[i], sums[i], *rest[SCATTER_REFS * i : SCATTER_REFS * (i + 1)]) for i in range(count)
+        ]
     factor = HD ** (-0.5)
     kt_ref[...] = k_ref[...].astype(F32).T.astype(BF)
     low = lax.broadcasted_iota(jnp.int32, (1, 128), 1) < HD
     below = lax.broadcasted_iota(jnp.int32, (128, 1), 0) < HD
     gp_ref[...] = jnp.zeros_like(gp_ref)
-    for start, size in chunks(rows, chunk):
+    for turn, (start, size) in enumerate(chunks(rows, chunk)):
+        pump(schedule, plans, turn)
         span = pl.ds(start, size)
         for half in range(2):
             head = pl.ds(half * HD, HD)
@@ -336,11 +722,13 @@
     out_ref[2] = (dot(e_ref[0], gp_ref[0], 1, 1) + dot(e_ref[1], gp_ref[1], 1, 1)).astype(BF)
 
 
-def attend_back(qkv, go, o, e, inv, chunk=256):
+def attend_back(qkv, go, o, e, inv, sizes, grads, chunk=256):
+    blocks = blocks_of(sizes, grads) if grads else []
+    count = len(blocks)
     rows, width = qkv.shape
     pairs = width // 384
     return pl.pallas_call(
-        functools.partial(attend_back_kernel, chunk),
+        functools.partial(attend_back_kernel, chunk, sizes, count),
         grid=(pairs,),
         in_specs=[
             pl.BlockSpec((rows, 128), lambda p: (0, p)),
@@ -350,19 +738,24 @@
             pl.BlockSpec((128, rows), lambda p: (p, 0)),
             pl.BlockSpec((2, rows, rows), lambda p: (p, 0, 0)),
             pl.BlockSpec((1, 2, rows), lambda p: (p, 0, 0)),
-        ],
-        out_specs=pl.BlockSpec((3, rows, 128), lambda p: (0, 0, p)),
-        out_shape=jax.ShapeDtypeStruct((3, rows, pairs * 128), BF),
+            *[pl.BlockSpec(memory_space=pltpu.HBM)] * count,
+        ],
+        out_specs=[pl.BlockSpec((3, rows, 128), lambda p: (0, 0, p)), *[whole(b.shape[-2:]) for b in blocks]],
+        out_shape=[
+            jax.ShapeDtypeStruct((3, rows, pairs * 128), BF),
+            *[jax.ShapeDtypeStruct(b.shape[-2:], F32) for b in blocks],
+        ],
         scratch_shapes=[
             pltpu.VMEM((128, rows), BF),
             pltpu.VMEM((128, rows), F32),
             pltpu.VMEM((2, rows, rows), BF),
             pltpu.VMEM((2, 128, rows), BF),
-        ],
-        compiler_params=params(),
+            *[s for b in blocks for s in scatter_scratch(sizes, *b.shape[-2:], b.dtype)],
+        ],
+        compiler_params=params(collective_id=2, has_side_effects=True) if count else params(),
         cost_estimate=cost(2 * pairs * 8 * rows * rows * 256, 4 * pairs * rows * rows),
         name="attend_back",
-    )(qkv, qkv, qkv, go, o, e, inv)
+    )(qkv, qkv, qkv, go, o, e, inv, *blocks)
 
 
 def finish_kernel(a1_ref, gqkv_ref, w_ref, x_ref, gm1_ref, gain_ref, dw_ref, cols_ref, gx_ref, sums_ref, ga_ref):
@@ -426,9 +819,38 @@
     )(a1, gqkv, w_in, x, gm1, gain)
 
 
-def layer(gather, scatter, scatter_small, inputs, segment_ids, cotangent, in_weight, out_weight, up_weight, down_weight, vectors):
+def take(a):
+    return lax.all_gather(a, AXES, axis=0, tiled=True)
+
+
+def give(g):
+    return lax.psum_scatter(g, AXES, scatter_dimension=0, tiled=True).astype(F32)
+
+
+def layer(
+    sizes, inputs, segment_ids, cotangent, in_weight, in_bias, out_weight, out_bias, first_gain, first_shift, first_scale,
+    up_weight, up_bias, down_weight, down_bias, second_gain, second_shift, second_scale,
+):
     rows, d = inputs.shape
-    w_in, w_out, w_up, w_down, vecs = gather(in_weight, out_weight, up_weight, down_weight, vectors)
+    n = lax.axis_size(AXES)
+    vectors = (
+        in_bias, out_bias, first_gain, first_shift, first_scale,
+        up_bias, down_bias, second_gain, second_shift, second_scale,
+    )
+    own = all(w.shape[0] % 8 == 0 for w in (in_weight, out_weight, up_weight, down_weight))
+    joined = jnp.concatenate(vectors)[None]
+    used = joined.shape[1]
+    if own:
+        tile = jnp.pad(joined, ((0, 7), (0, -used % 128)))
+        w_in, vec = gather_all(sizes, [in_weight, tile], 0)
+        w_in, vec = w_in.reshape(-1, 3 * d), vec.reshape(n, 8, -1)[:, 0, :used]
+    else:
+        w_in, vec = take(in_weight), take(joined)
+    vecs = []
+    at = 0
+    for v in vectors:
+        vecs.append(vec[:, at : at + v.shape[0]].reshape(1, -1).astype(F32))
+        at += v.shape[0]
     in_bias, out_bias, gain1, shift1, scale1, up_bias, down_bias, gain2, shift2, scale2 = vecs
     lane = lax.broadcasted_iota(jnp.int32, (1, 128), 1) % HD
     same = segment_ids[:, None] == lane
@@ -437,7 +859,10 @@
     g = jnp.where((segment_ids < PADDING)[:, None], cotangent, jnp.zeros_like(cotangent))
     offset = jnp.concatenate([in_bias[:, :d], jnp.zeros((1, d), F32), in_bias[:, d:]], axis=1)
     a1, qkv = project(inputs, w_in, gain1, shift1, offset)
-    o, e, inv = attend(qkv, mark, far)
+    o, e, inv, *full = attend(qkv, mark, far, sizes, [out_weight, up_weight, down_weight] if own else [])
+    w_out, w_up, w_down = (
+        (f.reshape(-1, f.shape[-1]) for f in full) if own else (take(w) for w in (out_weight, up_weight, down_weight))
+    )
     blank = jnp.zeros((1, d), F32)
     m1, a2, gm, gm_sum = middle(
         o, inputs, g, w_out, jnp.concatenate([out_bias, scale1, gain2, shift2, scale2, blank, blank, blank])
@@ -446,77 +871,41 @@
     outputs, gm1, go, d_out, join_sums = join(
         m1, bm, ga2, inputs, g, o, w_out, jnp.concatenate([down_bias, scale1, gain2, scale2, blank, blank, blank, blank])
     )
-    gqkv = attend_back(qkv, go, o, e, inv)
+    gqkv, *done = attend_back(qkv, go, o, e, inv, sizes, [d_up, d_down, d_out] if own else [])
+    d_up, d_down, d_out = done if own else (give(v) for v in (d_up, d_down, d_out))
     d_in, col_sums, gx, last_sums = finish(a1, gqkv, w_in, inputs, gm1, gain1)
     s = jnp.sum
     j = s(join_sums, axis=1)
     c = s(col_sums, axis=1)
     t = s(last_sums, axis=1)
-    small = scatter_small(
-        [
-            jnp.concatenate([c[0], c[2]]),
-            j[4],
-            t[0],
-            t[1],
-            j[3] / scale1[0],
-            s(ub_sum, axis=0),
-            s(gm_sum, axis=0),
-            j[1],
-            j[2],
-            j[0],
-        ]
-    )
-    d_in, d_out, d_up, d_down = scatter(d_in, d_out, d_up, d_down)
+    sums = [
+        jnp.concatenate([c[0], c[2]]), j[4], t[0], t[1], j[3] / scale1[0],
+        s(ub_sum, axis=0), s(gm_sum, axis=0), j[1], j[2], j[0],
+    ]
+    small = jnp.concatenate(sums).reshape(-1, d)
+    small = jnp.pad(small, ((0, -small.shape[0] % 8), (0, 0)))
+    if own:
+        d_in, small = scatter_all(sizes, [d_in], small, 3)
+    else:
+        d_in, small = give(d_in), lax.psum(small, AXES)
+    small = small.reshape(-1)
+    here = lax.axis_index(AXES)
+    out = []
+    at = 0
+    for v in sums:
+        size = v.shape[0] // n
+        out.append(lax.dynamic_slice(small, (at + here * size,), (size,)))
+        at += v.shape[0]
     return (
-        outputs, gx, d_in, small[0], d_out, small[1], small[2], small[3], small[4],
-        d_up, small[5], d_down, small[6], small[7], small[8], small[9],
-    )
-
-
-def shards(
-    inputs, segment_ids, cotangent, in_weight, in_bias, out_weight, out_bias, first_gain, first_shift, first_scale,
-    up_weight, up_bias, down_weight, down_bias, second_gain, second_shift, second_scale,
-):
-    vectors = (
-        in_bias, out_bias, first_gain, first_shift, first_scale,
-        up_bias, down_bias, second_gain, second_shift, second_scale,
-    )
-
-    def gather(w_in, w_out, w_up, w_down, vectors):
-        take = lambda a: lax.all_gather(a, AXES, axis=0, tiled=True)
-        joined = jnp.concatenate(vectors)[None]
-        vec = take(joined)
-        vecs = []
-        at = 0
-        for v in vectors:
-            vecs.append(vec[:, at : at + v.shape[0]].reshape(1, -1).astype(F32))
-            at += v.shape[0]
-        return take(w_in), take(w_out), take(w_up), take(w_down), vecs
-
-    def scatter(*grads):
-        return [lax.psum_scatter(g, AXES, scatter_dimension=0, tiled=True).astype(F32) for g in grads]
-
-    def scatter_small(sums):
-        n = lax.axis_size(AXES)
-        joined = jnp.concatenate([v.reshape(n, -1) for v in sums], axis=1)
-        mine = lax.psum_scatter(joined, AXES, scatter_dimension=0, tiled=True)[0]
-        out = []
-        at = 0
-        for v in sums:
-            size = v.shape[0] // n
-            out.append(mine[at : at + size])
-            at += size
-        return out
-
-    return layer(
-        gather, scatter, scatter_small, inputs, segment_ids, cotangent, in_weight, out_weight, up_weight, down_weight, vectors
+        outputs, gx, d_in, out[0], d_out, out[1], out[2], out[3], out[4],
+        d_up, out[5], d_down, out[6], out[7], out[8], out[9],
     )
 
 
 def solution(mesh):
     wide, flat = P(AXES, None), P(AXES)
     return jax.shard_map(
-        shards,
+        functools.partial(layer, mesh_sizes(mesh)),
         mesh=mesh,
         in_specs=(wide, flat, wide, wide, flat, wide, flat, flat, flat, flat, wide, flat, wide, flat, flat, flat, flat),
         out_specs=(wide, wide, wide, flat, wide, flat, flat, flat, flat, wide, flat, wide, flat, flat, flat, flat),

time: 783 us -> 433 us (0.55)
  waiting for transfers between devices: 366 us -> 0 us
  Pallas kernels: 286 us -> 400 us
  blocking collectives: 81.9 us -> 0 us
  between operations: 14.7 us -> 1.19 us
    reduce_scatter x4 -> x0, waiting for transfers between devices: 280 us -> none  [scatter(): lax.psum_scatter(g, AXES, scatter_dimension=0, tiled=True).astype(F32)]
    pallas_call x2 -> x4, Pallas kernels: 138 us -> 251 us  [the longest x1 89.8 us: attend_back(): pl.pallas_call(functools.partial(attend_back_kernel, chunk, sizes, count)...]
    all_gather x4 -> x0, waiting for transfers between devices: 82 us -> none  [gather(): take = lambda a: lax.all_gather(a, AXES, axis=0, tiled=True)]
    unnamed x2 -> x0, blocking collectives: 81.9 us -> none
  transfers between devices with their start and end apart: 8 -> 0, of which waited for: 6 -> 0; matrix products, arithmetic and copies ran while one was open for 3% -> 0% of each run, Pallas kernels for 26% -> 0%
where the time goes in v2:
time: 433 us; the launch traced here: 429 us
  Pallas kernels  400 us (92%)
  local copies, waits for them, and re-layouts  19.4 us (4%)
  other arithmetic  7.8 us (2%)
    pallas_call x1, Pallas kernels, attend_back(): pl.pallas_call(functools.partial(attend_back_kernel, chunk, sizes, count)...  89.8 us
    pallas_call x1, Pallas kernels, attend(): pl.pallas_call(functools.partial(attend_kernel, chunk, sizes, count), gri...  85.2 us
    pallas_call x1, Pallas kernels, feed(): pl.pallas_call(functools.partial(feed_kernel, chunk), grid=(ff // block,)...  57.7 us
    pallas_call x1, Pallas kernels, scatter_all(): pl.pallas_call(functools.partial(scatter_kernel, sizes, len(grads), lag),...  41.2 us
    pallas_call x1, Pallas kernels, gather_all(): pl.pallas_call(functools.partial(gather_kernel, sizes, len(arrays)), in_s...  35.3 us
    pallas_call x1, Pallas kernels, finish(): pl.pallas_call(finish_kernel, grid=(3,), in_specs=[whole((rows, d)), pl.B...  31.6 us
    pallas_call x1, Pallas kernels, join(): pl.pallas_call(functools.partial(join_kernel, 32), grid=(rows // tile,),...  24 us
    pallas_call x1, Pallas kernels, middle(): pl.pallas_call(middle_kernel, out_shape=[jax.ShapeDtypeStruct((rows, d),...  18 us

profile of v2, /device:TPU:0, one launch (start us, length us, event | category | flops | bytes accessed | tf_op | source)
XLA Modules:
  0.0 428.6 jit_solution(7620317806908781909)
XLA Ops:
  0.7 6.8 %concatenate.21 = bf16[336]{0:T(512)(128)(2,1)S(1)} concatenate(bf16[48]{0:T(256)(128)(2,1)} %param.21, bf16[24]{0:T(256)(128)(2,1)} %param.23, bf16[24]{0:T(256)(128)(2,1)} %param.24, bf16[24]{0:T(256)(128)(2,1)} %param.25, bf16[24]{0:T(256)(128)(2,1)} %param.26, bf16[96]{0:T(256)(128)(2,1)} %param.28, bf16[24]{0:T(256)(128)(2,1)} %param.30, bf16[24]{0:T(256)(128)(2,1)} %param.31, ...), dimensions={0} | concatenate | bytes 1344 | tf_op jit(solution)/shard_map/concatenate | solution.py:841
  7.4 0.6 pad.8.refs_1_
  8.0 35.3 %gather_all.1 = (bf16[2,2,4,2,24,2304]{5,4,3,2,1,0:T(8,128)(2,1)}, bf16[2,2,4,2,8,384]{5,4,3,2,1,0:T(8,128)(2,1)}) custom-call(bf16[24,2304]{1,0:T(8,128)(2,1)} %refs_0_.2, bf16[8,384]{1,0:T(8,128)(2,1)} %pad.8.refs_1_), custom_call_target="tpu_custom_call" | custom-call | tf_op jit(solution)/shard_map/gather_all/pallas_call | solution.py:214
  43.3 1.0 slice.88
  44.8 0.6 concatenate.24.vec_ref
  45.5 0.7 reshape.249.gain_ref
  46.2 0.7 reshape.250.shift_ref
  46.9 0.6 fusion.offset_ref
  47.6 17.5 %project.1 = (bf16[1408,768]{1,0:T(8,128)(2,1)}, bf16[1408,2304]{1,0:T(8,128)(2,1)}) custom-call(bf16[1408,768]{1,0:T(8,128)(2,1)} %x_ref.7, bf16[768,2304]{1,0:T(8,128)(2,1)} %bitcast.19, f32[1,768]{1,0:T(1,128)} %reshape.249.gain_ref, f32[1,768]{1,0:T(1,128)} %reshape.250.shift_ref, f32[1,2304]{1,0:T(1,128)} %fusion.offset_ref), custom_call_target="tpu_custom_call" | custom-call | flops 4982833152 | bytes 14352384 | tf_op jit(solution)/shard_map/project/pallas_call | solution.py:406
  65.1 1.0 select_convert_fusion.far_ref
  66.1 1.0 compare_convert_fusion.mark_ref
  67.1 85.2 %attend.1 = (bf16[768,1408]{1,0:T(8,128)(2,1)}, bf16[12,1408,1408]{2,1,0:T(8,128)(2,1)}, f32[6,2,1408]{2,1,0:T(2,128)}, bf16[2,2,4,2,24,768]{5,4,3,2,1,0:T(8,128...) custom-call(bf16[1408,2304]{1,0:T(8,128)(2,1)} %get-tuple-element.52.q_ref.k_ref.v_ref, ...), custom_call_target="tpu_custom_call" | custom-call | flops 24360517632 | bytes 47579136 | tf_op jit(solution)/shard_map/attend/pallas_call | solution.py:481
  152.3 3.2 broadcast_select_fusion.g_ref
  155.4 18.0 %middle.1 = (f32[1408,768]{1,0:T(8,128)}, bf16[1408,768]{1,0:T(8,128)(2,1)}, bf16[1408,768]{1,0:T(8,128)(2,1)}, f32[8,768]{1,0:T(8,128)}) custom-call(bf16[768,1408]{1,0:T(8,128)(2,1)} %get-tuple-element.53.o_ref, bf16[1408,768]{1,0:T(8,128)(2,1)} %x_ref.7, bf16[1408,768]{1,0:T(8,128)(2,1)} %broadcast_select_fusion.g_ref, bf16[768,768]{1,0:T(8,128)(2,1)} %bitcast.12, ...), custom_call_target="tpu_custom_call" | custom-call | flops 1660944384 | bytes 15138816 | tf_op jit(solution)/shard_map/middle/pallas_call | solution.py:534
  173.5 0.7 reshape.257.ub_ref
  174.2 57.7 %feed.1 = (f32[1408,768]{1,0:T(8,128)}, f32[1408,768]{1,0:T(8,128)}, bf16[768,3072]{1,0:T(8,128)(2,1)}, bf16[3072,768]{1,0:T(8,128)(2,1)}, f32[8,3072]{1,0:T(8,128)}) custom-call(bf16[1408,768]{1,0:T(8,128)(2,1)} %get-tuple-element.56.a2_ref, bf16[1408,768]{1,0:T(8,128)(2,1)} %get-tuple-element.57.gm_ref, bf16[768,3072]{1,0:T(8,128)(2,1)} %bitcast.24, ...), custom_call_target="tpu_custom_call" | custom-call | flops 39862665216 | bytes 37748736 | tf_op jit(solution)/shard_map/feed/pallas_call | solution.py:590
  232.0 0.6 concatenate.26.vec_ref
  232.6 24.0 %join.1 = (bf16[1408,768]{1,0:T(8,128)(2,1)}, f32[1408,768]{1,0:T(8,128)}, bf16[768,1408]{1,0:T(8,128)(2,1)}, bf16[768,768]{1,0:T(8,128)(2,1)}, f32[5,8,768]{2,1,0:T(8,128)}) custom-call(f32[1408,768]{1,0:T(8,128)} %get-tuple-element.55.m1_ref, f32[1408,768]{1,0:T(8,128)} %get-tuple-element.60.bm_ref, f32[1408,768]{1,0:T(8,128)} %get-tuple-element.61.ga_ref, ...), custom_call_target="tpu_custom_call" | custom-call | flops 3321888768 | bytes 28114944 | tf_op jit(solution)/shard_map/join/pallas_call | solution.py:658
  256.6 89.8 %attend_back.1 = (bf16[3,1408,768]{2,1,0:T(8,128)(2,1)}, f32[24,3072]{1,0:T(8,128)}, f32[96,768]{1,0:T(8,128)}, f32[24,768]{1,0:T(8,128)}) custom-call(bf16[1408,2304]{1,0:T(8,128)(2,1)} %get-tuple-element.52.q_ref.k_ref.v_ref, bf16[1408,2304]{1,0:T(8,128)(2,1)} %get-tuple-element.52.q_ref.k_ref.v_ref, ...), custom_call_target="tpu_custom_call" | custom-call | flops 48721035264 | bytes 47579136 | tf_op jit(solution)/shard_map/attend_back/pallas_call | solution.py:730
  346.5 31.6 %finish.1 = (bf16[768,2304]{1,0:T(8,128)(2,1)}, f32[3,8,768]{2,1,0:T(8,128)}, f32[1408,768]{1,0:T(8,128)}, f32[2,8,768]{2,1,0:T(8,128)}) custom-call(bf16[1408,768]{1,0:T(8,128)(2,1)} %get-tuple-element.63.a1_ref, bf16[3,1408,768]{2,1,0:T(8,128)(2,1)} %get-tuple-element.70.gqkv_ref, bf16[768,2304]{1,0:T(8,128)(2,1)} %bitcast.20, bf16[1408,768]{1,0:T(8,128)(2,1)} %x_ref.7, ...), custom_call_target="tpu_custom_call" | custom-call | flops 9965666304 | bytes 21626880 | tf_op jit(solution)/shard_map/finish/pallas_call | solution.py:792
  378.1 0.9 reduce_sum.45
  379.2 0.8 reduce_sum.47
  380.3 0.6 pad.9.refs_1_
  380.9 41.2 %scatter_all.1 = (f32[24,2304]{1,0:T(8,128)}, f32[16,768]{1,0:T(8,128)}) custom-call(bf16[2,2,4,2,24,2304]{5,4,3,2,1,0:T(8,128)(2,1)} %bitcast.14, f32[16,768]{1,0:T(8,128)} %pad.9.refs_1_), custom_call_target="tpu_custom_call" | custom-call | tf_op jit(solution)/shard_map/scatter_all/pallas_call | solution.py:366
  422.2 0.8 reshape.248
  423.0 0.6 fusion.1
  423.6 0.6 dynamic_slice.35
  424.2 0.6 dynamic_slice.30
  424.8 1.6 copy.53
  426.4 0.6 copy.54
  427.0 0.7 copy.55
  427.7 0.7 copy.56
  (54 shorter events, 1.2 us)
Async XLA Ops:
  47.6 17.5 %copy-start.4 = (s32[1408]{0:T(1024)S(1)}, s32[1408]{0:T(1024)}, u32[]{:S(2)}) copy-start(s32[1408]{0:T(1024)} %param.18) | copy-start | bytes 16900
  346.5 32.6 %copy-start.2 = (f32[5,8,768]{2,1,0:T(8,128)S(1)}, f32[5,8,768]{2,1,0:T(8,128)}, u32[]{:S(2)}) copy-start(f32[5,8,768]{2,1,0:T(8,128)} %get-tuple-element.75) | copy-start | bytes 368644
  346.5 33.7 %copy-start.3 = (f32[8,3072]{1,0:T(8,128)S(1)}, f32[8,3072]{1,0:T(8,128)}, u32[]{:S(2)}) copy-start(f32[8,3072]{1,0:T(8,128)} %get-tuple-element.77) | copy-start | bytes 294916
  346.5 33.7 %copy-start.6 = (f32[8,768]{1,0:T(8,128)S(1)}, f32[8,768]{1,0:T(8,128)}, u32[]{:S(2)}) copy-start(f32[8,768]{1,0:T(8,128)} %get-tuple-element.78) | copy-start | bytes 73732
  380.3 46.1 %copy-start.5 = (f32[24,768]{1,0:T(8,128)S(1)}, f32[24,768]{1,0:T(8,128)}, u32[]{:S(2)}) copy-start(f32[24,768]{1,0:T(8,128)} %get-tuple-element.131) | copy-start | bytes 221188
  380.9 46.1 %copy-start.1 = (f32[24,3072]{1,0:T(8,128)S(1)}, f32[24,3072]{1,0:T(8,128)}, u32[]{:S(2)}) copy-start(f32[24,3072]{1,0:T(8,128)} %get-tuple-element.136) | copy-start | bytes 884740
  380.9 46.8 %copy-start = (f32[96,768]{1,0:T(8,128)S(1)}, f32[96,768]{1,0:T(8,128)}, u32[]{:S(2)}) copy-start(f32[96,768]{1,0:T(8,128)} %get-tuple-element.138) | copy-start | bytes 884740

commit v3 on v2

--- a/solution.py
+++ b/solution.py
@@ -119,18 +119,21 @@
             wire().wait_send()
 
 
-def halves(width):
+def halves(width, base=0):
     cut = (width // 256) * 128
-    return (pl.ds(0, cut), pl.ds(cut, width - cut)) if width > 512 else (pl.ds(0, width), None)
+    return pl.ds(base, cut), pl.ds(base + cut, width - cut)
 
 
 def gather_wires(sizes):
     return sizes["z"] + 4 * (sizes["x"] + sizes["y"] - 2)
 
 
-def gather_stages(near, mine, full, send, recv, own):
+def gather_stages(near, mine, full, send, recv, own, base=0, width=None):
     wires = Wires(near, send, recv)
     at = near.at
+    width = mine.shape[-1] if width is None else width
+    every = pl.ds(base, width)
+    mine = mine.at[:, every]
 
     def piece(cols, **fixed):
         return full.at[tuple(fixed.get(a, at[a]) for a in "xczy") + (ALL, cols)]
@@ -144,18 +147,17 @@
         parts = [piece(cols, **{a: ALL for a in done}, **{axis: near.along(axis, size - k)}) for k in near.shifts(axis)]
         return [wires.wire(p, p, "c", 1) for p in parts]
 
-    first, second = halves(mine.shape[-1])
-    whole_z = spread("z", "", ALL, mine)
-    column = piece(ALL, z=ALL)
+    first, second = halves(width, base)
+    whole_z = spread("z", "", every, mine)
+    column = piece(every, z=ALL)
     pair = [wires.wire(column, column, "c", 1)]
     one, two, one_on, two_on = [], [], [], []
     for cols, (a, b) in ((first, "yx"), (second, "xy")):
-        if cols is not None:
-            one += spread(a, "z", cols)
-            one_on += forward(a, "z", cols)
-            two += spread(b, "z" + a, cols)
-            two_on += forward(b, "z" + a, cols)
-    keep = lambda: pltpu.make_async_copy(mine, piece(ALL), own)
+        one += spread(a, "z", cols)
+        one_on += forward(a, "z", cols)
+        two += spread(b, "z" + a, cols)
+        two_on += forward(b, "z" + a, cols)
+    keep = lambda: pltpu.make_async_copy(mine, piece(every), own)
 
     def stage0():
         keep().start()
@@ -192,34 +194,6 @@
 
 def gathered(sizes, arrays):
     return [jax.ShapeDtypeStruct(lead(sizes) + a.shape, a.dtype) for a in arrays]
-
-
-def run_all(plans, lag=0):
-    for t in range(5 + lag * (len(plans) - 1)):
-        for i, plan in enumerate(plans):
-            if 0 <= t - lag * i < 5:
-                plan[t - lag * i]()
-
-
-def gather_kernel(sizes, count, *refs):
-    near = Near(sizes)
-    near.greet()
-    sems = refs[2 * count :]
-    run_all([
-        gather_stages(near, refs[i], refs[count + i], *sems[3 * i : 3 * i + 3]) for i in range(count)
-    ])
-
-
-def gather_all(sizes, arrays, collective_id):
-    return pl.pallas_call(
-        functools.partial(gather_kernel, sizes, len(arrays)),
-        in_specs=[pl.BlockSpec(memory_space=pltpu.VMEM)] * len(arrays),
-        out_specs=[pl.BlockSpec(memory_space=pltpu.HBM)] * len(arrays),
-        out_shape=gathered(sizes, arrays),
-        scratch_shapes=gather_scratch(sizes) * len(arrays),
-        compiler_params=params(collective_id=collective_id, has_side_effects=True),
-        name="gather_all",
-    )(*arrays)
 
 
 def scatter_wires(sizes):
@@ -250,7 +224,7 @@
     nz, ny, nx = sizes["z"], sizes["y"], sizes["x"]
     x, y, z = at["x"], at["y"], at["z"]
     first, second = halves(held.shape[-1])
-    load = lambda: pltpu.make_async_copy(grad.at[:, at["c"]], held, own)
+    loads = [] if own is None else [lambda: pltpu.make_async_copy(grad.at[:, at["c"]], held, own)]
     pair = [wires.wire(grad.at[:, 1 - at["c"]], got, "c", 1)]
     one = [wires.wire(held.at[near.along("x", k), :, :, :, first], x_first.at[k - 1], "x", k) for k in near.shifts("x")]
     one += [wires.wire(held.at[:, :, near.along("y", k), :, second], y_first.at[k - 1], "y", k) for k in near.shifts("y")]
@@ -265,18 +239,21 @@
         lax.fori_loop(0, nz, lambda i, carry: (body(i), carry)[1], 0)
 
     def stage0():
-        start(pair)
-        load().start()
+        start(pair, loads)
 
     def stage1():
-        load().wait()
+        for load in loads:
+            load().wait()
         landed(pair)
 
         @over_z
         def _(i):
             for a in range(nx):
                 for b in range(ny):
-                    add((a, i, b), [got[a, i, b]])
+                    if own is None:
+                        held[a, i, b] = (grad[a, at["c"], i, b].astype(F32) + got[a, i, b].astype(F32)).astype(held.dtype)
+                    else:
+                        add((a, i, b), [got[a, i, b]])
 
         start(one)
 
@@ -343,35 +320,8 @@
     return [stage(step) for step in range(5)]
 
 
-def scatter_kernel(sizes, count, lag, *refs):
-    near = Near(sizes)
-    near.greet()
-    ins, outs, rest = refs[: count + 1], refs[count + 1 : 2 * count + 2], refs[2 * count + 2 :]
-    plans = [
-        scatter_stages(near, ins[i], outs[i], *rest[SCATTER_REFS * i : SCATTER_REFS * (i + 1)]) for i in range(count)
-    ]
-    small = total_stages(near, ins[count], outs[count], *rest[SCATTER_REFS * count :])
-    run_all([*plans, small] if lag == 0 else plans, lag)
-    if lag:
-        run_all([small])
-
-
 def blocks_of(sizes, grads):
     return [g.reshape(lead(sizes) + (-1, g.shape[1])) for g in grads]
-
-
-def scatter_all(sizes, grads, small, collective_id, lag=0):
-    blocks = blocks_of(sizes, grads)
-    vmem, hbm = pl.BlockSpec(memory_space=pltpu.VMEM), pl.BlockSpec(memory_space=pltpu.HBM)
-    return pl.pallas_call(
-        functools.partial(scatter_kernel, sizes, len(grads), lag),
-        in_specs=[hbm] * len(grads) + [vmem],
-        out_specs=[vmem] * (len(grads) + 1),
-        out_shape=[jax.ShapeDtypeStruct(b.shape[-2:], F32) for b in blocks] + [jax.ShapeDtypeStruct(small.shape, F32)],
-        scratch_shapes=[s for b in blocks for s in scatter_scratch(sizes, *b.shape[-2:], b.dtype)] + total_scratch(sizes, small.shape),
-        compiler_params=params(collective_id=collective_id, has_side_effects=True),
-        name="scatter_all",
-    )(*blocks, small)
 
 
 def pump(schedule, plans, chunk):
@@ -396,7 +346,7 @@
             unit, _ = normalised(x_ref[rows, :].astype(F32))
             a1_ref[rows, :] = (unit * gain_ref[...] + shift_ref[...]).astype(BF)
 
-        row_loop(x_ref.shape[0], 32, body)
+        row_loop(x_ref.shape[0], 352, body)
 
     qkv_ref[...] = (dot(a1_ref[...], w_ref[...], 1, 0) + offset_ref[...]).astype(BF)
 
@@ -424,21 +374,139 @@
     )(x, w_in, gain, shift, offset)
 
 
+VEC_ROWS = 16
+UP_ROW = 10
+
+
+def placed(value, width, device):
+    size = value.shape[-1]
+    row = lax.broadcasted_iota(jnp.int32, (size, width), 0)
+    column = lax.broadcasted_iota(jnp.int32, (size, width), 1)
+    return dot(value, (column == row + device * size).astype(BF), 1, 0)
+
+
+def enter_kernel(sizes, tile, x_ref, w_ref, *refs):
+    vec_refs, (a1_out, qkv_out, w_out, vecs_ref) = refs[:10], refs[10:14]
+    a1_ref, qkv_ref, w_full, unit_ref, mine_ref = refs[14:19]
+    small_refs, gather_refs, out_sems = refs[19:23], refs[23:32], refs[32]
+    rows, d = x_ref.shape
+    near = Near(sizes)
+    near.greet()
+    device = lax.axis_index(AXES)
+    mine_ref[...] = jnp.zeros_like(mine_ref)
+    in_bias, *plain = vec_refs
+    up_bias = plain.pop(4)
+    for i, ref in enumerate(plain):
+        mine_ref[i : i + 1, :] = placed(ref[...], d, device)
+    both = placed(in_bias[...], 2 * d, device)
+    mine_ref[8:9, :] = both[:, :d]
+    mine_ref[9:10, :] = both[:, d:]
+    up = placed(up_bias[...], 6 * 512, device)
+    for i in range(6):
+        mine_ref[UP_ROW + i : UP_ROW + i + 1, :512] = up[:, 512 * i : 512 * (i + 1)]
+    plans = [
+        gather_stages(near, w_ref, w_full, *gather_refs[3 * t : 3 * t + 3], base=d * t, width=d) for t in range(3)
+    ]
+    small = total_stages(near, mine_ref, vecs_ref, *small_refs)
+    for plan in plans:
+        plan[0]()
+
+    def body(index, carry):
+        span = pl.ds(pl.multiple_of(index * tile, tile), tile)
+        unit_ref[span, :], _ = normalised(x_ref[span, :].astype(F32))
+        for step in range(3):
+            pl.when(index == step)(small[step])
+        return carry
+
+    lax.fori_loop(0, rows // tile, body, 0)
+    plans[0][1]()
+    small[3]()
+    plans[1][1]()
+    plans[0][2]()
+    plans[2][1]()
+    plans[1][2]()
+    small[4]()
+
+    def shifted(span):
+        a1_ref[span, :] = (unit_ref[span, :] * vecs_ref[1:2, :] + vecs_ref[2:3, :]).astype(BF)
+
+    row_loop(rows, tile, shifted)
+    sends = [pltpu.make_async_copy(a1_ref, a1_out, out_sems.at[0])]
+    sends[0].start()
+
+    def third(t):
+        cols = slice(d * t, d * (t + 1))
+        w = w_full[:, :, :, :, :, cols].astype(F32).reshape(d, d).astype(BF)
+        value = dot(a1_ref[...], w, 1, 0)
+        if t != 1:
+            value = value + vecs_ref[8 + t // 2 : 9 + t // 2, :]
+        qkv_ref[:, cols] = value.astype(BF)
+
+    def store(t):
+        cols = pl.ds(d * t, d)
+        sends.append(pltpu.make_async_copy(qkv_ref.at[:, cols], qkv_out.at[:, cols], out_sems.at[1 + t]))
+        sends[-1].start()
+
+    plans[0][3]()
+    plans[2][2]()
+    plans[0][4]()
+    third(0)
+    plans[1][3]()
+    store(0)
+    plans[1][4]()
+    plans[2][3]()
+    third(1)
+    store(1)
+    plans[2][4]()
+    sends.append(pltpu.make_async_copy(w_full, w_out, out_sems.at[4]))
+    sends[-1].start()
+    third(2)
+    store(2)
+    for copy in sends:
+        copy.wait()
+
+
+def enter(sizes, x, w_in, vectors, tile=352):
+    rows, d = x.shape
+    vmem, hbm = pl.BlockSpec(memory_space=pltpu.VMEM), pl.BlockSpec(memory_space=pltpu.HBM)
+    full = lead(sizes) + w_in.shape
+    return pl.pallas_call(
+        functools.partial(enter_kernel, sizes, tile),
+        in_specs=[vmem] * 12,
+        out_specs=[hbm, hbm, hbm, vmem],
+        out_shape=[
+            jax.ShapeDtypeStruct((rows, d), BF),
+            jax.ShapeDtypeStruct((rows, 3 * d), BF),
+            jax.ShapeDtypeStruct(full, BF),
+            jax.ShapeDtypeStruct((VEC_ROWS, d), F32),
+        ],
+        scratch_shapes=[
+            pltpu.VMEM((rows, d), BF),
+            pltpu.VMEM((rows, 3 * d), BF),
+            pltpu.VMEM(full, BF),
+            pltpu.VMEM((rows, d), F32),
+            pltpu.VMEM((VEC_ROWS, d), F32),
+            *total_scratch(sizes, (VEC_ROWS, d)),
+            *gather_scratch(sizes) * 3,
+            pltpu.SemaphoreType.DMA((5,)),
+        ],
+        compiler_params=params(collective_id=0, has_side_effects=True),
+        name="enter",
+    )(x, w_in, *[v[None] for v in vectors])
+
+
 def chunks(rows, size):
     return [(start, min(size, rows - start)) for start in range(0, rows, size)]
 
 
 GATHER_AT = {
     (0, 0): [(0, 0), (1, 0)],
-    (0, 3): [(0, 1)],
-    (1, 0): [(2, 0), (0, 2)],
-    (1, 3): [(1, 1)],
-    (2, 0): [(0, 3)],
-    (2, 3): [(1, 2)],
-    (3, 0): [(2, 1)],
-    (4, 0): [(1, 3), (2, 2)],
-    (5, 3): [(2, 3)],
-    (5, 5): [(0, 4), (1, 4), (2, 4)],
+    (1, 0): [(0, 1), (2, 0)],
+    (2, 0): [(1, 1), (0, 2)],
+    (3, 0): [(2, 1), (1, 2), (0, 3)],
+    (4, 0): [(2, 2)],
+    (5, 0): [(1, 3)],
+    (5, -1): [(2, 3), (0, 4), (1, 4), (2, 4)],
 }
 
 
@@ -472,6 +540,7 @@
             inv_ref[0, half : half + 1, span] = inverse
             head = pl.ds(half * HD, HD)
             o_ref[head, span] = (dot(vt_ref[head, :], weights_low, 1, 0) * inverse).astype(BF)
+    pump(schedule, plans, -1)
 
 
 def attend(qkv, mark, far, sizes, shards, chunk=256):
@@ -513,7 +582,7 @@
 
 
 def middle_kernel(o_ref, x_ref, g_ref, w_ref, vec_ref, m1_ref, a2_ref, gm_ref, gmsum_ref):
-    bias, scale1, gain2, shift2, scale2 = (vec_ref[i : i + 1, :] for i in range(5))
+    bias, scale1, gain2, shift2, scale2 = (vec_ref[i : i + 1, :] for i in (0, 3, 5, 6, 7))
     m1_ref[...] = dot(o_ref[...], w_ref[...], 0, 0)
     gmsum_ref[...] = jnp.zeros_like(gmsum_ref)
 
@@ -526,7 +595,7 @@
         gm_ref[rows, :] = gm
         gmsum_ref[...] += jnp.sum(gm.astype(F32).reshape(-1, 8, gm.shape[-1]), axis=0)
 
-    row_loop(x_ref.shape[0], 32, body)
+    row_loop(x_ref.shape[0], 352, body)
 
 
 def middle(o, x, g, w_out, vec):
@@ -558,7 +627,7 @@
     return u * phi, phi + u * bell * 0.3989422804014327
 
 
-def feed_kernel(chunk, a2_ref, gm_ref, up_ref, ub_ref, down_ref, bm_ref, ga_ref, dup_ref, ddown_ref, dub_ref, gl_ref, gu_ref):
+def feed_kernel(chunk, a2_ref, gm_ref, up_ref, vec_ref, down_ref, bm_ref, ga_ref, dup_ref, ddown_ref, dub_ref, gl_ref, gu_ref):
     first = pl.program_id(0) == 0
 
     @pl.when(first)
@@ -566,10 +635,11 @@
         bm_ref[...] = jnp.zeros_like(bm_ref)
         ga_ref[...] = jnp.zeros_like(ga_ref)
 
-    total = jnp.zeros((8, ub_ref.shape[-1]), F32)
+    bias = vec_ref[pl.ds(UP_ROW + pl.program_id(0), 1), : up_ref.shape[-1]]
+    total = jnp.zeros((8, up_ref.shape[-1]), F32)
     for start, size in chunks(a2_ref.shape[0], chunk):
         rows = pl.ds(start, size)
-        u = dot(a2_ref[rows, :], up_ref[...], 1, 0) + ub_ref[...]
+        u = dot(a2_ref[rows, :], up_ref[...], 1, 0) + bias
         back = dot(gm_ref[rows, :], down_ref[...], 1, 1)
         active, slope = gelu_parts(u)
         low = active.astype(BF)
@@ -584,7 +654,7 @@
     dup_ref[...] = dot(a2_ref[...], gu_ref[...], 0, 0).astype(dup_ref.dtype)
 
 
-def feed(a2, gm, w_up, b_up, w_down, block=512, chunk=704, kind=BF):
+def feed(a2, gm, w_up, vecs, w_down, block=512, chunk=704, kind=BF):
     rows, d = a2.shape
     ff = w_up.shape[1]
     return pl.pallas_call(
@@ -594,7 +664,7 @@
             whole((rows, d)),
             whole((rows, d)),
             pl.BlockSpec((d, block), lambda f: (0, f)),
-            pl.BlockSpec((1, block), lambda f: (0, f)),
+            whole((VEC_ROWS, d)),
             pl.BlockSpec((block, d), lambda f: (f, 0)),
         ],
         out_specs=[
@@ -615,11 +685,11 @@
         compiler_params=params(),
         cost_estimate=cost(12 * rows * d * ff, 4 * 4 * d * ff),
         name="feed",
-    )(a2, gm, w_up, b_up, w_down)
+    )(a2, gm, w_up, vecs, w_down)
 
 
 def join_kernel(size, m1_ref, bm_ref, ga_ref, x_ref, g_ref, o_ref, w_ref, vec_ref, out_ref, gm1_ref, go_ref, dout_ref, sums_ref, gb_ref):
-    bias2, scale1, gain2, scale2 = (vec_ref[i : i + 1, :] for i in range(4))
+    bias2, scale1, gain2, scale2 = (vec_ref[i : i + 1, :] for i in (4, 3, 5, 7))
     step = pl.program_id(0)
 
     @pl.when(step == 0)
@@ -652,13 +722,13 @@
         dout_ref[...] = dot(o_ref[...], gb_ref[...], 1, 0).astype(dout_ref.dtype)
 
 
-def join(m1, bm, ga, x, g, o, w_out, vec, tile=128, kind=BF):
+def join(m1, bm, ga, x, g, o, w_out, vec, tile=352, kind=BF):
     rows, d = x.shape
     by_rows = pl.BlockSpec((tile, d), lambda i: (i, 0))
     return pl.pallas_call(
-        functools.partial(join_kernel, 32),
+        functools.partial(join_kernel, 352),
         grid=(rows // tile,),
-        in_specs=[by_rows] * 5 + [whole((d, rows)), whole((d, d)), whole((8, d))],
+        in_specs=[by_rows] * 5 + [whole((d, rows)), whole((d, d)), whole((VEC_ROWS, d))],
         out_specs=[by_rows, by_rows, whole((d, rows)), whole((d, d)), whole((5, 8, d))],
         out_shape=[
             jax.ShapeDtypeStruct((rows, d), BF),
@@ -675,16 +745,13 @@
 
 
 SCATTER_AT = {
-    (0, 0): [(0, 0)],
-    (0, 3): [(0, 1), (1, 0)],
-    (1, 3): [(2, 0)],
+    (0, 0): [(0, 0), (1, 0)],
+    (1, 0): [(0, 1), (2, 0)],
     (2, 0): [(0, 2), (1, 1)],
-    (3, 0): [(0, 3)],
-    (4, 0): [(1, 2), (2, 1)],
-    (4, 3): [(0, 4)],
-    (5, 0): [(1, 3), (2, 2)],
-    (5, 3): [(2, 3)],
-    (5, 5): [(1, 4), (2, 4)],
+    (3, 0): [(0, 3), (2, 1)],
+    (4, 0): [(1, 2), (2, 2)],
+    (5, 0): [(1, 3), (2, 3), (0, 4)],
+    (5, -1): [(1, 4), (2, 4)],
 }
 
 
@@ -720,6 +787,7 @@
     gk = [dot(gs_ref[half], q_ref[...], 1, 0) for half in range(2)]
     out_ref[1] = (jnp.where(low, gk[0], gk[1]) * factor).astype(BF)
     out_ref[2] = (dot(e_ref[0], gp_ref[0], 1, 1) + dot(e_ref[1], gp_ref[1], 1, 1)).astype(BF)
+    pump(schedule, plans, -1)
 
 
 def attend_back(qkv, go, o, e, inv, sizes, grads, chunk=256):
@@ -784,7 +852,7 @@
             for index, value in enumerate((ga * unit, ga)):
                 sums_ref[index] += jnp.sum(value.reshape(-1, 8, value.shape[-1]), axis=0)
 
-        row_loop(x_ref.shape[0], 32, body)
+        row_loop(x_ref.shape[0], 352, body)
 
 
 def finish(a1, gqkv, w_in, x, gm1, gain, kind=BF):
@@ -819,6 +887,186 @@
     )(a1, gqkv, w_in, x, gm1, gain)
 
 
+def leave_kernel(sizes, tile, a1_in, gqkv_in, w_in, x_in, gm1_in, vec_ref, join_ref, ub_ref, gmsum_ref, gx_out, dw_ref, early_ref, late_ref, *refs):
+    a1_ref, gqkv_ref, w_ref, x_ref, gm1_ref, gx_ref, ga_ref, sums_ref, mine_ref, last_ref = refs[:10]
+    grad_refs, refs = refs[10:13], refs[13:]
+    scatter_refs, refs = [refs[9 * t : 9 * t + 9] for t in range(3)], refs[27:]
+    early_refs, late_refs, in_sems, out_sems = refs[:4], refs[4:8], refs[8], refs[9]
+    rows, d = x_in.shape
+    count = rows // tile
+    moves = [(a1_in, a1_ref), *[(gqkv_in.at[t], gqkv_ref.at[t]) for t in range(3)], (w_in, w_ref), (x_in, x_ref), (gm1_in, gm1_ref)]
+    fetch = [pltpu.make_async_copy(src, dst, in_sems.at[n]) for n, (src, dst) in enumerate(moves)]
+    for copy in fetch:
+        copy.start()
+    near = Near(sizes)
+    near.greet()
+    row = lambda value: jnp.sum(value, axis=0, keepdims=True)
+    mine_ref[...] = jnp.zeros_like(mine_ref)
+    for i, value in enumerate(
+        (row(join_ref[4]), row(join_ref[3]) / vec_ref[3:4, :], row(gmsum_ref[...]), row(join_ref[1]), row(join_ref[2]), row(join_ref[0]))
+    ):
+        mine_ref[i : i + 1, :] = value
+    for i in range(4):
+        mine_ref[8 + i : 9 + i, :] = row(ub_ref[:, d * i : d * (i + 1)])
+    plans = [
+        scatter_stages(near, grad_refs[t], dw_ref.at[:, pl.ds(d * t, d)], *scatter_refs[t], None) for t in range(3)
+    ]
+    early = total_stages(near, mine_ref, early_ref, *early_refs)
+    late = total_stages(near, last_ref, late_ref, *late_refs)
+    last_ref[...] = jnp.zeros_like(last_ref)
+
+    def weight(t):
+        fetch[1 + t].wait()
+        value = dot(a1_ref[...], gqkv_ref[t], 0, 0)
+        grad_refs[t][...] = value.reshape(grad_refs[t].shape).astype(BF)
+
+    def back(t):
+        part = dot(gqkv_ref[t], w_ref[:, d * t : d * (t + 1)], 1, 1)
+        if t == 0:
+            ga_ref[...] = part
+        else:
+            ga_ref[...] += part
+        if t != 1:
+            total = jnp.zeros((1, d), F32)
+            for start_row, size in chunks(rows, tile):
+                total += row(gqkv_ref[t, pl.ds(start_row, size), :].astype(F32))
+            last_ref[2 + t // 2 : 3 + t // 2, :] = total
+
+    fetch[0].wait()
+    weight(0)
+    early[0]()
+    plans[0][0]()
+    weight(1)
+    plans[0][1]()
+    plans[1][0]()
+    early[1]()
+    weight(2)
+    plans[1][1]()
+    plans[2][0]()
+    fetch[4].wait()
+    back(0)
+    plans[0][2]()
+    plans[2][1]()
+    early[2]()
+    back(1)
+    plans[1][2]()
+    back(2)
+    plans[0][3]()
+    early[3]()
+    fetch[5].wait()
+    fetch[6].wait()
+    sums_ref[...] = jnp.zeros_like(sums_ref)
+
+    def send(index):
+        span = pl.ds(pl.multiple_of(index * tile, tile), tile)
+        return pltpu.make_async_copy(gx_ref.at[span], gx_out.at[span], out_sems.at[index])
+
+    between = [[], [plans[2][2], plans[1][3]], []]
+
+    def body(index, carry):
+        span = pl.ds(pl.multiple_of(index * tile, tile), tile)
+        unit, inverse = normalised(x_ref[span, :].astype(F32))
+        ga = ga_ref[span, :]
+        gx_ref[span, :] = gm1_ref[span, :] + norm_back(unit, inverse, ga * vec_ref[1:2, :])
+        for n, value in enumerate((ga * unit, ga)):
+            sums_ref[n] += jnp.sum(value.reshape(-1, 8, d), axis=0)
+        for n, stages in enumerate(between):
+
+            @pl.when(index == n)
+            def _():
+                for stage in stages:
+                    stage()
+
+        pl.when(index > 0)(lambda: send(index - 1).start())
+        return carry
+
+    lax.fori_loop(0, count, body, 0)
+    for n in range(2):
+        last_ref[n : n + 1, :] = row(sums_ref[n])
+    late[0]()
+    send(count - 1).start()
+    early[4]()
+    plans[2][3]()
+    late[1]()
+    plans[0][4]()
+    late[2]()
+    plans[1][4]()
+    late[3]()
+    plans[2][4]()
+    late[4]()
+    for index in range(count):
+        send(index).wait()
+
+
+def leave(sizes, a1, gqkv, w_in, x, gm1, vecs, join_sums, ub_sum, gm_sum, tile=352):
+    rows, d = x.shape
+    vmem, hbm = pl.BlockSpec(memory_space=pltpu.VMEM), pl.BlockSpec(memory_space=pltpu.HBM)
+    block = d // (sizes["x"] * 2 * sizes["z"] * sizes["y"])
+    return pl.pallas_call(
+        functools.partial(leave_kernel, sizes, tile),
+        in_specs=[hbm] * 5 + [vmem] * 4,
+        out_specs=[hbm, vmem, vmem, vmem],
+        out_shape=[
+            jax.ShapeDtypeStruct((rows, d), F32),
+            jax.ShapeDtypeStruct((block, 3 * d), F32),
+            jax.ShapeDtypeStruct((16, d), F32),
+            jax.ShapeDtypeStruct((8, d), F32),
+        ],
+        scratch_shapes=[
+            pltpu.VMEM((rows, d), BF),
+            pltpu.VMEM((3, rows, d), BF),
+            pltpu.VMEM((d, 3 * d), BF),
+            pltpu.VMEM((rows, d), BF),
+            pltpu.VMEM((rows, d), F32),
+            pltpu.VMEM((rows, d), F32),
+            pltpu.VMEM((rows, d), F32),
+            pltpu.VMEM((2, 8, d), F32),
+            pltpu.VMEM((16, d), F32),
+            pltpu.VMEM((8, d), F32),
+            *[pltpu.VMEM(lead(sizes) + (block, d), BF)] * 3,
+            *scatter_scratch(sizes, block, d, BF)[:-1] * 3,
+            *total_scratch(sizes, (16, d)),
+            *total_scratch(sizes, (8, d)),
+            pltpu.SemaphoreType.DMA((7,)),
+            pltpu.SemaphoreType.DMA((rows // tile,)),
+        ],
+        compiler_params=params(collective_id=3, has_side_effects=True),
+        name="leave",
+    )(a1, gqkv, w_in, x, gm1, vecs, join_sums, ub_sum, gm_sum)
+
+
+def share_kernel(early_ref, late_ref, *refs):
+    grads, outs, vec_outs = refs[:4], refs[4:8], refs[8:]
+    for src, dst in zip(grads, outs):
+        dst[...] = src[...]
+    device = lax.axis_index(AXES)
+    d = early_ref.shape[-1]
+
+    def entries(ref, first_row, size):
+        at = device * size
+        line = ref[pl.ds(first_row + lax.div(at, d), 1), :]
+        return pltpu.roll(jnp.broadcast_to(line, (8, d)), lax.rem(d - lax.rem(at, d), d), 1)[:1, :size]
+
+    spots = [
+        (late_ref, 2), (early_ref, 0), (late_ref, 0), (late_ref, 1), (early_ref, 1),
+        (early_ref, 8), (early_ref, 2), (early_ref, 3), (early_ref, 4), (early_ref, 5),
+    ]
+    for (ref, first_row), out in zip(spots, vec_outs):
+        out[...] = entries(ref, first_row, out.shape[-1])
+
+
+def share(early, late, grads, sizes):
+    vmem = pl.BlockSpec(memory_space=pltpu.VMEM)
+    return pl.pallas_call(
+        share_kernel,
+        in_specs=[vmem] * 6,
+        out_specs=[vmem] * 14,
+        out_shape=[jax.ShapeDtypeStruct(g.shape, F32) for g in grads] + [jax.ShapeDtypeStruct((1, n), F32) for n in sizes],
+        compiler_params=params(),
+        name="share",
+    )(early, late, *grads)
+
+
 def take(a):
     return lax.all_gather(a, AXES, axis=0, tiled=True)
 
@@ -832,70 +1080,49 @@
     up_weight, up_bias, down_weight, down_bias, second_gain, second_shift, second_scale,
 ):
     rows, d = inputs.shape
-    n = lax.axis_size(AXES)
     vectors = (
         in_bias, out_bias, first_gain, first_shift, first_scale,
         up_bias, down_bias, second_gain, second_shift, second_scale,
     )
     own = all(w.shape[0] % 8 == 0 for w in (in_weight, out_weight, up_weight, down_weight))
-    joined = jnp.concatenate(vectors)[None]
-    used = joined.shape[1]
     if own:
-        tile = jnp.pad(joined, ((0, 7), (0, -used % 128)))
-        w_in, vec = gather_all(sizes, [in_weight, tile], 0)
-        w_in, vec = w_in.reshape(-1, 3 * d), vec.reshape(n, 8, -1)[:, 0, :used]
+        a1, qkv, w_in, vecs = enter(sizes, inputs, in_weight, vectors)
+        w_in = w_in.reshape(d, 3 * d)
     else:
-        w_in, vec = take(in_weight), take(joined)
-    vecs = []
-    at = 0
-    for v in vectors:
-        vecs.append(vec[:, at : at + v.shape[0]].reshape(1, -1).astype(F32))
-        at += v.shape[0]
-    in_bias, out_bias, gain1, shift1, scale1, up_bias, down_bias, gain2, shift2, scale2 = vecs
+        w_in = take(in_weight)
+        row = lambda v: take(v).astype(F32).reshape(-1, d)
+        vecs = jnp.concatenate(
+            [row(v) for v in (out_bias, first_gain, first_shift, first_scale, down_bias, second_gain, second_shift, second_scale, in_bias)]
+            + [jnp.pad(take(up_bias).astype(F32).reshape(6, 512), ((0, 0), (0, d - 512)))]
+        )
+        offset = jnp.concatenate([vecs[8:9], jnp.zeros((1, d), F32), vecs[9:10]], axis=1)
+        a1, qkv = project(inputs, w_in, vecs[1:2], vecs[2:3], offset)
     lane = lax.broadcasted_iota(jnp.int32, (1, 128), 1) % HD
     same = segment_ids[:, None] == lane
     mark = same.astype(BF)
     far = jnp.where(same | (lane > PADDING), 0.0, FAR).astype(BF)
     g = jnp.where((segment_ids < PADDING)[:, None], cotangent, jnp.zeros_like(cotangent))
-    offset = jnp.concatenate([in_bias[:, :d], jnp.zeros((1, d), F32), in_bias[:, d:]], axis=1)
-    a1, qkv = project(inputs, w_in, gain1, shift1, offset)
     o, e, inv, *full = attend(qkv, mark, far, sizes, [out_weight, up_weight, down_weight] if own else [])
     w_out, w_up, w_down = (
         (f.reshape(-1, f.shape[-1]) for f in full) if own else (take(w) for w in (out_weight, up_weight, down_weight))
     )
-    blank = jnp.zeros((1, d), F32)
-    m1, a2, gm, gm_sum = middle(
-        o, inputs, g, w_out, jnp.concatenate([out_bias, scale1, gain2, shift2, scale2, blank, blank, blank])
-    )
-    bm, ga2, d_up, d_down, ub_sum = feed(a2, gm, w_up, up_bias, w_down)
-    outputs, gm1, go, d_out, join_sums = join(
-        m1, bm, ga2, inputs, g, o, w_out, jnp.concatenate([down_bias, scale1, gain2, scale2, blank, blank, blank, blank])
-    )
+    m1, a2, gm, gm_sum = middle(o, inputs, g, w_out, vecs)
+    bm, ga2, d_up, d_down, ub_sum = feed(a2, gm, w_up, vecs, w_down)
+    outputs, gm1, go, d_out, join_sums = join(m1, bm, ga2, inputs, g, o, w_out, vecs)
     gqkv, *done = attend_back(qkv, go, o, e, inv, sizes, [d_up, d_down, d_out] if own else [])
-    d_up, d_down, d_out = done if own else (give(v) for v in (d_up, d_down, d_out))
-    d_in, col_sums, gx, last_sums = finish(a1, gqkv, w_in, inputs, gm1, gain1)
-    s = jnp.sum
-    j = s(join_sums, axis=1)
-    c = s(col_sums, axis=1)
-    t = s(last_sums, axis=1)
-    sums = [
-        jnp.concatenate([c[0], c[2]]), j[4], t[0], t[1], j[3] / scale1[0],
-        s(ub_sum, axis=0), s(gm_sum, axis=0), j[1], j[2], j[0],
-    ]
-    small = jnp.concatenate(sums).reshape(-1, d)
-    small = jnp.pad(small, ((0, -small.shape[0] % 8), (0, 0)))
     if own:
-        d_in, small = scatter_all(sizes, [d_in], small, 3)
+        gx, d_in, early, late = leave(sizes, a1, gqkv, w_in, inputs, gm1, vecs, join_sums, ub_sum, gm_sum)
+        d_up, d_down, d_out, d_in, *out = share(early, late, [*done, d_in], [v.shape[0] for v in vectors])
+        out = [v.reshape(-1) for v in out]
     else:
-        d_in, small = give(d_in), lax.psum(small, AXES)
-    small = small.reshape(-1)
-    here = lax.axis_index(AXES)
-    out = []
-    at = 0
-    for v in sums:
-        size = v.shape[0] // n
-        out.append(lax.dynamic_slice(small, (at + here * size,), (size,)))
-        at += v.shape[0]
+        d_in, col_sums, gx, last_sums = finish(a1, gqkv, w_in, inputs, gm1, vecs[1:2])
+        d_in, d_up, d_down, d_out = (give(v) for v in (d_in, d_up, d_down, d_out))
+        s = jnp.sum
+        j, c, t = (s(v, axis=1) for v in (join_sums, col_sums, last_sums))
+        sums = (
+            jnp.concatenate([c[0], c[2]]), j[4], t[0], t[1], j[3] / vecs[3], s(ub_sum, axis=0), s(gm_sum, axis=0), j[1], j[2], j[0],
+        )
+        out = [give(v) for v in sums]
     return (
         outputs, gx, d_in, out[0], d_out, out[1], out[2], out[3], out[4],
         d_up, out[5], d_down, out[6], out[7], out[8], out[9],

time: 433 us -> 357 us (0.82)
  Pallas kernels: 400 us -> 338 us
  local copies, waits for them, and re-layouts: 19.4 us -> 4.56 us
    pallas_call x5 -> x4, Pallas kernels: 150 us -> 101 us  [the longest x1 44.3 us: leave(): pl.pallas_call(functools.partial(leave_kernel, sizes, tile), in_specs=[hb...]
    concatenate x7 -> x0, local copies, waits for them, and re-layouts: 8.07 us -> none  [the longest x1 6.77 us: layer(): joined = jnp.concatenate(vectors)[None]]
    pallas_call x1, Pallas kernels: 18 us -> 11.4 us  [middle(): pl.pallas_call(middle_kernel, out_shape=[jax.ShapeDtypeStruct((rows, d),...]
where the time goes in v3:
time: 357 us; the launch traced here: 352 us
  Pallas kernels  338 us (95%)
  other arithmetic  7.37 us (2%)
  local copies, waits for them, and re-layouts  4.56 us (1%)
    pallas_call x1, Pallas kernels, attend_back(): pl.pallas_call(functools.partial(attend_back_kernel, chunk, sizes, count)...  85.7 us
    pallas_call x1, Pallas kernels, attend(): pl.pallas_call(functools.partial(attend_kernel, chunk, sizes, count), gri...  81.2 us
    pallas_call x1, Pallas kernels, feed(): pl.pallas_call(functools.partial(feed_kernel, chunk), grid=(ff // block,)...  59 us
    pallas_call x1, Pallas kernels, leave(): pl.pallas_call(functools.partial(leave_kernel, sizes, tile), in_specs=[hb...  44.3 us
    pallas_call x1, Pallas kernels, enter(): pl.pallas_call(functools.partial(enter_kernel, sizes, tile), in_specs=[vm...  37.7 us
    pallas_call x1, Pallas kernels, join(): pl.pallas_call(functools.partial(join_kernel, 352), grid=(rows // tile,),...  17.1 us
    pallas_call x1, Pallas kernels, middle(): pl.pallas_call(middle_kernel, out_shape=[jax.ShapeDtypeStruct((rows, d),...  11.4 us

profile of v3, /device:TPU:0, one launch (start us, length us, event | category | flops | bytes accessed | tf_op | source)
XLA Modules:
  0.0 351.6 jit_solution(11734543592764342269)
XLA Ops:
  0.7 0.7 broadcast_compare_fusion
  1.4 1.7 select_convert_fusion.far_ref
  3.1 1.7 compare_convert_fusion.mark_ref
  4.7 3.3 broadcast_select_fusion.g_ref
  8.0 37.7 %enter.1 = (bf16[1408,768]{1,0:T(8,128)(2,1)}, bf16[1408,2304]{1,0:T(8,128)(2,1)}, bf16[2,2,4,2,24,2304]{5,4,3,2,1,0:T(8,128)(2,1)}, f32[16,768]{1,0:T(8,128)}) custom-call(bf16[1408,768]{1,0:T(8,128)(2,1)} %x_in.1, bf16[24,2304]{1,0:T(8,128)(2,1)} %w_ref.1, bf16[1,48]{1,0:T(2,128)(2,1)} %bitcast.30, bf16[1,24]{1,0:T(2,128)(2,1)} %bitcast.31, ...), custom_call_target="tpu_custom_call" | custom-call | tf_op jit(solution)/shard_map/enter/pallas_call | solution.py:473
  45.7 81.2 %attend.1 = (bf16[768,1408]{1,0:T(8,128)(2,1)}, bf16[12,1408,1408]{2,1,0:T(8,128)(2,1)}, f32[6,2,1408]{2,1,0:T(2,128)}, bf16[2,2,4,2,24,768]{5,4,3,2,1,0:T(8,128...) custom-call(bf16[1408,2304]{1,0:T(8,128)(2,1)} %get-tuple-element.62.q_ref.k_ref.v_ref, ...), custom_call_target="tpu_custom_call" | custom-call | flops 24360517632 | bytes 47579136 | tf_op jit(solution)/shard_map/attend/pallas_call | solution.py:550
  127.0 11.4 %middle.1 = (f32[1408,768]{1,0:T(8,128)}, bf16[1408,768]{1,0:T(8,128)(2,1)}, bf16[1408,768]{1,0:T(8,128)(2,1)}, f32[8,768]{1,0:T(8,128)}) custom-call(bf16[768,1408]{1,0:T(8,128)(2,1)} %get-tuple-element.63.o_ref, bf16[1408,768]{1,0:T(8,128)(2,1)} %x_in.1, bf16[1408,768]{1,0:T(8,128)(2,1)} %broadcast_select_fusion.g_ref, bf16[768,768]{1,0:T(8,128)(2,1)} %bitcast.27, ...), custom_call_target="tpu_custom_call" | custom-call | flops 1660944384 | bytes 15138816 | tf_op jit(solution)/shard_map/middle/pallas_call | solution.py:603
  138.4 59.0 %feed.1 = (f32[1408,768]{1,0:T(8,128)}, f32[1408,768]{1,0:T(8,128)}, bf16[768,3072]{1,0:T(8,128)(2,1)}, bf16[3072,768]{1,0:T(8,128)(2,1)}, f32[8,3072]{1,0:T(8,128)}) custom-call(bf16[1408,768]{1,0:T(8,128)(2,1)} %get-tuple-element.67.a2_ref, bf16[1408,768]{1,0:T(8,128)(2,1)} %get-tuple-element.68.gm_ref, bf16[768,3072]{1,0:T(8,128)(2,1)} %bitcast.53, ...), custom_call_target="tpu_custom_call" | custom-call | flops 39862665216 | bytes 37748736 | tf_op jit(solution)/shard_map/feed/pallas_call | solution.py:660
  197.4 17.1 %join.1 = (bf16[1408,768]{1,0:T(8,128)(2,1)}, f32[1408,768]{1,0:T(8,128)}, bf16[768,1408]{1,0:T(8,128)(2,1)}, bf16[768,768]{1,0:T(8,128)(2,1)}, f32[5,8,768]{2,1,0:T(8,128)}) custom-call(f32[1408,768]{1,0:T(8,128)} %get-tuple-element.66.m1_ref, f32[1408,768]{1,0:T(8,128)} %get-tuple-element.71.bm_ref, f32[1408,768]{1,0:T(8,128)} %get-tuple-element.72.ga_ref, ...), custom_call_target="tpu_custom_call" | custom-call | flops 3321888768 | bytes 28114944 | tf_op jit(solution)/shard_map/join/pallas_call | solution.py:728
  214.4 85.7 %attend_back.1 = (bf16[3,1408,768]{2,1,0:T(8,128)(2,1)}, f32[24,3072]{1,0:T(8,128)}, f32[96,768]{1,0:T(8,128)}, f32[24,768]{1,0:T(8,128)}) custom-call(bf16[1408,2304]{1,0:T(8,128)(2,1)} %get-tuple-element.62.q_ref.k_ref.v_ref, bf16[1408,2304]{1,0:T(8,128)(2,1)} %get-tuple-element.62.q_ref.k_ref.v_ref, ...), custom_call_target="tpu_custom_call" | custom-call | flops 48721035264 | bytes 47579136 | tf_op jit(solution)/shard_map/attend_back/pallas_call | solution.py:798
  300.1 44.3 %leave.1 = (f32[1408,768]{1,0:T(8,128)}, f32[24,2304]{1,0:T(8,128)}, f32[16,768]{1,0:T(8,128)}, f32[8,768]{1,0:T(8,128)}) custom-call(bf16[1408,768]{1,0:T(8,128)(2,1)} %get-tuple-element.74.a1_in, bf16[3,1408,768]{2,1,0:T(8,128)(2,1)} %get-tuple-element.81.gqkv_in, bf16[768,2304]{1,0:T(8,128)(2,1)} %bitcast.29, bf16[1408,768]{1,0:T(8,128)(2,1)} %x_in.1, ...), custom_call_target="tpu_custom_call" | custom-call | tf_op jit(solution)/shard_map/leave/pallas_call | solution.py:1005
  344.3 2.2 share.1
  346.5 4.6 %copy.34 = f32[1408,768]{1,0:T(8,128)} copy(f32[1408,768]{1,0:T(8,128)} %get-tuple-element.125) | data formatting | bytes 8650752
  (2 shorter events, 0.0 us)

commit v4 on v3

--- a/solution.py
+++ b/solution.py
@@ -128,12 +128,13 @@
     return sizes["z"] + 4 * (sizes["x"] + sizes["y"] - 2)
 
 
-def gather_stages(near, mine, full, send, recv, own, base=0, width=None):
+def gather_stages(near, mine, full, send, recv, own, base=0, width=None, part="all"):
     wires = Wires(near, send, recv)
     at = near.at
-    width = mine.shape[-1] if width is None else width
+    width = full.shape[-1] if width is None else width
     every = pl.ds(base, width)
-    mine = mine.at[:, every]
+    if part != "rest":
+        mine = mine.at[:, every]
 
     def piece(cols, **fixed):
         return full.at[tuple(fixed.get(a, at[a]) for a in "xczy") + (ALL, cols)]
@@ -148,7 +149,7 @@
         return [wires.wire(p, p, "c", 1) for p in parts]
 
     first, second = halves(width, base)
-    whole_z = spread("z", "", every, mine)
+    whole_z = [] if part == "rest" else spread("z", "", every, mine)
     column = piece(every, z=ALL)
     pair = [wires.wire(column, column, "c", 1)]
     one, two, one_on, two_on = [], [], [], []
@@ -163,9 +164,14 @@
         keep().start()
         start(whole_z)
 
-    def stage1():
+    def arrive():
         keep().wait()
         landed(whole_z)
+        left(whole_z)
+
+    def stage1():
+        if part != "rest":
+            arrive()
         start(one, pair)
 
     def stage2():
@@ -177,10 +183,10 @@
         start(two_on)
 
     def stage4():
-        left(whole_z, pair, one, two, one_on, two_on)
+        left(pair, one, two, one_on, two_on)
         landed(pair, one_on, two_on)
 
-    return [stage0, stage1, stage2, stage3, stage4]
+    return [stage0, arrive] if part == "first" else [stage0, stage1, stage2, stage3, stage4]
 
 
 def gather_scratch(sizes):
@@ -218,7 +224,7 @@
     ]
 
 
-def scatter_stages(near, grad, out, held, got, x_first, y_first, y_then, x_then, z_last, send, recv, own):
+def scatter_stages(near, grad, out, held, got, x_first, y_first, y_then, x_then, z_last, send, recv, own, early=False):
     wires = Wires(near, send, recv)
     at, sizes = near.at, near.sizes
     nz, ny, nx = sizes["z"], sizes["y"], sizes["x"]
@@ -276,15 +282,32 @@
         def _(i):
             add((x, i, y, ALL, first), [y_then[k - 1, i] for k in near.shifts("y")])
             add((x, i, y, ALL, second), [x_then[k - 1, i] for k in near.shifts("x")])
-
-        start(last)
+            if early:
+                out[i] = held[x, i, y]
+
+        if early:
+            left(pair, one, two)
+        else:
+            start(last)
 
     def stage4():
         landed(last)
         out[...] = sum([z_last[k - 1].astype(F32) for k in near.shifts("z")], held[x, z, y].astype(F32))
         left(pair, one, two, last)
 
-    return [stage0, stage1, stage2, stage3, stage4]
+    return [stage0, stage1, stage2, stage3] if early else [stage0, stage1, stage2, stage3, stage4]
+
+
+def column_stages(near, column, out, z_last, send, recv):
+    wires = Wires(near, send, recv)
+    last = [wires.wire(column.at[near.along("z", k)], z_last.at[k - 1], "z", k) for k in near.shifts("z")]
+
+    def finish():
+        landed(last)
+        out[...] = sum([z_last[k - 1].astype(F32) for k in near.shifts("z")], column[near.at["z"]].astype(F32))
+        left(last)
+
+    return [lambda: start(last), finish]
 
 
 def total_scratch(sizes, shape):
@@ -385,10 +408,10 @@
     return dot(value, (column == row + device * size).astype(BF), 1, 0)
 
 
-def enter_kernel(sizes, tile, x_ref, w_ref, *refs):
-    vec_refs, (a1_out, qkv_out, w_out, vecs_ref) = refs[:10], refs[10:14]
-    a1_ref, qkv_ref, w_full, unit_ref, mine_ref = refs[14:19]
-    small_refs, gather_refs, out_sems = refs[19:23], refs[23:32], refs[32]
+def enter_kernel(sizes, tile, x_ref, w_ref, seg_ref, wo_ref, wu_ref, *refs):
+    vec_refs, (a1_out, qkv_out, w_out, vecs_ref, mark_ref, far_ref, wo_full, wu_full) = refs[:10], refs[10:18]
+    a1_ref, qkv_ref, w_full, unit_ref, mine_ref, third_ref = refs[18:24]
+    small_refs, gather_refs, ahead_refs, out_sems = refs[24:28], refs[28:37], refs[37:43], refs[43]
     rows, d = x_ref.shape
     near = Near(sizes)
     near.greet()
@@ -401,11 +424,15 @@
     both = placed(in_bias[...], 2 * d, device)
     mine_ref[8:9, :] = both[:, :d]
     mine_ref[9:10, :] = both[:, d:]
-    up = placed(up_bias[...], 6 * 512, device)
-    for i in range(6):
-        mine_ref[UP_ROW + i : UP_ROW + i + 1, :512] = up[:, 512 * i : 512 * (i + 1)]
+    up = placed(up_bias[...], 4 * d, device)
+    for i in range(4):
+        mine_ref[UP_ROW + i : UP_ROW + i + 1, :] = up[:, d * i : d * (i + 1)]
     plans = [
         gather_stages(near, w_ref, w_full, *gather_refs[3 * t : 3 * t + 3], base=d * t, width=d) for t in range(3)
+    ]
+    ahead = [
+        gather_stages(near, wo_ref, wo_full, *ahead_refs[:3], part="first"),
+        gather_stages(near, wu_ref, wu_full, *ahead_refs[3:], part="first"),
     ]
     small = total_stages(near, mine_ref, vecs_ref, *small_refs)
     for plan in plans:
@@ -421,6 +448,12 @@
     lax.fori_loop(0, rows // tile, body, 0)
     plans[0][1]()
     small[3]()
+    for plan in ahead:
+        plan[0]()
+    image = lax.broadcasted_iota(jnp.int32, (128, rows), 0) % HD
+    same = seg_ref[...] == image
+    mark_ref[...] = same.astype(F32).T.astype(BF)
+    far_ref[...] = jnp.where(same | (image > PADDING), 0.0, FAR).T.astype(BF)
     plans[1][1]()
     plans[0][2]()
     plans[2][1]()
@@ -436,11 +469,15 @@
 
     def third(t):
         cols = slice(d * t, d * (t + 1))
-        w = w_full[:, :, :, :, :, cols].astype(F32).reshape(d, d).astype(BF)
-        value = dot(a1_ref[...], w, 1, 0)
-        if t != 1:
-            value = value + vecs_ref[8 + t // 2 : 9 + t // 2, :]
-        qkv_ref[:, cols] = value.astype(BF)
+        third_ref[...] = w_full[:, :, :, :, :, cols].astype(F32).reshape(d, d).astype(BF)
+
+        def body(span):
+            value = dot(a1_ref[span, :], third_ref[...], 1, 0)
+            if t != 1:
+                value = value + vecs_ref[8 + t // 2 : 9 + t // 2, :]
+            qkv_ref[span, cols] = value.astype(BF)
+
+        row_loop(rows, rows // 2, body)
 
     def store(t):
         cols = pl.ds(d * t, d)
@@ -462,23 +499,28 @@
     sends[-1].start()
     third(2)
     store(2)
+    for plan in ahead:
+        plan[1]()
     for copy in sends:
         copy.wait()
 
 
-def enter(sizes, x, w_in, vectors, tile=352):
+def enter(sizes, x, w_in, segment_ids, w_out, w_up, vectors, tile=352):
     rows, d = x.shape
     vmem, hbm = pl.BlockSpec(memory_space=pltpu.VMEM), pl.BlockSpec(memory_space=pltpu.HBM)
     full = lead(sizes) + w_in.shape
     return pl.pallas_call(
         functools.partial(enter_kernel, sizes, tile),
-        in_specs=[vmem] * 12,
-        out_specs=[hbm, hbm, hbm, vmem],
+        in_specs=[vmem] * 15,
+        out_specs=[hbm, hbm, hbm, vmem, vmem, vmem, hbm, hbm],
         out_shape=[
             jax.ShapeDtypeStruct((rows, d), BF),
             jax.ShapeDtypeStruct((rows, 3 * d), BF),
             jax.ShapeDtypeStruct(full, BF),
             jax.ShapeDtypeStruct((VEC_ROWS, d), F32),
+            jax.ShapeDtypeStruct((rows, 128), BF),
+            jax.ShapeDtypeStruct((rows, 128), BF),
+            *gathered(sizes, [w_out, w_up]),
         ],
         scratch_shapes=[
             pltpu.VMEM((rows, d), BF),
@@ -486,13 +528,14 @@
             pltpu.VMEM(full, BF),
             pltpu.VMEM((rows, d), F32),
             pltpu.VMEM((VEC_ROWS, d), F32),
+            pltpu.VMEM((d, d), BF),
             *total_scratch(sizes, (VEC_ROWS, d)),
-            *gather_scratch(sizes) * 3,
+            *gather_scratch(sizes) * 5,
             pltpu.SemaphoreType.DMA((5,)),
         ],
         compiler_params=params(collective_id=0, has_side_effects=True),
         name="enter",
-    )(x, w_in, *[v[None] for v in vectors])
+    )(x, w_in, segment_ids[None], w_out, w_up, *[v[None] for v in vectors])
 
 
 def chunks(rows, size):
@@ -500,25 +543,26 @@
 
 
 GATHER_AT = {
-    (0, 0): [(0, 0), (1, 0)],
-    (1, 0): [(0, 1), (2, 0)],
-    (2, 0): [(1, 1), (0, 2)],
-    (3, 0): [(2, 1), (1, 2), (0, 3)],
-    (4, 0): [(2, 2)],
-    (5, 0): [(1, 3)],
-    (5, -1): [(2, 3), (0, 4), (1, 4), (2, 4)],
+    (0, 0): [(2, 0), (0, 1), (1, 1)],
+    (1, 0): [(0, 2), (1, 2)],
+    (2, 0): [(2, 1), (0, 3)],
+    (3, 0): [(2, 2), (1, 3)],
+    (5, 0): [(2, 3)],
+    (5, -1): [(0, 4), (1, 4), (2, 4)],
 }
 
 
 def attend_kernel(chunk, sizes, count, q_ref, k_ref, v_ref, mark_ref, far_ref, *refs):
-    shards, (o_ref, e_ref, inv_ref) = refs[:count], refs[count : count + 3]
+    shards, (o_ref, e_ref, inv_ref) = refs[:count][::-1], refs[count : count + 3]
     full, (vt_ref, k2_ref), sems = refs[count + 3 : 2 * count + 3], refs[2 * count + 3 : 2 * count + 5], refs[2 * count + 5 :]
     rows = q_ref.shape[0]
     plans, schedule = [], {}
     if count:
         near, schedule = Near(sizes), GATHER_AT
         pl.when(pl.program_id(0) == 0)(near.greet)
-        plans = [gather_stages(near, shards[i], full[i], *sems[3 * i : 3 * i + 3]) for i in range(count)]
+        plans = [
+            gather_stages(near, shards[i], full[i], *sems[3 * i : 3 * i + 3], part="all" if i == 2 else "rest") for i in range(count)
+        ]
     vt_ref[...] = v_ref[...].astype(F32).T.astype(BF)
     low = lax.broadcasted_iota(jnp.int32, (1, 128), 1) < HD
     for half in range(2):
@@ -545,6 +589,7 @@
 
 def attend(qkv, mark, far, sizes, shards, chunk=256):
     count = len(shards)
+    hbm = pl.BlockSpec(memory_space=pltpu.HBM)
     rows, width = qkv.shape
     pairs = width // 384
     return pl.pallas_call(
@@ -556,19 +601,19 @@
             pl.BlockSpec((rows, 128), lambda p: (0, 2 * pairs + p)),
             whole((rows, 128)),
             whole((rows, 128)),
-            *[whole(a.shape) for a in shards],
+            *([whole(shards[2].shape), hbm, hbm] if count else []),
         ],
         out_specs=[
             pl.BlockSpec((128, rows), lambda p: (p, 0)),
             pl.BlockSpec((2, rows, rows), lambda p: (p, 0, 0)),
             pl.BlockSpec((1, 2, rows), lambda p: (p, 0, 0)),
-            *[pl.BlockSpec(memory_space=pltpu.HBM)] * count,
+            *[hbm] * count,
         ],
         out_shape=[
             jax.ShapeDtypeStruct((pairs * 128, rows), BF),
             jax.ShapeDtypeStruct((2 * pairs, rows, rows), BF),
             jax.ShapeDtypeStruct((pairs, 2, rows), F32),
-            *(gathered(sizes, shards) if count else []),
+            *([*shards[:2], *gathered(sizes, shards[2:])] if count else []),
         ],
         scratch_shapes=[
             pltpu.VMEM((128, rows), BF),
@@ -577,11 +622,17 @@
         ],
         compiler_params=params(collective_id=1, has_side_effects=True) if count else params(),
         cost_estimate=cost(2 * pairs * 4 * rows * rows * 256, 4 * pairs * rows * rows, 2 * pairs * rows * rows),
+        input_output_aliases={7: 3, 6: 4} if count else {},
         name="attend",
-    )(qkv, qkv, qkv, mark, far, *shards)
-
-
-def middle_kernel(o_ref, x_ref, g_ref, w_ref, vec_ref, m1_ref, a2_ref, gm_ref, gmsum_ref):
+    )(qkv, qkv, qkv, mark, far, *shards[::-1])
+
+
+def masked(g_ref, mark_ref, rows):
+    padding = mark_ref[rows, PADDING : PADDING + 1].astype(F32)
+    return jnp.where(padding > 0, 0.0, g_ref[rows, :].astype(F32))
+
+
+def middle_kernel(o_ref, x_ref, g_ref, mark_ref, w_ref, vec_ref, m1_ref, a2_ref, gm_ref, gmsum_ref):
     bias, scale1, gain2, shift2, scale2 = (vec_ref[i : i + 1, :] for i in (0, 3, 5, 6, 7))
     m1_ref[...] = dot(o_ref[...], w_ref[...], 0, 0)
     gmsum_ref[...] = jnp.zeros_like(gmsum_ref)
@@ -591,14 +642,14 @@
         m1_ref[rows, :] = m1
         unit, _ = normalised(m1)
         a2_ref[rows, :] = (unit * gain2 + shift2).astype(BF)
-        gm = (scale2 * g_ref[rows, :].astype(F32)).astype(BF)
+        gm = (scale2 * masked(g_ref, mark_ref, rows)).astype(BF)
         gm_ref[rows, :] = gm
         gmsum_ref[...] += jnp.sum(gm.astype(F32).reshape(-1, 8, gm.shape[-1]), axis=0)
 
     row_loop(x_ref.shape[0], 352, body)
 
 
-def middle(o, x, g, w_out, vec):
+def middle(o, x, g, mark, w_out, vec):
     rows, d = x.shape
     return pl.pallas_call(
         middle_kernel,
@@ -611,7 +662,7 @@
         compiler_params=params(),
         cost_estimate=cost(2 * rows * d * d, 14 * rows * d),
         name="middle",
-    )(o, x, g, w_out, vec)
+    )(o, x, g, mark, w_out, vec)
 
 
 def gelu_parts(u):
@@ -635,7 +686,9 @@
         bm_ref[...] = jnp.zeros_like(bm_ref)
         ga_ref[...] = jnp.zeros_like(ga_ref)
 
-    bias = vec_ref[pl.ds(UP_ROW + pl.program_id(0), 1), : up_ref.shape[-1]]
+    d = vec_ref.shape[-1]
+    spread = up_ref.shape[-1] // d
+    bias = jnp.concatenate([vec_ref[pl.ds(UP_ROW + pl.program_id(0) * spread + i, 1), :] for i in range(spread)], axis=1)
     total = jnp.zeros((8, up_ref.shape[-1]), F32)
     for start, size in chunks(a2_ref.shape[0], chunk):
         rows = pl.ds(start, size)
@@ -654,7 +707,7 @@
     dup_ref[...] = dot(a2_ref[...], gu_ref[...], 0, 0).astype(dup_ref.dtype)
 
 
-def feed(a2, gm, w_up, vecs, w_down, block=512, chunk=704, kind=BF):
+def feed(a2, gm, w_up, vecs, w_down, block=768, chunk=704, kind=BF):
     rows, d = a2.shape
     ff = w_up.shape[1]
     return pl.pallas_call(
@@ -688,7 +741,7 @@
     )(a2, gm, w_up, vecs, w_down)
 
 
-def join_kernel(size, m1_ref, bm_ref, ga_ref, x_ref, g_ref, o_ref, w_ref, vec_ref, out_ref, gm1_ref, go_ref, dout_ref, sums_ref, gb_ref):
+def join_kernel(size, m1_ref, bm_ref, ga_ref, x_ref, g_ref, mark_ref, o_ref, w_ref, vec_ref, out_ref, gm1_ref, go_ref, dout_ref, sums_ref, gb_ref):
     bias2, scale1, gain2, scale2 = (vec_ref[i : i + 1, :] for i in (4, 3, 5, 7))
     step = pl.program_id(0)
 
@@ -701,7 +754,7 @@
     def body(rows):
         m1 = m1_ref[rows, :]
         bm = bm_ref[rows, :] + bias2
-        g = g_ref[rows, :].astype(F32)
+        g = masked(g_ref, mark_ref, rows)
         out_ref[rows, :] = (m1 + scale2 * bm).astype(BF)
         unit, inverse = normalised(m1)
         ga = ga_ref[rows, :]
@@ -722,13 +775,13 @@
         dout_ref[...] = dot(o_ref[...], gb_ref[...], 1, 0).astype(dout_ref.dtype)
 
 
-def join(m1, bm, ga, x, g, o, w_out, vec, tile=352, kind=BF):
+def join(m1, bm, ga, x, g, mark, o, w_out, vec, tile=352, kind=BF):
     rows, d = x.shape
     by_rows = pl.BlockSpec((tile, d), lambda i: (i, 0))
     return pl.pallas_call(
         functools.partial(join_kernel, 352),
         grid=(rows // tile,),
-        in_specs=[by_rows] * 5 + [whole((d, rows)), whole((d, d)), whole((VEC_ROWS, d))],
+        in_specs=[by_rows] * 5 + [pl.BlockSpec((tile, 128), lambda i: (i, 0)), whole((d, rows)), whole((d, d)), whole((VEC_ROWS, d))],
         out_specs=[by_rows, by_rows, whole((d, rows)), whole((d, d)), whole((5, 8, d))],
         out_shape=[
             jax.ShapeDtypeStruct((rows, d), BF),
@@ -741,17 +794,17 @@
         compiler_params=params(),
         cost_estimate=cost(4 * rows * d * d, 26 * rows * d),
         name="join",
-    )(m1, bm, ga, x, g, o, w_out, vec)
+    )(m1, bm, ga, x, g, mark, o, w_out, vec)
 
 
 SCATTER_AT = {
-    (0, 0): [(0, 0), (1, 0)],
-    (1, 0): [(0, 1), (2, 0)],
-    (2, 0): [(0, 2), (1, 1)],
-    (3, 0): [(0, 3), (2, 1)],
-    (4, 0): [(1, 2), (2, 2)],
-    (5, 0): [(1, 3), (2, 3), (0, 4)],
-    (5, -1): [(1, 4), (2, 4)],
+    (0, 0): [(2, 0), (0, 0), (1, 0)],
+    (1, 0): [(0, 1), (2, 1)],
+    (2, 0): [(1, 1)],
+    (3, 0): [(0, 2), (2, 2)],
+    (4, 0): [(1, 2), (0, 3)],
+    (5, 0): [(2, 3), (1, 3)],
+    (5, -1): [(0, 4), (2, 4)],
 }
 
 
@@ -764,7 +817,8 @@
         near, schedule = Near(sizes), SCATTER_AT
         pl.when(pl.program_id(0) == 0)(near.greet)
         plans = [
-            scatter_stages(near, grads[i], sums[i], *rest[SCATTER_REFS * i : SCATTER_REFS * (i + 1)]) for i in range(count)
+            scatter_stages(near, grads[i], sums[i], *rest[SCATTER_REFS * i : SCATTER_REFS * (i + 1)], early=i == 1)
+            for i in range(count)
         ]
     factor = HD ** (-0.5)
     kt_ref[...] = k_ref[...].astype(F32).T.astype(BF)
@@ -793,6 +847,9 @@
 def attend_back(qkv, go, o, e, inv, sizes, grads, chunk=256):
     blocks = blocks_of(sizes, grads) if grads else []
     count = len(blocks)
+    sums = [jax.ShapeDtypeStruct(b.shape[-2:], F32) for b in blocks]
+    if count:
+        sums[1] = jax.ShapeDtypeStruct((sizes["z"],) + sums[1].shape, BF)
     rows, width = qkv.shape
     pairs = width // 384
     return pl.pallas_call(
@@ -808,10 +865,10 @@
             pl.BlockSpec((1, 2, rows), lambda p: (p, 0, 0)),
             *[pl.BlockSpec(memory_space=pltpu.HBM)] * count,
         ],
-        out_specs=[pl.BlockSpec((3, rows, 128), lambda p: (0, 0, p)), *[whole(b.shape[-2:]) for b in blocks]],
+        out_specs=[pl.BlockSpec((3, rows, 128), lambda p: (0, 0, p)), *[whole(v.shape) for v in sums]],
         out_shape=[
             jax.ShapeDtypeStruct((3, rows, pairs * 128), BF),
-            *[jax.ShapeDtypeStruct(b.shape[-2:], F32) for b in blocks],
+            *sums,
         ],
         scratch_shapes=[
             pltpu.VMEM((128, rows), BF),
@@ -887,11 +944,11 @@
     )(a1, gqkv, w_in, x, gm1, gain)
 
 
-def leave_kernel(sizes, tile, a1_in, gqkv_in, w_in, x_in, gm1_in, vec_ref, join_ref, ub_ref, gmsum_ref, gx_out, dw_ref, early_ref, late_ref, *refs):
+def leave_kernel(sizes, tile, a1_in, gqkv_in, w_in, x_in, gm1_in, vec_ref, join_ref, ub_ref, gmsum_ref, column_ref, gx_out, dw_ref, early_ref, late_ref, ddown_ref, *refs):
     a1_ref, gqkv_ref, w_ref, x_ref, gm1_ref, gx_ref, ga_ref, sums_ref, mine_ref, last_ref = refs[:10]
     grad_refs, refs = refs[10:13], refs[13:]
     scatter_refs, refs = [refs[9 * t : 9 * t + 9] for t in range(3)], refs[27:]
-    early_refs, late_refs, in_sems, out_sems = refs[:4], refs[4:8], refs[8], refs[9]
+    early_refs, late_refs, column_refs, in_sems, out_sems = refs[:4], refs[4:8], refs[8:11], refs[11], refs[12]
     rows, d = x_in.shape
     count = rows // tile
     moves = [(a1_in, a1_ref), *[(gqkv_in.at[t], gqkv_ref.at[t]) for t in range(3)], (w_in, w_ref), (x_in, x_ref), (gm1_in, gm1_ref)]
@@ -913,6 +970,8 @@
     ]
     early = total_stages(near, mine_ref, early_ref, *early_refs)
     late = total_stages(near, last_ref, late_ref, *late_refs)
+    column = column_stages(near, column_ref, ddown_ref, *column_refs)
+    column[0]()
     last_ref[...] = jnp.zeros_like(last_ref)
 
     def weight(t):
@@ -921,11 +980,11 @@
         grad_refs[t][...] = value.reshape(grad_refs[t].shape).astype(BF)
 
     def back(t):
-        part = dot(gqkv_ref[t], w_ref[:, d * t : d * (t + 1)], 1, 1)
-        if t == 0:
-            ga_ref[...] = part
-        else:
-            ga_ref[...] += part
+        def body(span):
+            part = dot(gqkv_ref[t, span, :], w_ref[:, d * t : d * (t + 1)], 1, 1)
+            ga_ref[span, :] = part if t == 0 else ga_ref[span, :] + part
+
+        row_loop(rows, rows // 2, body)
         if t != 1:
             total = jnp.zeros((1, d), F32)
             for start_row, size in chunks(rows, tile):
@@ -952,6 +1011,7 @@
     plans[1][2]()
     back(2)
     plans[0][3]()
+    column[1]()
     early[3]()
     fetch[5].wait()
     fetch[6].wait()
@@ -998,19 +1058,20 @@
         send(index).wait()
 
 
-def leave(sizes, a1, gqkv, w_in, x, gm1, vecs, join_sums, ub_sum, gm_sum, tile=352):
+def leave(sizes, a1, gqkv, w_in, x, gm1, vecs, join_sums, ub_sum, gm_sum, column, tile=352):
     rows, d = x.shape
     vmem, hbm = pl.BlockSpec(memory_space=pltpu.VMEM), pl.BlockSpec(memory_space=pltpu.HBM)
     block = d // (sizes["x"] * 2 * sizes["z"] * sizes["y"])
     return pl.pallas_call(
         functools.partial(leave_kernel, sizes, tile),
-        in_specs=[hbm] * 5 + [vmem] * 4,
-        out_specs=[hbm, vmem, vmem, vmem],
+        in_specs=[hbm] * 5 + [vmem] * 5,
+        out_specs=[hbm, vmem, vmem, vmem, vmem],
         out_shape=[
             jax.ShapeDtypeStruct((rows, d), F32),
             jax.ShapeDtypeStruct((block, 3 * d), F32),
             jax.ShapeDtypeStruct((16, d), F32),
             jax.ShapeDtypeStruct((8, d), F32),
+            jax.ShapeDtypeStruct(column.shape[1:], F32),
         ],
         scratch_shapes=[
             pltpu.VMEM((rows, d), BF),
@@ -1027,12 +1088,15 @@
             *scatter_scratch(sizes, block, d, BF)[:-1] * 3,
             *total_scratch(sizes, (16, d)),
             *total_scratch(sizes, (8, d)),
+            pltpu.VMEM((sizes["z"] - 1,) + column.shape[1:], BF),
+            pltpu.SemaphoreType.DMA((sizes["z"] - 1,)),
+            pltpu.SemaphoreType.DMA((sizes["z"] - 1,)),
             pltpu.SemaphoreType.DMA((7,)),
             pltpu.SemaphoreType.DMA((rows // tile,)),
         ],
         compiler_params=params(collective_id=3, has_side_effects=True),
         name="leave",
-    )(a1, gqkv, w_in, x, gm1, vecs, join_sums, ub_sum, gm_sum)
+    )(a1, gqkv, w_in, x, gm1, vecs, join_sums, ub_sum, gm_sum, column)
 
 
 def share_kernel(early_ref, late_ref, *refs):
@@ -1086,33 +1150,35 @@
     )
     own = all(w.shape[0] % 8 == 0 for w in (in_weight, out_weight, up_weight, down_weight))
     if own:
-        a1, qkv, w_in, vecs = enter(sizes, inputs, in_weight, vectors)
+        a1, qkv, w_in, vecs, mark, far, *begun = enter(
+            sizes, inputs, in_weight, segment_ids, out_weight, up_weight, vectors
+        )
         w_in = w_in.reshape(d, 3 * d)
     else:
         w_in = take(in_weight)
         row = lambda v: take(v).astype(F32).reshape(-1, d)
         vecs = jnp.concatenate(
             [row(v) for v in (out_bias, first_gain, first_shift, first_scale, down_bias, second_gain, second_shift, second_scale, in_bias)]
-            + [jnp.pad(take(up_bias).astype(F32).reshape(6, 512), ((0, 0), (0, d - 512)))]
+            + [row(up_bias), jnp.zeros((VEC_ROWS - 14, d), F32)]
         )
         offset = jnp.concatenate([vecs[8:9], jnp.zeros((1, d), F32), vecs[9:10]], axis=1)
         a1, qkv = project(inputs, w_in, vecs[1:2], vecs[2:3], offset)
-    lane = lax.broadcasted_iota(jnp.int32, (1, 128), 1) % HD
-    same = segment_ids[:, None] == lane
-    mark = same.astype(BF)
-    far = jnp.where(same | (lane > PADDING), 0.0, FAR).astype(BF)
-    g = jnp.where((segment_ids < PADDING)[:, None], cotangent, jnp.zeros_like(cotangent))
-    o, e, inv, *full = attend(qkv, mark, far, sizes, [out_weight, up_weight, down_weight] if own else [])
+        lane = lax.broadcasted_iota(jnp.int32, (1, 128), 1) % HD
+        same = segment_ids[:, None] == lane
+        mark = same.astype(BF)
+        far = jnp.where(same | (lane > PADDING), 0.0, FAR).astype(BF)
+    o, e, inv, *full = attend(qkv, mark, far, sizes, [*begun, down_weight] if own else [])
     w_out, w_up, w_down = (
         (f.reshape(-1, f.shape[-1]) for f in full) if own else (take(w) for w in (out_weight, up_weight, down_weight))
     )
-    m1, a2, gm, gm_sum = middle(o, inputs, g, w_out, vecs)
+    m1, a2, gm, gm_sum = middle(o, inputs, cotangent, mark, w_out, vecs)
     bm, ga2, d_up, d_down, ub_sum = feed(a2, gm, w_up, vecs, w_down)
-    outputs, gm1, go, d_out, join_sums = join(m1, bm, ga2, inputs, g, o, w_out, vecs)
+    outputs, gm1, go, d_out, join_sums = join(m1, bm, ga2, inputs, cotangent, mark, o, w_out, vecs)
     gqkv, *done = attend_back(qkv, go, o, e, inv, sizes, [d_up, d_down, d_out] if own else [])
     if own:
-        gx, d_in, early, late = leave(sizes, a1, gqkv, w_in, inputs, gm1, vecs, join_sums, ub_sum, gm_sum)
-        d_up, d_down, d_out, d_in, *out = share(early, late, [*done, d_in], [v.shape[0] for v in vectors])
+        d_up, column, d_out = done
+        gx, d_in, early, late, d_down = leave(sizes, a1, gqkv, w_in, inputs, gm1, vecs, join_sums, ub_sum, gm_sum, column)
+        d_up, d_down, d_out, d_in, *out = share(early, late, [d_up, d_down, d_out, d_in], [v.shape[0] for v in vectors])
         out = [v.reshape(-1) for v in out]
     else:
         d_in, col_sums, gx, last_sums = finish(a1, gqkv, w_in, inputs, gm1, vecs[1:2])

time: 357 us -> 341 us (0.955)
  Pallas kernels: 338 us -> 330 us
  other arithmetic: 7.37 us -> 0 us
    pallas_call x1, Pallas kernels: 85.7 us -> 78.5 us  [attend_back(): pl.pallas_call(functools.partial(attend_back_kernel, chunk, sizes, count)...]
    pallas_call x1, Pallas kernels: 37.7 us -> 42.3 us  [enter(): pl.pallas_call(functools.partial(enter_kernel, sizes, tile), in_specs=[vm...]
where the time goes in v4:
time: 341 us; the launch traced here: 337 us
  Pallas kernels  330 us (97%)
  local copies, waits for them, and re-layouts  5.85 us (2%)
    pallas_call x1, Pallas kernels, attend_back(): pl.pallas_call(functools.partial(attend_back_kernel, chunk, sizes, count)...  78.5 us
    pallas_call x1, Pallas kernels, attend(): pl.pallas_call(functools.partial(attend_kernel, chunk, sizes, count), gri...  78.2 us
    pallas_call x1, Pallas kernels, feed(): pl.pallas_call(functools.partial(feed_kernel, chunk), grid=(ff // block,)...  56.6 us
    pallas_call x1, Pallas kernels, leave(): pl.pallas_call(functools.partial(leave_kernel, sizes, tile), in_specs=[hb...  43.5 us
    pallas_call x1, Pallas kernels, enter(): pl.pallas_call(functools.partial(enter_kernel, sizes, tile), in_specs=[vm...  42.3 us
    pallas_call x1, Pallas kernels, join(): pl.pallas_call(functools.partial(join_kernel, 352), grid=(rows // tile,),...  17.5 us
    pallas_call x1, Pallas kernels, middle(): pl.pallas_call(middle_kernel, out_shape=[jax.ShapeDtypeStruct((rows, d),...  11.4 us

profile of v4, /device:TPU:0, one launch (start us, length us, event | category | flops | bytes accessed | tf_op | source)
XLA Modules:
  0.0 336.9 jit_solution(7009050414129429250)
XLA Ops:
  0.6 1.3 broadcast_in_dim.33.seg_ref
  1.9 42.3 %enter.1 = (bf16[1408,768]{1,0:T(8,128)(2,1)}, bf16[1408,2304]{1,0:T(8,128)(2,1)}, bf16[2,2,4,2,24,2304]{5,4,3,2,1,0:T(8,128)(2,1)}, f32[16,768]{1,0:T(8,128)}, ...) custom-call(bf16[1408,768]{1,0:T(8,128)(2,1)} %x_in.1, ...), custom_call_target="tpu_custom_call" | custom-call | tf_op jit(solution)/shard_map/enter/pallas_call | solution.py:512
  44.3 78.2 %attend.1 = (bf16[768,1408]{1,0:T(8,128)(2,1)}, bf16[12,1408,1408]{2,1,0:T(8,128)(2,1)}, f32[6,2,1408]{2,1,0:T(2,128)}, bf16[2,2,4,2,24,768]{5,4,3,2,1,0:T(8,128...) custom-call(bf16[1408,2304]{1,0:T(8,128)(2,1)} %get-tuple-element.67, ...), custom_call_target="tpu_custom_call", output_to_operand_aliasing={{3}: (7, {}), {4}: (6, {})} | custom-call | flops 24360517632 | bytes 47579136 | tf_op jit(solution)/shard_map/attend/pallas_call | solution.py:595
  122.5 11.4 %middle.1 = (f32[1408,768]{1,0:T(8,128)}, bf16[1408,768]{1,0:T(8,128)(2,1)}, bf16[1408,768]{1,0:T(8,128)(2,1)}, f32[8,768]{1,0:T(8,128)}) custom-call(bf16[768,1408]{1,0:T(8,128)(2,1)} %get-tuple-element.72.o_ref, bf16[1408,768]{1,0:T(8,128)(2,1)} %x_in.1, bf16[1408,768]{1,0:T(8,128)(2,1)} %g_ref.3, bf16[1408,128]{1,0:T(8,128)(2,1)} %get-tuple-element.68.mark_ref, ...), custom_call_target="tpu_custom_call" | custom-call | flops 1660944384 | bytes 15138816 | tf_op jit(solution)/shard_map/middle/pallas_call | solution.py:654
  133.9 56.6 %feed.1 = (f32[1408,768]{1,0:T(8,128)}, f32[1408,768]{1,0:T(8,128)}, bf16[768,3072]{1,0:T(8,128)(2,1)}, bf16[3072,768]{1,0:T(8,128)(2,1)}, f32[8,3072]{1,0:T(8,128)}) custom-call(bf16[1408,768]{1,0:T(8,128)(2,1)} %get-tuple-element.76.a2_ref, bf16[1408,768]{1,0:T(8,128)(2,1)} %get-tuple-element.77.gm_ref, bf16[768,3072]{1,0:T(8,128)(2,1)} %bitcast.40, ...), custom_call_target="tpu_custom_call" | custom-call | flops 39862665216 | bytes 37748736 | tf_op jit(solution)/shard_map/feed/pallas_call | solution.py:713
  190.5 17.5 %join.1 = (bf16[1408,768]{1,0:T(8,128)(2,1)}, f32[1408,768]{1,0:T(8,128)}, bf16[768,1408]{1,0:T(8,128)(2,1)}, bf16[768,768]{1,0:T(8,128)(2,1)}, f32[5,8,768]{2,1,0:T(8,128)}) custom-call(f32[1408,768]{1,0:T(8,128)} %get-tuple-element.75.m1_ref, f32[1408,768]{1,0:T(8,128)} %get-tuple-element.80.bm_ref, f32[1408,768]{1,0:T(8,128)} %get-tuple-element.81.ga_ref, ...), custom_call_target="tpu_custom_call" | custom-call | flops 3321888768 | bytes 28114944 | tf_op jit(solution)/shard_map/join/pallas_call | solution.py:781
  208.0 78.5 %attend_back.1 = (bf16[3,1408,768]{2,1,0:T(8,128)(2,1)}, f32[24,3072]{1,0:T(8,128)}, bf16[4,96,768]{2,1,0:T(8,128)(2,1)}, f32[24,768]{1,0:T(8,128)}) custom-call(bf16[1408,2304]{1,0:T(8,128)(2,1)} %get-tuple-element.67.q_ref.k_ref.v_ref, bf16[1408,2304]{1,0:T(8,128)(2,1)} %get-tuple-element.67.q_ref.k_ref.v_ref, ...), custom_call_target="tpu_custom_call" | custom-call | flops 48721035264 | bytes 47579136 | tf_op jit(solution)/shard_map/attend_back/pallas_call | solution.py:855
  286.4 43.5 %leave.1 = (f32[1408,768]{1,0:T(8,128)}, f32[24,2304]{1,0:T(8,128)}, f32[16,768]{1,0:T(8,128)}, f32[8,768]{1,0:T(8,128)}, f32[96,768]{1,0:T(8,128)}) custom-call(bf16[1408,768]{1,0:T(8,128)(2,1)} %get-tuple-element.83.a1_in, bf16[3,1408,768]{2,1,0:T(8,128)(2,1)} %get-tuple-element.90.gqkv_in, bf16[768,2304]{1,0:T(8,128)(2,1)} %bitcast.29, ...), custom_call_target="tpu_custom_call" | custom-call | tf_op jit(solution)/shard_map/leave/pallas_call | solution.py:1065
  329.9 2.2 share.1
  332.1 4.6 %copy.38 = f32[1408,768]{1,0:T(8,128)} copy(f32[1408,768]{1,0:T(8,128)} %get-tuple-element.135) | data formatting | bytes 8650752

commit v5 on v4

--- a/solution.py
+++ b/solution.py
@@ -543,12 +543,13 @@
 
 
 GATHER_AT = {
-    (0, 0): [(2, 0), (0, 1), (1, 1)],
-    (1, 0): [(0, 2), (1, 2)],
-    (2, 0): [(2, 1), (0, 3)],
-    (3, 0): [(2, 2), (1, 3)],
-    (5, 0): [(2, 3)],
-    (5, -1): [(0, 4), (1, 4), (2, 4)],
+    (0, 0): [(2, 0), (1, 1), (0, 1)],
+    (1, 0): [(1, 2)],
+    (2, 0): [(2, 1)],
+    (3, 0): [(0, 2), (1, 3), (2, 2)],
+    (4, 0): [(0, 3)],
+    (5, 0): [(2, 3), (0, 4)],
+    (5, -1): [(1, 4), (2, 4)],
 }
 
 
@@ -587,7 +588,7 @@
     pump(schedule, plans, -1)
 
 
-def attend(qkv, mark, far, sizes, shards, chunk=256):
+def attend(qkv, mark, far, sizes, shards, chunk=704):
     count = len(shards)
     hbm = pl.BlockSpec(memory_space=pltpu.HBM)
     rows, width = qkv.shape
@@ -798,13 +799,13 @@
 
 
 SCATTER_AT = {
-    (0, 0): [(2, 0), (0, 0), (1, 0)],
-    (1, 0): [(0, 1), (2, 1)],
-    (2, 0): [(1, 1)],
-    (3, 0): [(0, 2), (2, 2)],
-    (4, 0): [(1, 2), (0, 3)],
-    (5, 0): [(2, 3), (1, 3)],
-    (5, -1): [(0, 4), (2, 4)],
+    (0, 0): [(0, 0), (2, 0)],
+    (1, 0): [(0, 1)],
+    (2, 0): [(1, 0), (2, 1)],
+    (3, 0): [(0, 2), (1, 1)],
+    (4, 0): [(2, 2), (0, 3)],
+    (5, 0): [(1, 2), (2, 3)],
+    (5, -1): [(1, 3), (2, 4), (0, 4)],
 }
 
 
@@ -844,7 +845,7 @@
     pump(schedule, plans, -1)
 
 
-def attend_back(qkv, go, o, e, inv, sizes, grads, chunk=256):
+def attend_back(qkv, go, o, e, inv, sizes, grads, chunk=512):
     blocks = blocks_of(sizes, grads) if grads else []
     count = len(blocks)
     sums = [jax.ShapeDtypeStruct(b.shape[-2:], F32) for b in blocks]

time: 341 us -> 323 us (0.947)
  Pallas kernels: 330 us -> 313 us
    pallas_call x1, Pallas kernels: 78.2 us -> 62.6 us  [attend(): pl.pallas_call(functools.partial(attend_kernel, chunk, sizes, count), gri...]
    pallas_call x1, Pallas kernels: 78.5 us -> 66.3 us  [attend_back(): pl.pallas_call(functools.partial(attend_back_kernel, chunk, sizes, count)...]
    pallas_call x1, Pallas kernels: 17.5 us -> 28.2 us  [join(): pl.pallas_call(functools.partial(join_kernel, 352), grid=(rows // tile,),...]
where the time goes in v5:
time: 323 us; the launch traced here: 320 us
  Pallas kernels  313 us (97%)
  local copies, waits for them, and re-layouts  5.85 us (2%)
    pallas_call x1, Pallas kernels, attend_back(): pl.pallas_call(functools.partial(attend_back_kernel, chunk, sizes, count)...  66.3 us
    pallas_call x1, Pallas kernels, attend(): pl.pallas_call(functools.partial(attend_kernel, chunk, sizes, count), gri...  62.6 us
    pallas_call x1, Pallas kernels, feed(): pl.pallas_call(functools.partial(feed_kernel, chunk), grid=(ff // block,)...  56.6 us
    pallas_call x1, Pallas kernels, leave(): pl.pallas_call(functools.partial(leave_kernel, sizes, tile), in_specs=[hb...  43.7 us
    pallas_call x1, Pallas kernels, enter(): pl.pallas_call(functools.partial(enter_kernel, sizes, tile), in_specs=[vm...  42.3 us
    pallas_call x1, Pallas kernels, join(): pl.pallas_call(functools.partial(join_kernel, 352), grid=(rows // tile,),...  28.2 us
    pallas_call x1, Pallas kernels, middle(): pl.pallas_call(middle_kernel, out_shape=[jax.ShapeDtypeStruct((rows, d),...  11 us

profile of v5, /device:TPU:0, one launch (start us, length us, event | category | flops | bytes accessed | tf_op | source)
XLA Modules:
  0.0 319.7 jit_solution(7335327336161646554)
XLA Ops:
  0.6 1.3 broadcast_in_dim.33.seg_ref
  1.9 42.3 %enter.1 = (bf16[1408,768]{1,0:T(8,128)(2,1)}, bf16[1408,2304]{1,0:T(8,128)(2,1)}, bf16[2,2,4,2,24,2304]{5,4,3,2,1,0:T(8,128)(2,1)}, f32[16,768]{1,0:T(8,128)}, ...) custom-call(bf16[1408,768]{1,0:T(8,128)(2,1)} %x_in.1, ...), custom_call_target="tpu_custom_call" | custom-call | tf_op jit(solution)/shard_map/enter/pallas_call | solution.py:512
  44.3 62.6 %attend.1 = (bf16[768,1408]{1,0:T(8,128)(2,1)}, bf16[12,1408,1408]{2,1,0:T(8,128)(2,1)}, f32[6,2,1408]{2,1,0:T(2,128)}, bf16[2,2,4,2,24,768]{5,4,3,2,1,0:T(8,128...) custom-call(bf16[1408,2304]{1,0:T(8,128)(2,1)} %get-tuple-element.67, ...), custom_call_target="tpu_custom_call", output_to_operand_aliasing={{3}: (7, {}), {4}: (6, {})} | custom-call | flops 24360517632 | bytes 47579136 | tf_op jit(solution)/shard_map/attend/pallas_call | solution.py:596
  106.9 11.0 %middle.1 = (f32[1408,768]{1,0:T(8,128)}, bf16[1408,768]{1,0:T(8,128)(2,1)}, bf16[1408,768]{1,0:T(8,128)(2,1)}, f32[8,768]{1,0:T(8,128)}) custom-call(bf16[768,1408]{1,0:T(8,128)(2,1)} %get-tuple-element.72.o_ref, bf16[1408,768]{1,0:T(8,128)(2,1)} %x_in.1, bf16[1408,768]{1,0:T(8,128)(2,1)} %g_ref.3, bf16[1408,128]{1,0:T(8,128)(2,1)} %get-tuple-element.68.mark_ref, ...), custom_call_target="tpu_custom_call" | custom-call | flops 1660944384 | bytes 15138816 | tf_op jit(solution)/shard_map/middle/pallas_call | solution.py:655
  117.9 56.6 %feed.1 = (f32[1408,768]{1,0:T(8,128)}, f32[1408,768]{1,0:T(8,128)}, bf16[768,3072]{1,0:T(8,128)(2,1)}, bf16[3072,768]{1,0:T(8,128)(2,1)}, f32[8,3072]{1,0:T(8,128)}) custom-call(bf16[1408,768]{1,0:T(8,128)(2,1)} %get-tuple-element.76.a2_ref, bf16[1408,768]{1,0:T(8,128)(2,1)} %get-tuple-element.77.gm_ref, bf16[768,3072]{1,0:T(8,128)(2,1)} %bitcast.40, ...), custom_call_target="tpu_custom_call" | custom-call | flops 39862665216 | bytes 37748736 | tf_op jit(solution)/shard_map/feed/pallas_call | solution.py:714
  174.5 28.2 %join.1 = (bf16[1408,768]{1,0:T(8,128)(2,1)}, f32[1408,768]{1,0:T(8,128)}, bf16[768,1408]{1,0:T(8,128)(2,1)}, bf16[768,768]{1,0:T(8,128)(2,1)}, f32[5,8,768]{2,1,0:T(8,128)}) custom-call(f32[1408,768]{1,0:T(8,128)} %get-tuple-element.75.m1_ref, f32[1408,768]{1,0:T(8,128)} %get-tuple-element.80.bm_ref, f32[1408,768]{1,0:T(8,128)} %get-tuple-element.81.ga_ref, ...), custom_call_target="tpu_custom_call" | custom-call | flops 3321888768 | bytes 28114944 | tf_op jit(solution)/shard_map/join/pallas_call | solution.py:782
  202.7 66.3 %attend_back.1 = (bf16[3,1408,768]{2,1,0:T(8,128)(2,1)}, f32[24,3072]{1,0:T(8,128)}, bf16[4,96,768]{2,1,0:T(8,128)(2,1)}, f32[24,768]{1,0:T(8,128)}) custom-call(bf16[1408,2304]{1,0:T(8,128)(2,1)} %get-tuple-element.67.q_ref.k_ref.v_ref, bf16[1408,2304]{1,0:T(8,128)(2,1)} %get-tuple-element.67.q_ref.k_ref.v_ref, ...), custom_call_target="tpu_custom_call" | custom-call | flops 48721035264 | bytes 47579136 | tf_op jit(solution)/shard_map/attend_back/pallas_call | solution.py:856
  269.0 43.7 %leave.1 = (f32[1408,768]{1,0:T(8,128)}, f32[24,2304]{1,0:T(8,128)}, f32[16,768]{1,0:T(8,128)}, f32[8,768]{1,0:T(8,128)}, f32[96,768]{1,0:T(8,128)}) custom-call(bf16[1408,768]{1,0:T(8,128)(2,1)} %get-tuple-element.83.a1_in, bf16[3,1408,768]{2,1,0:T(8,128)(2,1)} %get-tuple-element.90.gqkv_in, bf16[768,2304]{1,0:T(8,128)(2,1)} %bitcast.29, ...), custom_call_target="tpu_custom_call" | custom-call | tf_op jit(solution)/shard_map/leave/pallas_call | solution.py:1066
  312.7 2.2 share.1
  314.9 4.6 %copy.38 = f32[1408,768]{1,0:T(8,128)} copy(f32[1408,768]{1,0:T(8,128)} %get-tuple-element.135) | data formatting | bytes 8650752
